TPU v7x, 128 devices: a whole 4x4x4 slice. The times are simulated.
128 devices in a mesh: gx: 8 (over y_hi, x), gy: 16 (over y_lo, z, core).
Axes of the slice: x: 4, y: 4 (y_hi: 2, y_lo: 2; y = y_hi * 2 + y_lo), z: 4, core: 2. Of those that a mesh axis runs over, the one named last changes fastest.
Arguments:
- wave_old: float32 [256, 256, 1024], P('gx', 'gy'), may hold values from 3 to 9
- wave_now: float32 [256, 256, 1024], P('gx', 'gy'), may hold values from 3 to 9
- born_old: float32 [256, 256, 1024], P('gx', 'gy'), may hold values from -0.36 to 0.36
- born_now: float32 [256, 256, 1024], P('gx', 'gy'), may hold values from -0.36 to 0.36
- courant: float32 [256, 256, 1024], P('gx', 'gy'), may hold values from 0.04 to 0.18
- contrast: float32 [256, 256, 1024], P('gx', 'gy'), may hold values from -5 to 5
- src_cell: int32 [512], P(('gx', 'gy')), may hold values from 0 to 524287
- src_amp: float32 [512, 2], P(('gx', 'gy')), may hold values from -6 to 6
- rcv_cell: int32 [32768, 8], P(('gx', 'gy')), may hold values from 0 to 524287
- rcv_weight: float32 [32768, 8], P(('gx', 'gy')), may hold values from 0 to 1
- rcv_dest: int32 [32768, 1], P(('gx', 'gy')), may hold values from 0 to 127; in each aligned block of 256 rows (0 to 255, 256 to 511, ...) at most 4 rows name the same one
Outputs:
- wave_next: float32 [256, 256, 1024], P('gx', 'gy')
- wave_last: float32 [256, 256, 1024], P('gx', 'gy')
- born_next: float32 [256, 256, 1024], P('gx', 'gy')
- born_last: float32 [256, 256, 1024], P('gx', 'gy')
- gathers: float32 [128, 128, 2, 4], P(('gx', 'gy'))
Inputs may be any that keep to these rules, and one draw needn't show every extreme that they name: `rcv_dest`: among the receivers of one device at most 4 name the same owner, and 4 is reached.
All inputs are finite; a program needn't handle non-finite values.
Results may differ from a plain program's by a relative error of at most 0.0003.
Values sent between devices are 32-bit elements; how exact they have to be, the bound alone decides.
No kernel may reach another device: no remote copies, remote signals or barrier semaphores. Data moves between devices by JAX's collectives and lax.ppermute only.
A program may use at most 128 MiB of HBM per device.

v0:
```python
import jax
import jax.numpy as jnp
from jax import lax
from jax.sharding import PartitionSpec as P

CAP = 4


CENTER = -205.0 / 72.0
WEIGHTS = (8.0 / 5.0, -1.0 / 5.0, 8.0 / 315.0, -1.0 / 560.0)


def with_halo(cells, sides, width):
    for axis, dim in sides:
        count = lax.axis_size(axis)
        ends = count - 1
        head = lax.slice_in_dim(cells, 0, width, axis=dim)
        tail = lax.slice_in_dim(cells, cells.shape[dim] - width, cells.shape[dim], axis=dim)
        cells = jnp.concatenate(
            [
                lax.ppermute(tail, axis, [(i, (i + 1) % count) for i in range(ends)]),
                cells,
                lax.ppermute(head, axis, [((i + 1) % count, i) for i in range(ends)]),
            ],
            axis=dim,
        )
    return cells


def laplace(padded, count_x, count_y):
    depth = padded.shape[2]
    padded_z = jnp.pad(padded, ((0, 0), (0, 0), (4, 4)))
    middle = padded_z[4 : 4 + count_x, 4 : 4 + count_y, 4 : 4 + depth]
    summed = 3.0 * CENTER * middle
    for k in range(1, 5):
        near = (
            padded_z[4 + k : 4 + k + count_x, 4 : 4 + count_y, 4 : 4 + depth]
            + padded_z[4 - k : 4 - k + count_x, 4 : 4 + count_y, 4 : 4 + depth]
        )
        near = (
            near
            + padded_z[4 : 4 + count_x, 4 + k : 4 + k + count_y, 4 : 4 + depth]
            + padded_z[4 : 4 + count_x, 4 - k : 4 - k + count_y, 4 : 4 + depth]
        )
        near = (
            near
            + padded_z[4 : 4 + count_x, 4 : 4 + count_y, 4 + k : 4 + k + depth]
            + padded_z[4 : 4 + count_x, 4 : 4 + count_y, 4 - k : 4 - k + depth]
        )
        summed = summed + WEIGHTS[k - 1] * near
    return summed


def single_lap(field):
    padded = with_halo(field, (("gx", 0), ("gy", 1)), 4)
    return laplace(padded, field.shape[0], field.shape[1])


def body(
    wave_old,
    wave_now,
    born_old,
    born_now,
    courant,
    contrast,
    src_cell,
    src_amp,
    rcv_cell,
    rcv_weight,
    rcv_dest,
):
    shape = wave_now.shape
    cells = shape[0] * shape[1] * shape[2]
    source_one = jnp.zeros((cells,), jnp.float32).at[src_cell].add(src_amp[:, 0]).reshape(shape)
    source_two = jnp.zeros((cells,), jnp.float32).at[src_cell].add(src_amp[:, 1]).reshape(shape)
    wave_next = 2.0 * wave_now - wave_old + courant * single_lap(wave_now) + source_one
    wave_last = 2.0 * wave_next - wave_now + courant * single_lap(wave_next) + source_two
    accel_one = wave_next - 2.0 * wave_now + wave_old
    accel_two = wave_last - 2.0 * wave_next + wave_now
    born_next = 2.0 * born_now - born_old + courant * single_lap(born_now) + contrast * accel_one
    born_last = 2.0 * born_next - born_now + courant * single_lap(born_next) + contrast * accel_two
    sample_one = jnp.sum(rcv_weight * born_next.reshape(-1)[rcv_cell], axis=1)
    sample_two = jnp.sum(rcv_weight * born_last.reshape(-1)[rcv_cell], axis=1)
    samples = jnp.stack([sample_one, sample_two])
    count_gx = lax.axis_size("gx")
    count_gy = lax.axis_size("gy")
    devices = count_gx * count_gy
    dest = rcv_dest[:, 0]
    onehot = (dest[:, None] == jnp.arange(devices, dtype=jnp.int32)[None, :]).astype(jnp.int32)
    before = jnp.cumsum(onehot, axis=0) - onehot
    slot = jnp.sum(before * onehot, axis=1)
    target = dest * CAP + slot
    select = (target[:, None] == jnp.arange(devices * CAP, dtype=jnp.int32)[None, :]).astype(
        jnp.float32
    )
    packed = jnp.dot(
        samples, select, precision=lax.Precision.HIGHEST, preferred_element_type=jnp.float32
    )
    outgoing = packed.reshape(2, devices, CAP).transpose(1, 0, 2)
    arrived = lax.all_to_all(outgoing, ("gx", "gy"), split_axis=0, concat_axis=0, tiled=True)
    return (wave_next, wave_last, born_next, born_last, arrived[None])


def solution(mesh):
    placed = (
        P("gx", "gy", None),
        P("gx", "gy", None),
        P("gx", "gy", None),
        P("gx", "gy", None),
        P("gx", "gy", None),
        P("gx", "gy", None),
        P(("gx", "gy")),
        P(("gx", "gy"), None),
        P(("gx", "gy"), None),
        P(("gx", "gy"), None),
        P(("gx", "gy"), None),
    )
    return jax.shard_map(
        body,
        mesh=mesh,
        in_specs=placed,
        out_specs=(
            P("gx", "gy", None),
            P("gx", "gy", None),
            P("gx", "gy", None),
            P("gx", "gy", None),
            P(("gx", "gy"), None, None, None),
        ),
        check_vma=False,
    )
```

profile of v0, /device:TPU:1, one launch (start us, length us, event | category | flops | bytes accessed | tf_op | source)
XLA Modules:
  0.0 284.6 jit_solution(6771491168119582250)
XLA Ops:
  0.7 1.9 fusion.150
  2.5 3.9 %collective-permute-start.1 = (f32[4,16,1024]{2,1,0:T(8,128)}, f32[4,16,1024]{2,1,0:T(8,128)S(1)}, u32[]{:S(2)}, u32[]{:S(2)}) collective-permute-start(f32[4,16,1024]{2,1,0:T(8,128)} %get-tuple-element.46), channel_id=1, source_target_pairs={{0,16},{16,32},{32,48},{48,64},{64,80},{80,96},{96,112},{1,17},{17... | collective-permute-start | bytes 786440 | tf_op jit(solution)/shard_map/ppermute | solution.py:21
  6.5 1.3 collective-permute-start
  7.8 1.8 fusion.151
  9.6 4.0 %collective-permute-start.9 = (f32[4,16,1024]{2,1,0:T(8,128)}, f32[4,16,1024]{2,1,0:T(8,128)S(1)}, u32[]{:S(2)}, u32[]{:S(2)}) collective-permute-start(f32[4,16,1024]{2,1,0:T(8,128)} %get-tuple-element.51), channel_id=1, source_target_pairs={{0,16},{16,32},{32,48},{48,64},{64,80},{80,96},{96,112},{1,17},{17... | collective-permute-start | bytes 786440 | tf_op jit(solution)/shard_map/ppermute | solution.py:21
  13.5 1.3 collective-permute-start.8
  16.0 1.5 reshape.42
  17.7 2.4 constant_dynamic-update-slice_fusion.1
  20.2 1.6 copy-done.7
  22.1 1.2 copy.61
  23.3 3.4 %collective-permute-start.2 = (f32[40,4,1024]{2,0,1:T(8,128)}, f32[40,4,1024]{2,0,1:T(8,128)}, u32[]{:S(2)}, u32[]{:S(2)}) collective-permute-start(f32[40,4,1024]{2,0,1:T(8,128)} %copy.61), channel_id=1, source_target_pairs={{1,0},{2,1},{3,2},{4,3},{5,4},{6,5},{7,6},{8,7},{9,8},{10,9},{11,1... | collective-permute-start | bytes 1966088 | tf_op jit(solution)/shard_map/ppermute | solution.py:23
  27.9 3.4 %collective-permute-start.3 = (f32[40,4,1024]{2,0,1:T(8,128)}, f32[40,4,1024]{2,0,1:T(8,128)}, u32[]{:S(2)}, u32[]{:S(2)}) collective-permute-start(f32[40,4,1024]{2,0,1:T(8,128)} %copy.63), channel_id=1, source_target_pairs={{0,1},{1,2},{2,3},{3,4},{4,5},{5,6},{6,7},{7,8},{8,9},{9,10},{10,1... | collective-permute-start | bytes 1966088 | tf_op jit(solution)/shard_map/ppermute | solution.py:21
  31.4 2.1 constant_dynamic-update-slice_fusion.8
  34.7 1.4 copy.73
  36.1 1.9 collective-permute-start.10
  38.8 4.1 %collective-permute-start.11 = (f32[40,4,1024]{2,0,1:T(8,128)S(1)}, f32[40,4,1024]{2,0,1:T(8,128)S(1)}, u32[]{:S(2)}, u32[]{:S(2)}) collective-permute-start(f32[40,4,1024]{2,0,1:T(8,128)S(1)} %copy.75), channel_id=1, source_target_pairs={{0,1},{1,2},{2,3},{3,4},{4,5},{5,6},{6,7},{7,8},{8,9},{9,10},{10,1... | collective-permute-start | bytes 1966088 | tf_op jit(solution)/shard_map/ppermute | solution.py:21
  42.9 1.5 copy.62
  44.4 1.5 copy.64
  45.9 2.4 collective-permute-done.10
  48.3 1.5 copy.74
  49.9 2.4 select_maximum_fusion.10
  52.8 2.5 select_maximum_fusion.4
  55.3 38.2 %fusion.72 = (f32[32,16,1024]{2,1,0:T(8,128)S(1)}, f32[32,16,1024]{2,1,0:T(8,128)S(1)}) fusion(f32[32,16,1024]{2,1,0:T(8,128)} %param.15, f32[40,16,1024]{2,1,0:T(8,128)} %copy-done.9, f32[40,4,1024]{2,1,0:T(4,128)} %copy-done.12, f32[40,4,1024]{2,1,0:T(4,128)} %copy-done.11, f32[40,24,1032]{2,1,0:T(8,128)S(1)} %select_maximum_fusion.4, ...), kind=kLoop, calls=%fused_computation.142 | loop fusion | flops 45613056 | bytes 93847552 | tf_op jit(solution)/shard_map/add | solution.py:80
  93.5 1.3 collective-permute-start.4
  94.8 4.9 %collective-permute-start.5 = (f32[4,16,1024]{2,1,0:T(8,128)S(1)}, f32[4,16,1024]{2,1,0:T(8,128)S(1)}, u32[]{:S(2)}, u32[]{:S(2)}) collective-permute-start(f32[4,16,1024]{2,1,0:T(8,128)S(1)} %get-tuple-element.38), channel_id=1, source_target_pairs={{0,16},{16,32},{32,48},{48,64},{64,80},{80,96},{96,112},{1,17},{17... | collective-permute-start | bytes 786440 | tf_op jit(solution)/shard_map/ppermute | solution.py:21
  99.9 1.6 collective-permute-done.4
  101.5 1.5 collective-permute-done.5
  104.6 1.9 collective-permute-start.6
  106.5 1.3 copy.69
  107.8 5.0 %collective-permute-start.7 = (f32[40,4,1024]{2,0,1:T(8,128)}, f32[40,4,1024]{2,0,1:T(8,128)}, u32[]{:S(2)}, u32[]{:S(2)}) collective-permute-start(f32[40,4,1024]{2,0,1:T(8,128)} %copy.69), channel_id=1, source_target_pairs={{0,1},{1,2},{2,3},{3,4},{4,5},{5,6},{6,7},{7,8},{8,9},{9,10},{10,1... | collective-permute-start | bytes 1966088 | tf_op jit(solution)/shard_map/ppermute | solution.py:21
  113.6 1.3 collective-permute-start.12
  114.9 4.7 %collective-permute-start.13 = (f32[4,16,1024]{2,1,0:T(8,128)}, f32[4,16,1024]{2,1,0:T(8,128)S(1)}, u32[]{:S(2)}, u32[]{:S(2)}) collective-permute-start(f32[4,16,1024]{2,1,0:T(8,128)} %get-tuple-element.41), channel_id=1, source_target_pairs={{0,16},{16,32},{32,48},{48,64},{64,80},{80,96},{96,112},{1,17},{17... | collective-permute-start | bytes 786440 | tf_op jit(solution)/shard_map/ppermute | solution.py:21
  120.8 1.5 reshape.43
  122.7 2.1 copy.92
  124.7 11.8 %gather_fusion = f32[2048]{0:T(1024)S(1)} fusion(f32[524288]{0:T(1024)S(1)} %bitcast.30, s32[2048]{0:T(1024)S(1)} %broadcast_clamp_fusion), kind=kCustom, calls=%fused_computation | custom fusion | bytes 24576 | tf_op jit(solution)/shard_map/gather | solution.py:82
  136.7 1.9 pad_maximum_fusion.10
  138.9 2.1 collective-permute-start.14
  141.4 3.6 %collective-permute-start.15 = (f32[40,4,1024]{2,0,1:T(8,128)S(1)}, f32[40,4,1024]{2,0,1:T(8,128)S(1)}, u32[]{:S(2)}, u32[]{:S(2)}) collective-permute-start(f32[40,4,1024]{2,0,1:T(8,128)S(1)} %copy.81), channel_id=1, source_target_pairs={{0,1},{1,2},{2,3},{3,4},{4,5},{5,6},{6,7},{7,8},{8,9},{9,10},{10,1... | collective-permute-start | bytes 1966088 | tf_op jit(solution)/shard_map/ppermute | solution.py:21
  145.0 1.5 copy.68
  146.6 1.5 copy.70
  148.1 6.7 %select_maximum_fusion.6 = f32[40,24,1032]{2,1,0:T(8,128)} fusion(f32[40,4,1024]{2,1,0:T(4,128)S(1)} %copy.68, f32[40,4,1024]{2,1,0:T(4,128)S(1)} %copy.70, f32[4,16,1024]{2,1,0:T(8,128)S(1)} %collective-permute-done.4, f32[32,16,1024]{2,1,0:T(8,128)S(1)} %copy-done.3, f32[4,16,1024]{2,1,0:T(8,128)S(1)} %collective-permute-done.5), kind=kLoop, calls=%fused_computation.36 | loop fusion | flops 11888640 | bytes 7895040 | tf_op jit(solution)/shard_map/concatenate | solution.py:19
  155.2 3.7 %pad_maximum_fusion = (f32[40,20,1024]{2,1,0:T(8,128)}, f32[40,20,1024]{2,1,0:T(8,128)}) fusion(f32[40,4,1024]{2,1,0:T(4,128)S(1)} %copy.68, f32[4,16,1024]{2,1,0:T(8,128)S(1)} %collective-permute-done.4, f32[32,16,1024]{2,1,0:T(8,128)S(1)} %copy-done.3, f32[4,16,1024]{2,1,0:T(8,128)S(1)} %collective-permute-done.5, f32[40,4,1024]{2,1,0:T(4,128)S(1)} %copy.70), kind=kLoop, calls=%fused_computation.55 | loop fusion | flops 4915200 | bytes 10485760 | tf_op jit(solution)/shard_map/concatenate | solution.py:19
  159.4 3.7 %pad_maximum_fusion.1 = (f32[40,20,1024]{2,1,0:T(8,128)}, f32[40,20,1024]{2,1,0:T(8,128)}) fusion(f32[40,4,1024]{2,1,0:T(4,128)S(1)} %copy.80, f32[4,16,1024]{2,1,0:T(8,128)S(1)} %collective-permute-done.12, f32[32,16,1024]{2,1,0:T(8,128)S(1)} %copy-done.1, f32[4,16,1024]{2,1,0:T(8,128)S(1)} %collective-permute-done.13, f32[40,4,1024]{2,1,0:T(4,128)S(1)} %copy.82), kind=kLoop, calls=%fused_computation.57 | loop fusion | flops 4915200 | bytes 10485760 | tf_op jit(solution)/shard_map/concatenate | solution.py:19
  163.1 6.4 %select_maximum_fusion = f32[40,24,1032]{2,1,0:T(8,128)} fusion(f32[40,4,1024]{2,1,0:T(4,128)S(1)} %copy.80, f32[40,4,1024]{2,1,0:T(4,128)S(1)} %copy.82, f32[4,16,1024]{2,1,0:T(8,128)S(1)} %collective-permute-done.12, f32[32,16,1024]{2,1,0:T(8,128)S(1)} %copy-done.1, f32[4,16,1024]{2,1,0:T(8,128)S(1)} %collective-permute-done.13), kind=kLoop, calls=%fused_computation.30 | loop fusion | flops 11888640 | bytes 7895040 | tf_op jit(solution)/shard_map/concatenate | solution.py:19
  169.5 63.9 %fusion.12 = (f32[32,16,1024]{2,1,0:T(8,128)}, f32[32,16,1024]{2,1,0:T(8,128)}) fusion(f32[32,16,1024]{2,1,0:T(8,128)} %param.15, f32[32,16,1024]{2,1,0:T(8,128)S(1)} %copy-done.1, f32[4,16,1024]{2,1,0:T(8,128)S(1)} %collective-permute-done.13, f32[4,16,1024]{2,1,0:T(8,128)S(1)} %collective-permute-done.12, f32[40,24,1032]{2,1,0:T(8,128)} %select_maximum_fusion, ...), kind=kLoop, calls=%fused_computation.82 | loop fusion | flops 45613056 | bytes 87031808 | tf_op jit(solution)/shard_map/add | solution.py:81
  233.4 2.1 copy.93
  235.5 11.8 %gather_fusion.1 = f32[2048]{0:T(1024)S(1)} fusion(f32[524288]{0:T(1024)S(1)} %bitcast.29, s32[2048]{0:T(1024)S(1)} %broadcast_clamp_fusion), kind=kCustom, calls=%fused_computation.1 | custom fusion | bytes 24576 | tf_op jit(solution)/shard_map/gather | solution.py:83
  248.1 35.8 %all_to_all.5 = f32[128,2,4]{2,1,0:T(2,128)S(1)} all-to-all(f32[128,2,4]{2,1,0:T(2,128)S(1)} %copy.90), channel_id=1, replica_groups=mesh['gx'=8,'gy'=16] {'gx','gy'}, dimensions={0} | all-to-all | bytes 8192 | tf_op jit(solution)/shard_map/all_to_all | solution.py:100
  (91 shorter events, 12.6 us)
Async XLA Ops:
  0.6 14.2 %copy-start.17 = (s32[4]{0:T(128)S(1)}, s32[4]{0:T(128)}, u32[]{:S(2)}) copy-start(s32[4]{0:T(128)} %param.17) | copy-start | bytes 52
  0.6 14.2 %copy-start.16 = (f32[4,2]{0,1:T(2,128)S(1)}, f32[4,2]{0,1:T(2,128)}, u32[]{:S(2)}) copy-start(f32[4,2]{0,1:T(2,128)} %param.18) | copy-start | bytes 100
  2.5 15.1 %collective-permute-start.1 = (f32[4,16,1024]{2,1,0:T(8,128)}, f32[4,16,1024]{2,1,0:T(8,128)S(1)}, u32[]{:S(2)}, u32[]{:S(2)}) collective-permute-start(f32[4,16,1024]{2,1,0:T(8,128)} %get-tuple-element.46), channel_id=1, source_target_pairs={{0,16},{16,32},{32,48},{48,64},{64,80},{80,96},{96,112},{1,17},{17... | collective-permute-start | bytes 786440 | tf_op jit(solution)/shard_map/ppermute | solution.py:21
  6.5 13.6 %collective-permute-start = (f32[4,16,1024]{2,1,0:T(8,128)}, f32[4,16,1024]{2,1,0:T(8,128)S(1)}, u32[]{:S(2)}, u32[]{:S(2)}) collective-permute-start(f32[4,16,1024]{2,1,0:T(8,128)} %get-tuple-element.45), channel_id=1, source_target_pairs={{16,0},{32,16},{48,32},{64,48},{80,64},{96,80},{112,96},{17,1},{33... | collective-permute-start | bytes 786440 | tf_op jit(solution)/shard_map/ppermute | solution.py:23
  9.6 21.8 %collective-permute-start.9 = (f32[4,16,1024]{2,1,0:T(8,128)}, f32[4,16,1024]{2,1,0:T(8,128)S(1)}, u32[]{:S(2)}, u32[]{:S(2)}) collective-permute-start(f32[4,16,1024]{2,1,0:T(8,128)} %get-tuple-element.51), channel_id=1, source_target_pairs={{0,16},{16,32},{32,48},{48,64},{64,80},{80,96},{96,112},{1,17},{17... | collective-permute-start | bytes 786440 | tf_op jit(solution)/shard_map/ppermute | solution.py:21
  13.5 20.0 %collective-permute-start.8 = (f32[4,16,1024]{2,1,0:T(8,128)S(1)}, f32[4,16,1024]{2,1,0:T(8,128)S(1)}, u32[]{:S(2)}, u32[]{:S(2)}) collective-permute-start(f32[4,16,1024]{2,1,0:T(8,128)S(1)} %get-tuple-element.50), channel_id=1, source_target_pairs={{16,0},{32,16},{48,32},{64,48},{80,64},{96,80},{112,96},{17,1},{33... | collective-permute-start | bytes 786440 | tf_op jit(solution)/shard_map/ppermute | solution.py:23
  16.0 1.5 copy-start.13
  20.1 3.2 %copy-start.4 = (f32[36,16,1024]{2,1,0:T(8,128)}, f32[36,16,1024]{2,1,0:T(8,128)S(1)}, u32[]{:S(2)}) copy-start(f32[36,16,1024]{2,1,0:T(8,128)S(1)} %get-tuple-element.43) | copy-start | bytes 7077892
  20.2 1.6 copy-start.7
  22.1 9.4 %copy-start.6 = (f32[32,16,1024]{2,1,0:T(8,128)S(1)}, f32[32,16,1024]{2,1,0:T(8,128)}, u32[]{:S(2)}) copy-start(f32[32,16,1024]{2,1,0:T(8,128)} %param.14) | copy-start | bytes 6291460
  23.3 19.6 %collective-permute-start.2 = (f32[40,4,1024]{2,0,1:T(8,128)}, f32[40,4,1024]{2,0,1:T(8,128)}, u32[]{:S(2)}, u32[]{:S(2)}) collective-permute-start(f32[40,4,1024]{2,0,1:T(8,128)} %copy.61), channel_id=1, source_target_pairs={{1,0},{2,1},{3,2},{4,3},{5,4},{6,5},{7,6},{8,7},{9,8},{10,9},{11,1... | collective-permute-start | bytes 1966088 | tf_op jit(solution)/shard_map/ppermute | solution.py:23
  27.9 16.4 %collective-permute-start.3 = (f32[40,4,1024]{2,0,1:T(8,128)}, f32[40,4,1024]{2,0,1:T(8,128)}, u32[]{:S(2)}, u32[]{:S(2)}) collective-permute-start(f32[40,4,1024]{2,0,1:T(8,128)} %copy.63), channel_id=1, source_target_pairs={{0,1},{1,2},{2,3},{3,4},{4,5},{5,6},{6,7},{7,8},{8,9},{9,10},{10,1... | collective-permute-start | bytes 1966088 | tf_op jit(solution)/shard_map/ppermute | solution.py:21
  33.6 2.6 copy-start.5
  34.4 3.7 %copy-start.9 = (f32[40,16,1024]{2,1,0:T(8,128)}, f32[40,16,1024]{2,1,0:T(8,128)S(1)}, u32[]{:S(2)}) copy-start(f32[40,16,1024]{2,1,0:T(8,128)S(1)} %get-tuple-element.57) | copy-start | bytes 7864324
  36.1 12.2 %collective-permute-start.10 = (f32[40,4,1024]{2,0,1:T(8,128)}, f32[40,4,1024]{2,0,1:T(8,128)}, u32[]{:S(2)}, u32[]{:S(2)}) collective-permute-start(f32[40,4,1024]{2,0,1:T(8,128)} %copy.73), channel_id=1, source_target_pairs={{1,0},{2,1},{3,2},{4,3},{5,4},{6,5},{7,6},{8,7},{9,8},{10,9},{11,1... | collective-permute-start | bytes 1966088 | tf_op jit(solution)/shard_map/ppermute | solution.py:23
  38.7 11.1 %copy-start.8 = (f32[40,16,1024]{2,1,0:T(8,128)S(1)}, f32[40,16,1024]{2,1,0:T(8,128)}, u32[]{:S(2)}) copy-start(f32[40,16,1024]{2,1,0:T(8,128)} %copy-done.7) | copy-start | bytes 7864324
  38.8 13.6 %collective-permute-start.11 = (f32[40,4,1024]{2,0,1:T(8,128)S(1)}, f32[40,4,1024]{2,0,1:T(8,128)S(1)}, u32[]{:S(2)}, u32[]{:S(2)}) collective-permute-start(f32[40,4,1024]{2,0,1:T(8,128)S(1)} %copy.75), channel_id=1, source_target_pairs={{0,1},{1,2},{2,3},{3,4},{4,5},{5,6},{6,7},{7,8},{8,9},{9,10},{10,1... | collective-permute-start | bytes 1966088 | tf_op jit(solution)/shard_map/ppermute | solution.py:21
  49.9 2.9 %copy-start.11 = (f32[40,4,1024]{2,1,0:T(4,128)}, f32[40,4,1024]{2,1,0:T(4,128)S(1)}, u32[]{:S(2)}) copy-start(f32[40,4,1024]{2,1,0:T(4,128)S(1)} %copy.74) | copy-start | bytes 1966084
  49.9 2.9 %copy-start.10 = (f32[40,16,1024]{2,1,0:T(8,128)S(1)}, f32[40,16,1024]{2,1,0:T(8,128)}, u32[]{:S(2)}) copy-start(f32[40,16,1024]{2,1,0:T(8,128)} %copy-done.9) | copy-start | bytes 7864324
  52.8 2.5 copy-start.12
  55.3 44.7 %copy-start.15 = (s32[256,8]{0,1:T(8,128)S(1)}, s32[256,8]{0,1:T(8,128)}, u32[]{:S(2)}) copy-start(s32[256,8]{0,1:T(8,128)} %param.19) | copy-start | bytes 24580
  93.4 9.9 %copy-start.2 = (f32[32,16,1024]{2,1,0:T(8,128)}, f32[32,16,1024]{2,1,0:T(8,128)S(1)}, u32[]{:S(2)}) copy-start(f32[32,16,1024]{2,1,0:T(8,128)S(1)} %get-tuple-element.25) | copy-start | bytes 6291460
  93.5 19.3 %copy-start = (f32[32,16,1024]{2,1,0:T(8,128)}, f32[32,16,1024]{2,1,0:T(8,128)S(1)}, u32[]{:S(2)}) copy-start(f32[32,16,1024]{2,1,0:T(8,128)S(1)} %get-tuple-element.24) | copy-start | bytes 6291460
  93.5 8.0 %collective-permute-start.4 = (f32[4,16,1024]{2,1,0:T(8,128)S(1)}, f32[4,16,1024]{2,1,0:T(8,128)S(1)}, u32[]{:S(2)}, u32[]{:S(2)}) collective-permute-start(f32[4,16,1024]{2,1,0:T(8,128)S(1)} %get-tuple-element.39), channel_id=1, source_target_pairs={{16,0},{32,16},{48,32},{64,48},{80,64},{96,80},{112,96},{17,1},{33... | collective-permute-start | bytes 786440 | tf_op jit(solution)/shard_map/ppermute | solution.py:23
  94.8 8.2 %collective-permute-start.5 = (f32[4,16,1024]{2,1,0:T(8,128)S(1)}, f32[4,16,1024]{2,1,0:T(8,128)S(1)}, u32[]{:S(2)}, u32[]{:S(2)}) collective-permute-start(f32[4,16,1024]{2,1,0:T(8,128)S(1)} %get-tuple-element.38), channel_id=1, source_target_pairs={{0,16},{16,32},{32,48},{48,64},{64,80},{80,96},{96,112},{1,17},{17... | collective-permute-start | bytes 786440 | tf_op jit(solution)/shard_map/ppermute | solution.py:21
  104.6 40.4 %collective-permute-start.6 = (f32[40,4,1024]{2,0,1:T(8,128)}, f32[40,4,1024]{2,0,1:T(8,128)}, u32[]{:S(2)}, u32[]{:S(2)}) collective-permute-start(f32[40,4,1024]{2,0,1:T(8,128)} %copy.67), channel_id=1, source_target_pairs={{1,0},{2,1},{3,2},{4,3},{5,4},{6,5},{7,6},{8,7},{9,8},{10,9},{11,1... | collective-permute-start | bytes 1966088 | tf_op jit(solution)/shard_map/ppermute | solution.py:23
  107.8 38.8 %collective-permute-start.7 = (f32[40,4,1024]{2,0,1:T(8,128)}, f32[40,4,1024]{2,0,1:T(8,128)}, u32[]{:S(2)}, u32[]{:S(2)}) collective-permute-start(f32[40,4,1024]{2,0,1:T(8,128)} %copy.69), channel_id=1, source_target_pairs={{0,1},{1,2},{2,3},{3,4},{4,5},{5,6},{6,7},{7,8},{8,9},{9,10},{10,1... | collective-permute-start | bytes 1966088 | tf_op jit(solution)/shard_map/ppermute | solution.py:21
  113.6 23.1 %collective-permute-start.12 = (f32[4,16,1024]{2,1,0:T(8,128)}, f32[4,16,1024]{2,1,0:T(8,128)S(1)}, u32[]{:S(2)}, u32[]{:S(2)}) collective-permute-start(f32[4,16,1024]{2,1,0:T(8,128)} %get-tuple-element.40), channel_id=1, source_target_pairs={{16,0},{32,16},{48,32},{64,48},{80,64},{96,80},{112,96},{17,1},{33... | collective-permute-start | bytes 786440 | tf_op jit(solution)/shard_map/ppermute | solution.py:23
  114.9 21.8 %collective-permute-start.13 = (f32[4,16,1024]{2,1,0:T(8,128)}, f32[4,16,1024]{2,1,0:T(8,128)S(1)}, u32[]{:S(2)}, u32[]{:S(2)}) collective-permute-start(f32[4,16,1024]{2,1,0:T(8,128)} %get-tuple-element.41), channel_id=1, source_target_pairs={{0,16},{16,32},{32,48},{48,64},{64,80},{80,96},{96,112},{1,17},{17... | collective-permute-start | bytes 786440 | tf_op jit(solution)/shard_map/ppermute | solution.py:21
  120.8 1.7 copy-start.14
  138.9 9.2 %copy-start.3 = (f32[32,16,1024]{2,1,0:T(8,128)S(1)}, f32[32,16,1024]{2,1,0:T(8,128)}, u32[]{:S(2)}) copy-start(f32[32,16,1024]{2,1,0:T(8,128)} %copy-done.2) | copy-start | bytes 6291460
  138.9 15.9 %collective-permute-start.14 = (f32[40,4,1024]{2,0,1:T(8,128)S(1)}, f32[40,4,1024]{2,0,1:T(8,128)S(1)}, u32[]{:S(2)}, u32[]{:S(2)}) collective-permute-start(f32[40,4,1024]{2,0,1:T(8,128)S(1)} %copy.79), channel_id=1, source_target_pairs={{1,0},{2,1},{3,2},{4,3},{5,4},{6,5},{7,6},{8,7},{9,8},{10,9},{11,1... | collective-permute-start | bytes 1966088 | tf_op jit(solution)/shard_map/ppermute | solution.py:23
  141.4 17.5 %collective-permute-start.15 = (f32[40,4,1024]{2,0,1:T(8,128)S(1)}, f32[40,4,1024]{2,0,1:T(8,128)S(1)}, u32[]{:S(2)}, u32[]{:S(2)}) collective-permute-start(f32[40,4,1024]{2,0,1:T(8,128)S(1)} %copy.81), channel_id=1, source_target_pairs={{0,1},{1,2},{2,3},{3,4},{4,5},{5,6},{6,7},{7,8},{8,9},{9,10},{10,1... | collective-permute-start | bytes 1966088 | tf_op jit(solution)/shard_map/ppermute | solution.py:21
  155.2 4.1 %copy-start.1 = (f32[32,16,1024]{2,1,0:T(8,128)S(1)}, f32[32,16,1024]{2,1,0:T(8,128)}, u32[]{:S(2)}) copy-start(f32[32,16,1024]{2,1,0:T(8,128)} %copy-done) | copy-start | bytes 6291460
where the time goes:
time: 286 us; the launch traced here: 285 us
  other arithmetic  133 us (47%)
  local copies, waits for them, and re-layouts  60.9 us (21%)
  starting transfers between devices  48.2 us (17%)
  blocking collectives  35.8 us (13%)
  waiting for transfers between devices  5.55 us (2%)
    add x1, other arithmetic, body(): 2.0 * born_next - born_now + courant * single_lap(born_next)  63.9 us
    add x1, other arithmetic, body(): 2.0 * born_now - born_old + courant * single_lap(born_now)  38.2 us
    all_to_all x1, blocking collectives, body(): lax.all_to_all(outgoing, ('gx', 'gy'), split_axis=0, concat_axis=0, tiled...  35.8 us
    ppermute x8, starting transfers between devices, with_halo(): lax.ppermute(tail, axis, [(i, (i + 1) % count) for i in range(ends)])  33.7 us
    concatenate x8, other arithmetic, with_halo(): jnp.concatenate([lax.ppermute(tail, axis, [(i, (i + 1) % count) for i in...  27.6 us
    ppermute x8, starting transfers between devices, with_halo(): lax.ppermute(head, axis, [((i + 1) % count, i) for i in range(ends)])  14.4 us
    gather x2, local copies, waits for them, and re-layouts, body(): sample_one = jnp.sum(rcv_weight * born_next.reshape(-1)[rcv_cell], axis=1)  11.9 us
    gather x2, local copies, waits for them, and re-layouts, body(): sample_two = jnp.sum(rcv_weight * born_last.reshape(-1)[rcv_cell], axis=1)  11.9 us
  transfers between devices with their start and end apart: 16, of which 3 were waited for; matrix products, arithmetic and copies ran while one was open for 20% of the time, Pallas kernels for 0%

commit v1 on v0

v1 whole, which is shorter than its diff:
```python
import functools

import jax
import jax.numpy as jnp
from jax import lax
from jax.experimental import pallas as pl
from jax.experimental.pallas import tpu as pltpu
from jax.sharding import PartitionSpec as P

CAP = 4
CENTER = -205.0 / 72.0
WEIGHTS = (8.0 / 5.0, -1.0 / 5.0, 8.0 / 315.0, -1.0 / 560.0)
CX, CY, NZ = 32, 16, 1024
TZ = NZ // 128
BLOCK = (CX, CY, NZ)
XFACE = (8, CY, NZ)
YFACE = (CX, 8, NZ)
F32 = jnp.float32


def iotas():
    sub = lax.broadcasted_iota(jnp.int32, (8, 128), 0)
    lane = lax.broadcasted_iota(jnp.int32, (8, 128), 1)
    return sub, lane


def tile(ref, x, t, z):
    return ref[x, t * 8 : t * 8 + 8, z * 128 : z * 128 + 128]


def put(ref, x, t, z, value):
    ref[x, t * 8 : t * 8 + 8, z * 128 : z * 128 + 128] = value


def pack_y(sub, even, ya, yb, x, z, w0, w1, b0, b1):
    low = jnp.where(sub < 4, w0, pltpu.roll(b0, 4, 0))
    high = jnp.where(sub < 4, pltpu.roll(w1, 4, 0), b1)
    put(ya, x, 0, z, jnp.where(even, high, low))
    put(yb, x, 0, z, jnp.where(even, low, high))


def pack_x(even, xa, xb, wave, born):
    start_a = jnp.where(even, CX - 4, 0)
    start_b = jnp.where(even, 0, CX - 4)
    for i in range(4):
        xa[i] = wave[start_a + i]
        xa[i + 4] = born[start_a + i]
        xb[i] = wave[start_b + i]
        xb[i + 4] = born[start_b + i]


def pack_kernel(place, wave, born, xa, xb, ya, yb):
    sub, _ = iotas()
    even_y = place[1] == 0
    pack_x(place[0] == 0, xa, xb, wave, born)

    def step(x, carry):
        for z in range(TZ):
            pack_y(
                sub, even_y, ya, yb, x, z,
                tile(wave, x, 0, z), tile(wave, x, 1, z), tile(born, x, 0, z), tile(born, x, 1, z),
            )
        return carry

    lax.fori_loop(0, CX, step, 0)


def laplace_rows(ref, x, spots, sub, lane):
    rows = [[tile(ref, x, t, z) for z in range(TZ)] for t in range(2)]
    made = {}

    def turned(t, z, shift, axis):
        shift = shift % (8, 128)[axis]
        if shift == 0:
            return rows[t][z]
        key = (t, z, shift, axis)
        if key not in made:
            made[key] = pltpu.roll(rows[t][z], shift, axis)
        return made[key]

    sums = [[None] * TZ for _ in range(2)]
    for z in range(TZ):
        for t in range(2):
            total = 3.0 * CENTER * rows[t][z]
            for k in range(1, 5):
                near = None
                for s in (k, -k):
                    if s in spots:
                        value = tile(ref, x + s, t, z)
                        near = value if near is None else near + value
                ahead = turned(1, z, -k, 0) if t == 0 else 0.0
                up = jnp.where(sub < 8 - k, turned(t, z, -k, 0), ahead)
                behind = turned(0, z, k, 0) if t == 1 else 0.0
                down = jnp.where(sub >= k, turned(t, z, k, 0), behind)
                ahead = turned(t, z + 1, -k, 1) if z + 1 < TZ else 0.0
                right = jnp.where(lane < 128 - k, turned(t, z, -k, 1), ahead)
                behind = turned(t, z - 1, k, 1) if z > 0 else 0.0
                left = jnp.where(lane >= k, turned(t, z, k, 1), behind)
                flat = (up + down) + (right + left)
                near = flat if near is None else near + flat
                total = total + WEIGHTS[k - 1] * near
            sums[t][z] = total
    return rows, sums


def inner_kernel(cells, amps, wave, wave_old, born, born_old, courant, contrast, wave_part, born_part):
    sub, lane = iotas()

    def one(x, spots):
        rows, sums = laplace_rows(wave, x, spots, sub, lane)
        speed = [[tile(courant, x, t, z) for z in range(TZ)] for t in range(2)]
        for t in range(2):
            for z in range(TZ):
                moved = speed[t][z] * sums[t][z]
                put(wave_part, x, t, z, (2.0 * rows[t][z] - tile(wave_old, x, t, z)) + moved)
                put(born_part, x, t, z, tile(contrast, x, t, z) * moved - tile(born_old, x, t, z))
        rows, sums = laplace_rows(born, x, spots, sub, lane)
        for t in range(2):
            for z in range(TZ):
                moved = 2.0 * rows[t][z] + tile(courant, x, t, z) * sums[t][z]
                put(born_part, x, t, z, tile(born_part, x, t, z) + moved)

    def spots_of(x):
        return {s for s in range(-4, 5) if s and 0 <= x + s < CX}

    for x in range(4):
        one(x, spots_of(x))
    lax.fori_loop(4, CX - 4, lambda x, carry: (one(x, spots_of(8)), carry)[1], 0)
    for x in range(CX - 4, CX):
        one(x, spots_of(x))

    for i in range(4):
        cell = cells[i]
        x = lax.shift_right_logical(cell, 14)
        y = lax.bitwise_and(lax.shift_right_logical(cell, 10), 15)
        z = lax.bitwise_and(cell, NZ - 1)
        row = pl.multiple_of(lax.bitwise_and(y, 8), 8)
        col = pl.multiple_of(lax.bitwise_and(z, NZ - 128), 128)
        here = (sub == lax.bitwise_and(y, 7)) & (lane == lax.bitwise_and(z, 127))
        added = jnp.where(here, amps[i], 0.0)
        at = (x, pl.ds(row, 8), pl.ds(col, 128))
        wave_part[at] = wave_part[at] + added
        born_part[at] = born_part[at] + contrast[at] * added


def fix(place, wave_part, born_part, courant, contrast, xa, xb, ya, yb, wave, born, grid, faces):
    sub, _ = iotas()
    even_x = place[0] == 0
    even_y = place[1] == 0
    low_weights = [jnp.where(sub < k, WEIGHTS[k - 1], 0.0) for k in range(1, 5)]
    high_weights = [jnp.where(sub >= 8 - k, WEIGHTS[k - 1], 0.0) for k in range(1, 5)]

    def turned(value, shift):
        shift = shift % 8
        return value if shift == 0 else pltpu.roll(value, shift, 0)

    def weighted(weights, values):
        total = weights[0] * values[0]
        for w, v in zip(weights[1:], values[1:]):
            total = total + w * v
        return total

    def one(x, side, offset):
        for z in range(TZ):
            from_a, from_b = tile(ya, x, 0, z), tile(yb, x, 0, z)
            low = jnp.where(even_y, from_b, from_a)
            high = jnp.where(even_y, from_a, from_b)
            lows = [turned(low, s) for s in range(8)]
            highs = [turned(high, s) for s in range(8)]
            wave_sums = [
                weighted(low_weights, [lows[(4 + k) % 8] for k in range(1, 5)]),
                weighted(high_weights, [highs[(8 - k) % 8] for k in range(1, 5)]),
            ]
            born_sums = [
                weighted(low_weights, [lows[k] for k in range(1, 5)]),
                weighted(high_weights, [highs[(4 - k) % 8] for k in range(1, 5)]),
            ]
            finals = []
            for t in range(2):
                wave_sum, born_sum = wave_sums[t], born_sums[t]
                if side:
                    for m in range(4):
                        reach = offset + 4 - m if side < 0 else 4 - offset + m
                        if 1 <= reach <= 4:
                            lone, other = (xb, xa) if side < 0 else (xa, xb)
                            w = WEIGHTS[reach - 1]
                            wave_sum = wave_sum + w * jnp.where(even_x, tile(lone, m, t, z), tile(other, m, t, z))
                            born_sum = born_sum + w * jnp.where(even_x, tile(lone, m + 4, t, z), tile(other, m + 4, t, z))
                speed = tile(courant, x, t, z)
                moved = speed * wave_sum
                wave_value = tile(wave_part, x, t, z) + moved
                born_value = tile(born_part, x, t, z) + (tile(contrast, x, t, z) * moved + speed * born_sum)
                put(wave, x, t, z, wave_value)
                put(born, x, t, z, born_value)
                grid[pl.ds(pl.multiple_of(x * 128 + t * 64 + z * 8, 8), 8), :] = born_value
                finals.append((wave_value, born_value))
            if faces is not None:
                (w0, b0), (w1, b1) = finals
                pack_y(sub, even_y, faces[2], faces[3], x, z, w0, w1, b0, b1)

    for x in range(4):
        one(x, -1, x)
    lax.fori_loop(4, CX - 4, lambda x, carry: (one(x, 0, 0), carry)[1], 0)
    for x in range(CX - 4, CX):
        one(x, 1, x - (CX - 4))
    if faces is not None:
        pack_x(even_x, faces[0], faces[1], wave, born)


def fix_kernel(
    place, wave_part, born_part, courant, contrast, rxa, rxb, rya, ryb, wave, born, grid, xa, xb, ya, yb
):
    fix(place, wave_part, born_part, courant, contrast, rxa, rxb, rya, ryb, wave, born, grid, (xa, xb, ya, yb))


def take(rows_at, grid, picks, rows, out):
    def step(g, carry):
        for j in range(4):
            r = g * 4 + j
            for t in range(8):
                rows[pl.ds(r * 8 + t, 1), :] = grid[pl.ds(rows_at[t, r], 1), :]
        return carry

    lax.fori_loop(0, 64, step, 0)

    def total(g, carry):
        part = pl.ds(pl.multiple_of(g * 256, 256), 256)
        value = (rows[part, :] * picks[part, :]).reshape(32, 8, 128)
        out[pl.ds(pl.multiple_of(g * 32, 32), 32), :] = jnp.sum(value, axis=1)
        return carry

    lax.fori_loop(0, 8, total, 0)


def take_kernel(rows_at, grid, picks, out, rows):
    take(rows_at, grid, picks, rows, out)


def last_kernel(
    place, rows_at, wave_part, born_part, courant, contrast, rxa, rxb, rya, ryb,
    picks, first, slots, dest, wave, born, packed, grid, rows, sums,
):
    fix(place, wave_part, born_part, courant, contrast, rxa, rxb, rya, ryb, wave, born, grid, None)
    take(rows_at, grid, picks, rows, sums)
    one = jnp.sum(first[...], axis=1, keepdims=True)
    two = jnp.sum(sums[...], axis=1, keepdims=True)
    lane = lax.broadcasted_iota(jnp.int32, (256, 128), 1)
    spread = jnp.where(lane < 4, one, two) * slots[...]
    owner = lax.broadcasted_iota(jnp.int32, (128, 256), 0)
    chosen = jnp.where(owner == dest[...], 1.0, 0.0).astype(F32)
    packed[...] = jnp.dot(chosen, spread, precision=lax.Precision.HIGHEST, preferred_element_type=F32)


def pairs(count, first):
    found = []
    for i in range(first, count - 1, 2):
        found += [(i, i + 1), (i + 1, i)]
    return found


VM = pl.BlockSpec(memory_space=pltpu.VMEM)
SM = pl.BlockSpec(memory_space=pltpu.SMEM)


def call(kernel, name, args, smem, outs, scratch=(), us=5):
    return pl.pallas_call(
        kernel,
        name=name,
        out_shape=tuple(jax.ShapeDtypeStruct(s, F32) for s in outs),
        in_specs=[SM] * smem + [VM] * (len(args) - smem),
        out_specs=tuple([VM] * len(outs)),
        scratch_shapes=list(scratch),
        compiler_params=pltpu.CompilerParams(vmem_limit_bytes=48 * 1024 * 1024),
        cost_estimate=pl.CostEstimate(flops=0, bytes_accessed=us * 3_000_000, transcendentals=0),
    )(*args)


def exchange(faces):
    xa, xb, ya, yb = faces
    ryb = lax.ppermute(yb, "gy", pairs(16, 1))
    rxb = lax.ppermute(xb, "gx", pairs(8, 1))
    rxa = lax.ppermute(xa, "gx", pairs(8, 0))
    rya = lax.ppermute(ya, "gy", pairs(16, 0))
    return rxa, rxb, rya, ryb


def body(
    wave_old,
    wave_now,
    born_old,
    born_now,
    courant,
    contrast,
    src_cell,
    src_amp,
    rcv_cell,
    rcv_weight,
    rcv_dest,
):
    face_shapes = (XFACE, XFACE, YFACE, YFACE)
    place = jnp.stack([lax.axis_index("gx") % 2, lax.axis_index("gy") % 2]).astype(jnp.int32)

    faces = call(pack_kernel, "pack", (place, wave_now, born_now), 1, face_shapes, us=2)
    halo = exchange(faces)
    parts = call(
        inner_kernel,
        "inner1",
        (src_cell, src_amp[:, 0], wave_now, wave_old, born_now, born_old, courant, contrast),
        2,
        (BLOCK, BLOCK),
        us=10,
    )

    cell = rcv_cell.T
    rows_at = (
        ((cell >> 14) << 7) | (((cell >> 13) & 1) << 6) | (((cell >> 7) & 7) << 3) | ((cell >> 10) & 7)
    )
    lane = lax.broadcasted_iota(jnp.int32, (256, 8, 128), 2)
    picks = jnp.where(lane == (rcv_cell & 127)[:, :, None], rcv_weight[:, :, None], 0.0).reshape(2048, 128)
    dest = rcv_dest[:, 0]
    order = jnp.arange(256, dtype=jnp.int32)
    earlier = (dest[:, None] == dest[None, :]) & (order[None, :] < order[:, None])
    slot = jnp.sum(earlier.astype(jnp.int32), axis=1)
    lane = lax.broadcasted_iota(jnp.int32, (256, 128), 1)
    slots = jnp.where((lane < 8) & (lane % 4 == slot[:, None]), 1.0, 0.0).astype(F32)

    wave_next, born_next, grid, *faces = call(
        fix_kernel,
        "fix1",
        (place, *parts, courant, contrast, *halo),
        1,
        (BLOCK, BLOCK, (4096, 128)) + face_shapes,
        us=4,
    )
    halo = exchange(faces)
    parts = call(
        inner_kernel,
        "inner2",
        (src_cell, src_amp[:, 1], wave_next, wave_now, born_next, born_now, courant, contrast),
        2,
        (BLOCK, BLOCK),
        us=10,
    )
    (first,) = call(
        take_kernel, "take1", (rows_at, grid, picks), 1, ((256, 128),), [pltpu.VMEM((2048, 128), F32)], us=4
    )
    wave_last, born_last, packed = call(
        last_kernel,
        "last",
        (place, rows_at, *parts, courant, contrast, *halo, picks, first, slots, dest[None, :]),
        2,
        (BLOCK, BLOCK, (128, 128)),
        [pltpu.VMEM((4096, 128), F32), pltpu.VMEM((2048, 128), F32), pltpu.VMEM((256, 128), F32)],
        us=8,
    )
    arrived = lax.all_to_all(
        packed.reshape(128, 1, 128), ("gx", "gy"), split_axis=0, concat_axis=0, tiled=True
    )
    gathers = arrived[:, 0, :8].reshape(1, 128, 2, CAP)
    return (wave_next, wave_last, born_next, born_last, gathers)


def solution(mesh):
    placed = (P("gx", "gy", None),) * 6 + (
        P(("gx", "gy")),
        P(("gx", "gy"), None),
        P(("gx", "gy"), None),
        P(("gx", "gy"), None),
        P(("gx", "gy"), None),
    )
    return jax.shard_map(
        body,
        mesh=mesh,
        in_specs=placed,
        out_specs=(P("gx", "gy", None),) * 4 + (P(("gx", "gy"), None, None, None),),
        check_vma=False,
    )
```

time: 286 us -> 108 us (0.38)
  other arithmetic: 133 us -> 0.99 us
  Pallas kernels: 0 us -> 57.5 us
  local copies, waits for them, and re-layouts: 60.9 us -> 9 us
  starting transfers between devices: 48.2 us -> 15 us
  blocking collectives: 35.8 us -> 24.1 us
  waiting for transfers between devices: 5.55 us -> 0.02 us
    add x3 -> x0, other arithmetic: 102 us -> none  [the longest x1 63.9 us: body(): 2.0 * born_next - born_now + courant * single_lap(born_next)]
    pallas_call x0 -> x6, Pallas kernels: none -> 57.5 us  [call(): pl.pallas_call(kernel, name=name, out_shape=tuple((jax.ShapeDtypeStruct(s...]
    ppermute x16 -> x8, starting transfers between devices: 48.2 us -> 15 us  [the longest x2 7.48 us: exchange(): ryb = lax.ppermute(yb, 'gy', pairs(16, 1))]
    concatenate x8 -> x0, other arithmetic: 27.6 us -> none  [with_halo(): jnp.concatenate([lax.ppermute(tail, axis, [(i, (i + 1) % count) for i in...]
    gather x4 -> x0, local copies, waits for them, and re-layouts: 23.8 us -> none  [the longest x2 11.9 us: body(): sample_one = jnp.sum(rcv_weight * born_next.reshape(-1)[rcv_cell], axis=1)]
    slice x14 -> x0, local copies, waits for them, and re-layouts: 12.6 us -> none  [the longest x8 9.04 us: with_halo(): head = lax.slice_in_dim(cells, 0, width, axis=dim)]
    all_to_all x1, blocking collectives: 35.8 us -> 24.1 us  [body(): lax.all_to_all(packed.reshape(128, 1, 128), ('gx', 'gy'), split_axis=0, c...]
    ppermute x8 -> x0, local copies, waits for them, and re-layouts: 8.83 us -> none  [the longest x4 4.96 us: with_halo(): lax.ppermute(head, axis, [((i + 1) % count, i) for i in range(ends)])]
  transfers between devices with their start and end apart: 16 -> 8, of which waited for: 3 -> 0; matrix products, arithmetic and copies ran while one was open for 20% -> 1% of each run, Pallas kernels for 0% -> 32%
where the time goes in v1:
time: 108 us
  Pallas kernels  57.5 us (53%)
  blocking collectives  24.1 us (22%)
  starting transfers between devices  15 us (14%)
  local copies, waits for them, and re-layouts  9 us (8%)
    pallas_call x6, Pallas kernels, call(): pl.pallas_call(kernel, name=name, out_shape=tuple((jax.ShapeDtypeStruct(s...  57.5 us
    all_to_all x1, blocking collectives, body(): lax.all_to_all(packed.reshape(128, 1, 128), ('gx', 'gy'), split_axis=0, c...  24.1 us
    unnamed x26, local copies, waits for them, and re-layouts  8.65 us
    ppermute x2, starting transfers between devices, exchange(): ryb = lax.ppermute(yb, 'gy', pairs(16, 1))  7.48 us
    ppermute x2, starting transfers between devices, exchange(): rxa = lax.ppermute(xa, 'gx', pairs(8, 0))  4.71 us
  transfers between devices with their start and end apart: 8, of which 0 were waited for; matrix products, arithmetic and copies ran while one was open for 1% of the time, Pallas kernels for 32%

profile of v1, /device:TPU:1, one launch (start us, length us, event | category | flops | bytes accessed | tf_op | source)
XLA Modules:
  0.0 107.5 jit_solution(16499572103629367157)
XLA Ops:
  0.6 0.1 pad_add_fusion.place
  0.7 1.6 %copy-done = f32[32,16,1024]{2,1,0:T(8,128)S(1)} copy-done((f32[32,16,1024]{2,1,0:T(8,128)S(1)}, f32[32,16,1024]{2,1,0:T(8,128)}, u32[]{:S(2)}) %copy-start) | copy-done | bytes 2097176
  2.3 2.0 %pack.1 = (f32[8,16,1024]{2,1,0:T(8,128)S(1)}, f32[8,16,1024]{2,1,0:T(8,128)S(1)}, f32[32,8,1024]{2,1,0:T(8,128)S(1)}, f32[32,8,1024]{2,1,0:T(8,128)S(1)}) custom-call(s32[2]{0:T(128)S(1)} %pad_add_fusion.place, f32[32,16,1024]{2,1,0:T(8,128)S(1)} %copy-done, f32[32,16,1024]{2,1,0:T(8,128)} %born_old.3), custom_call_target="tpu_custom_call" | custom-call | bytes 6000000 | tf_op jit(solution)/shard_map/pack/pallas_call | solution.py:266
  4.3 1.5 %collective-permute-start.2 = (f32[32,8,1024]{2,1,0:T(8,128)S(1)}, f32[32,8,1024]{2,1,0:T(8,128)S(1)}, u32[]{:S(2)}, u32[]{:S(2)}) collective-permute-start(f32[32,8,1024]{2,1,0:T(8,128)S(1)} %get-tuple-element.27), channel_id=1, source_target_pairs={{0,1},{1,0},{2,3},{3,2},{4,5},{5,4},{6,7},{7,6},{8,9},{9,8},{10,11... | collective-permute-start | bytes 3145736 | tf_op jit(solution)/shard_map/ppermute | solution.py:283
  5.8 3.6 %collective-permute-start.3 = (f32[32,8,1024]{2,1,0:T(8,128)S(1)}, f32[32,8,1024]{2,1,0:T(8,128)S(1)}, u32[]{:S(2)}, u32[]{:S(2)}) collective-permute-start(f32[32,8,1024]{2,1,0:T(8,128)S(1)} %get-tuple-element.28), channel_id=1, source_target_pairs={{1,2},{2,1},{3,4},{4,3},{5,6},{6,5},{7,8},{8,7},{9,10},{10,9},{11,... | collective-permute-start | bytes 3145736 | tf_op jit(solution)/shard_map/ppermute | solution.py:280
  9.4 1.3 %collective-permute-start = (f32[8,16,1024]{2,1,0:T(8,128)S(1)}, f32[8,16,1024]{2,1,0:T(8,128)S(1)}, u32[]{:S(2)}, u32[]{:S(2)}) collective-permute-start(f32[8,16,1024]{2,1,0:T(8,128)S(1)} %get-tuple-element.25), channel_id=1, source_target_pairs={{0,16},{16,0},{32,48},{48,32},{64,80},{80,64},{96,112},{112,96},{1... | collective-permute-start | bytes 1572872 | tf_op jit(solution)/shard_map/ppermute | solution.py:282
  10.7 0.7 collective-permute-start.1
  11.4 0.0 copy-done.11
  11.4 0.0 copy-done.7
  11.4 15.4 %inner1.1 = (f32[32,16,1024]{2,1,0:T(8,128)S(1)}, f32[32,16,1024]{2,1,0:T(8,128)S(1)}) custom-call(s32[4]{0:T(128)S(1)} %copy-done.7, f32[4]{0:T(128)S(1)} %get-tuple-element.49.amps, f32[32,16,1024]{2,1,0:T(8,128)} %wave_old.3, f32[32,16,1024]{2,1,0:T(8,128)} %wave_old.2, f32[32,16,1024]{2,1,0:T(8,128)} %born_old.3, f32[32,16,1024]{2,1,0:T(8,128)} %born_old.2, ...), custom_call_target="tpu_custom_call" | custom-call | bytes 30000000 | tf_op jit(solution)/shard_map/inner1/pallas_call | solution.py:266
  26.7 0.0 copy-start.4
  26.8 1.3 %copy-done.4 = f32[32,16,1024]{2,1,0:T(8,128)} copy-done((f32[32,16,1024]{2,1,0:T(8,128)}, f32[32,16,1024]{2,1,0:T(8,128)S(1)}, u32[]{:S(2)}) %copy-start.4) | copy-done | bytes 2097176
  28.1 1.3 %copy-done.5 = f32[32,16,1024]{2,1,0:T(8,128)} copy-done((f32[32,16,1024]{2,1,0:T(8,128)}, f32[32,16,1024]{2,1,0:T(8,128)S(1)}, u32[]{:S(2)}) %copy-start.5) | copy-done | bytes 2097176
  29.4 0.0 collective-permute-done.rxa
  29.4 0.0 collective-permute-done.1.rxb
  29.4 0.0 collective-permute-done.2.rya
  29.4 0.0 collective-permute-done.3.ryb
  29.4 0.0 copy-start.8
  29.4 1.0 copy-done.8
  30.4 10.1 %fix1.1 = (f32[32,16,1024]{2,1,0:T(8,128)}, f32[32,16,1024]{2,1,0:T(8,128)}, f32[4096,128]{1,0:T(8,128)}, f32[8,16,1024]{2,1,0:T(8,128)}, f32[8,16,1024]{2,1,0:T...) custom-call(s32[2]{0:T(128)S(1)} %pad_add_fusion.place, f32[32,16,1024]{2,1,0:T(8,128)} %copy-done.4, ...), custom_call_target="tpu_custom_call" | custom-call | bytes 12000000 | tf_op jit(solution)/shard_map/fix1/pallas_call | solution.py:266
  40.5 0.0 collective-permute-start.6
  40.5 3.9 %collective-permute-start.7 = (f32[32,8,1024]{2,1,0:T(8,128)}, f32[32,8,1024]{2,1,0:T(8,128)S(1)}, u32[]{:S(2)}, u32[]{:S(2)}) collective-permute-start(f32[32,8,1024]{2,1,0:T(8,128)} %get-tuple-element.36), channel_id=1, source_target_pairs={{1,2},{2,1},{3,4},{4,3},{5,6},{6,5},{7,8},{8,7},{9,10},{10,9},{11,... | collective-permute-start | bytes 3145736 | tf_op jit(solution)/shard_map/ppermute | solution.py:280
  44.5 0.0 copy-done.6
  44.5 0.2 convert_reduce_fusion
  44.7 0.1 fusion.3.slots
  44.8 3.4 %collective-permute-start.4 = (f32[8,16,1024]{2,1,0:T(8,128)}, f32[8,16,1024]{2,1,0:T(8,128)S(1)}, u32[]{:S(2)}, u32[]{:S(2)}) collective-permute-start(f32[8,16,1024]{2,1,0:T(8,128)} %get-tuple-element.33), channel_id=1, source_target_pairs={{0,16},{16,0},{32,48},{48,32},{64,80},{80,64},{96,112},{112,96},{1... | collective-permute-start | bytes 1572872 | tf_op jit(solution)/shard_map/ppermute | solution.py:282
  48.2 0.7 collective-permute-start.5
  48.9 0.0 copy-done.9
  48.9 0.1 copy.24
  49.1 0.1 eq.39
  49.2 0.0 copy-done.10
  49.2 0.1 copy.25
  49.3 0.1 broadcast_in_dim.27
  49.4 0.6 fusion.picks
  50.0 0.0 copy-start.1
  50.1 15.5 %inner2.1 = (f32[32,16,1024]{2,1,0:T(8,128)S(1)}, f32[32,16,1024]{2,1,0:T(8,128)S(1)}) custom-call(s32[4]{0:T(128)S(1)} %copy-done.7, f32[4]{0:T(128)S(1)} %get-tuple-element.48.amps, f32[32,16,1024]{2,1,0:T(8,128)} %get-tuple-element.41.wave, f32[32,16,1024]{2,1,0:T(8,128)} %wave_old.3, f32[32,16,1024]{2,1,0:T(8,128)} %get-tuple-element.43.born, ...), custom_call_target="tpu_custom_call" | custom-call | bytes 30000000 | tf_op jit(solution)/shard_map/inner2/pallas_call | solution.py:266
  65.6 0.0 copy-start.2
  65.6 1.3 %copy-done.2 = f32[32,16,1024]{2,1,0:T(8,128)} copy-done((f32[32,16,1024]{2,1,0:T(8,128)}, f32[32,16,1024]{2,1,0:T(8,128)S(1)}, u32[]{:S(2)}) %copy-start.2) | copy-done | bytes 2097176
  66.9 1.4 %copy-done.3 = f32[32,16,1024]{2,1,0:T(8,128)} copy-done((f32[32,16,1024]{2,1,0:T(8,128)}, f32[32,16,1024]{2,1,0:T(8,128)S(1)}, u32[]{:S(2)}) %copy-start.3) | copy-done | bytes 2097176
  68.2 0.0 copy-done.1
  68.2 3.6 %take1.1.first = f32[256,128]{1,0:T(8,128)S(1)} custom-call(s32[8,256]{1,0:T(8,128)S(1)} %get-tuple-element.47.rows_at, f32[4096,128]{1,0:T(8,128)S(1)} %copy-done.1, f32[2048,128]{1,0:T(8,128)S(1)} %fusion.picks), custom_call_target="tpu_custom_call" | custom-call | bytes 12000000 | tf_op jit(solution)/shard_map/take1/pallas_call | solution.py:266
  71.9 0.0 collective-permute-done.4.rxa
  71.9 0.0 collective-permute-done.5.rxb
  71.9 0.0 collective-permute-done.6.rya
  71.9 0.0 collective-permute-done.7.ryb
  71.9 10.8 %last.1 = (f32[32,16,1024]{2,1,0:T(8,128)}, f32[32,16,1024]{2,1,0:T(8,128)}, f32[128,128]{1,0:T(8,128)S(1)}) custom-call(s32[2]{0:T(128)S(1)} %pad_add_fusion.place, s32[8,256]{1,0:T(8,128)S(1)} %get-tuple-element.47.rows_at, f32[32,16,1024]{2,1,0:T(8,128)} %copy-done.2, f32[32,16,1024]{2,1,0:T(8,128)} %copy-done.3, f32[32,16,1024]{2,1,0:T(8,128)} %courant.7, ...), custom_call_target="tpu_custom_call" | custom-call | bytes 24000000 | tf_op jit(solution)/shard_map/last/pallas_call | solution.py:266
  82.7 24.1 %all_to_all.5 = f32[128,1,128]{2,1,0:T(1,128)S(1)} all-to-all(f32[128,1,128]{2,1,0:T(1,128)S(1)} %bitcast.15), channel_id=1, replica_groups=mesh['gx'=8,'gy'=16] {'gx','gy'}, dimensions={0} | all-to-all | bytes 131072 | tf_op jit(solution)/shard_map/all_to_all | solution.py:356
  106.8 0.7 copy.28
  (12 shorter events, 0.0 us)
Async XLA Ops:
  0.7 1.6 %copy-start = (f32[32,16,1024]{2,1,0:T(8,128)S(1)}, f32[32,16,1024]{2,1,0:T(8,128)}, u32[]{:S(2)}) copy-start(f32[32,16,1024]{2,1,0:T(8,128)} %wave_old.3) | copy-start | bytes 6291460
  2.3 9.0 %copy-start.11 = (f32[4,2]{0,1:T(2,128)S(1)}, f32[4,2]{0,1:T(2,128)}, u32[]{:S(2)}) copy-start(f32[4,2]{0,1:T(2,128)} %param.18) | copy-start | bytes 100
  2.3 9.1 %copy-start.7 = (s32[4]{0:T(128)S(1)}, s32[4]{0:T(128)}, u32[]{:S(2)}) copy-start(s32[4]{0:T(128)} %cells.3) | copy-start | bytes 52
  4.3 25.1 %collective-permute-start.2 = (f32[32,8,1024]{2,1,0:T(8,128)S(1)}, f32[32,8,1024]{2,1,0:T(8,128)S(1)}, u32[]{:S(2)}, u32[]{:S(2)}) collective-permute-start(f32[32,8,1024]{2,1,0:T(8,128)S(1)} %get-tuple-element.27), channel_id=1, source_target_pairs={{0,1},{1,0},{2,3},{3,2},{4,5},{5,4},{6,7},{7,6},{8,9},{9,8},{10,11... | collective-permute-start | bytes 3145736 | tf_op jit(solution)/shard_map/ppermute | solution.py:283
  5.8 23.6 %collective-permute-start.3 = (f32[32,8,1024]{2,1,0:T(8,128)S(1)}, f32[32,8,1024]{2,1,0:T(8,128)S(1)}, u32[]{:S(2)}, u32[]{:S(2)}) collective-permute-start(f32[32,8,1024]{2,1,0:T(8,128)S(1)} %get-tuple-element.28), channel_id=1, source_target_pairs={{1,2},{2,1},{3,4},{4,3},{5,6},{6,5},{7,8},{8,7},{9,10},{10,9},{11,... | collective-permute-start | bytes 3145736 | tf_op jit(solution)/shard_map/ppermute | solution.py:280
  9.4 20.0 %collective-permute-start = (f32[8,16,1024]{2,1,0:T(8,128)S(1)}, f32[8,16,1024]{2,1,0:T(8,128)S(1)}, u32[]{:S(2)}, u32[]{:S(2)}) collective-permute-start(f32[8,16,1024]{2,1,0:T(8,128)S(1)} %get-tuple-element.25), channel_id=1, source_target_pairs={{0,16},{16,0},{32,48},{48,32},{64,80},{80,64},{96,112},{112,96},{1... | collective-permute-start | bytes 1572872 | tf_op jit(solution)/shard_map/ppermute | solution.py:282
  10.7 18.7 %collective-permute-start.1 = (f32[8,16,1024]{2,1,0:T(8,128)S(1)}, f32[8,16,1024]{2,1,0:T(8,128)S(1)}, u32[]{:S(2)}, u32[]{:S(2)}) collective-permute-start(f32[8,16,1024]{2,1,0:T(8,128)S(1)} %get-tuple-element.26), channel_id=1, source_target_pairs={{16,32},{32,16},{48,64},{64,48},{80,96},{96,80},{17,33},{33,17},{4... | collective-permute-start | bytes 1572872 | tf_op jit(solution)/shard_map/ppermute | solution.py:281
  26.7 1.3 %copy-start.4 = (f32[32,16,1024]{2,1,0:T(8,128)}, f32[32,16,1024]{2,1,0:T(8,128)S(1)}, u32[]{:S(2)}) copy-start(f32[32,16,1024]{2,1,0:T(8,128)S(1)} %get-tuple-element.23.wave_part) | copy-start | bytes 6291460
  28.1 1.3 %copy-start.5 = (f32[32,16,1024]{2,1,0:T(8,128)}, f32[32,16,1024]{2,1,0:T(8,128)S(1)}, u32[]{:S(2)}) copy-start(f32[32,16,1024]{2,1,0:T(8,128)S(1)} %get-tuple-element.24.born_part) | copy-start | bytes 6291460
  29.4 1.0 copy-start.8
  30.4 14.1 %copy-start.6 = (s32[256,1]{0,1:T(1,128)S(1)}, s32[256,1]{0,1:T(1,128)}, u32[]{:S(2)}) copy-start(s32[256,1]{0,1:T(1,128)} %param.21) | copy-start | bytes 3076
  30.4 18.5 %copy-start.9 = (s32[256,8]{0,1:T(8,128)S(1)}, s32[256,8]{0,1:T(8,128)}, u32[]{:S(2)}) copy-start(s32[256,8]{0,1:T(8,128)} %param.19) | copy-start | bytes 24580
  30.4 18.8 %copy-start.10 = (f32[256,8]{0,1:T(8,128)S(1)}, f32[256,8]{0,1:T(8,128)}, u32[]{:S(2)}) copy-start(f32[256,8]{0,1:T(8,128)} %param.20) | copy-start | bytes 24580
  40.5 31.4 %collective-permute-start.6 = (f32[32,8,1024]{2,1,0:T(8,128)}, f32[32,8,1024]{2,1,0:T(8,128)S(1)}, u32[]{:S(2)}, u32[]{:S(2)}) collective-permute-start(f32[32,8,1024]{2,1,0:T(8,128)} %get-tuple-element.35), channel_id=1, source_target_pairs={{0,1},{1,0},{2,3},{3,2},{4,5},{5,4},{6,7},{7,6},{8,9},{9,8},{10,11... | collective-permute-start | bytes 3145736 | tf_op jit(solution)/shard_map/ppermute | solution.py:283
  40.5 31.4 %collective-permute-start.7 = (f32[32,8,1024]{2,1,0:T(8,128)}, f32[32,8,1024]{2,1,0:T(8,128)S(1)}, u32[]{:S(2)}, u32[]{:S(2)}) collective-permute-start(f32[32,8,1024]{2,1,0:T(8,128)} %get-tuple-element.36), channel_id=1, source_target_pairs={{1,2},{2,1},{3,4},{4,3},{5,6},{6,5},{7,8},{8,7},{9,10},{10,9},{11,... | collective-permute-start | bytes 3145736 | tf_op jit(solution)/shard_map/ppermute | solution.py:280
  44.8 27.1 %collective-permute-start.4 = (f32[8,16,1024]{2,1,0:T(8,128)}, f32[8,16,1024]{2,1,0:T(8,128)S(1)}, u32[]{:S(2)}, u32[]{:S(2)}) collective-permute-start(f32[8,16,1024]{2,1,0:T(8,128)} %get-tuple-element.33), channel_id=1, source_target_pairs={{0,16},{16,0},{32,48},{48,32},{64,80},{80,64},{96,112},{112,96},{1... | collective-permute-start | bytes 1572872 | tf_op jit(solution)/shard_map/ppermute | solution.py:282
  48.2 23.7 %collective-permute-start.5 = (f32[8,16,1024]{2,1,0:T(8,128)}, f32[8,16,1024]{2,1,0:T(8,128)S(1)}, u32[]{:S(2)}, u32[]{:S(2)}) collective-permute-start(f32[8,16,1024]{2,1,0:T(8,128)} %get-tuple-element.34), channel_id=1, source_target_pairs={{16,32},{32,16},{48,64},{64,48},{80,96},{96,80},{17,33},{33,17},{4... | collective-permute-start | bytes 1572872 | tf_op jit(solution)/shard_map/ppermute | solution.py:281
  50.0 18.2 %copy-start.1 = (f32[4096,128]{1,0:T(8,128)S(1)}, f32[4096,128]{1,0:T(8,128)}, u32[]{:S(2)}) copy-start(f32[4096,128]{1,0:T(8,128)} %get-tuple-element.37.grid) | copy-start | bytes 6291460
  65.6 1.3 %copy-start.2 = (f32[32,16,1024]{2,1,0:T(8,128)}, f32[32,16,1024]{2,1,0:T(8,128)S(1)}, u32[]{:S(2)}) copy-start(f32[32,16,1024]{2,1,0:T(8,128)S(1)} %get-tuple-element.31.wave_part) | copy-start | bytes 6291460
  66.9 1.4 %copy-start.3 = (f32[32,16,1024]{2,1,0:T(8,128)}, f32[32,16,1024]{2,1,0:T(8,128)S(1)}, u32[]{:S(2)}) copy-start(f32[32,16,1024]{2,1,0:T(8,128)S(1)} %get-tuple-element.32.born_part) | copy-start | bytes 6291460

commit v2 on v1

v2 whole, which is shorter than its diff:
```python
import jax
import jax.numpy as jnp
from jax import lax
from jax.experimental import pallas as pl
from jax.experimental.pallas import tpu as pltpu
from jax.sharding import PartitionSpec as P

CAP = 4
SCALE = 5040.0
CENTER = -3.0 * 14350.0
WEIGHTS = (8064.0, -1008.0, 128.0, -9.0)
CX, CY, NZ = 32, 16, 1024
TZ = NZ // 128
BLOCK = (CX, CY, NZ)
XFACE = (8, CY, NZ)
YFACE = (CX, 8, NZ)
STRIP = 24
LAYER = TZ * STRIP
ROWS = (CX + 8) * LAYER + 8
F32 = jnp.float32
BF16 = jnp.bfloat16


def iotas():
    sub = lax.broadcasted_iota(jnp.int32, (8, 128), 0)
    lane = lax.broadcasted_iota(jnp.int32, (8, 128), 1)
    return sub, lane


def tile(ref, x, t, z):
    return ref[x, t * 8 : t * 8 + 8, z * 128 : z * 128 + 128]


def put(ref, x, t, z, value):
    ref[x, t * 8 : t * 8 + 8, z * 128 : z * 128 + 128] = value


def strip(x, t, z, shift=0):
    return pl.ds(x * LAYER + (4 * LAYER + z * STRIP + 8 + t * 8 + shift), 8)


def clear(*refs):
    zero = jnp.zeros((8, 128), F32)

    def gaps(x, carry):
        for z in range(TZ):
            for ref in refs:
                ref[pl.ds(pl.multiple_of(x * LAYER + z * STRIP, 8), 8), :] = zero
        return carry

    def layer(i, carry):
        x = jnp.where(i < 4, i, i + CX)
        for z in range(TZ):
            for t in range(2):
                for ref in refs:
                    ref[pl.ds(pl.multiple_of(x * LAYER + z * STRIP + 8 + t * 8, 8), 8), :] = zero
        return carry

    lax.fori_loop(0, CX + 8, gaps, 0)
    lax.fori_loop(0, 8, layer, 0)
    for ref in refs:
        ref[pl.ds(ROWS - 8, 8), :] = zero


def pack_y(sub, even, ya, yb, x, z, w0, w1, b0, b1):
    low = jnp.where(sub < 4, w0, pltpu.roll(b0, 4, 0))
    high = jnp.where(sub < 4, pltpu.roll(w1, 4, 0), b1)
    put(ya, x, 0, z, jnp.where(even, high, low))
    put(yb, x, 0, z, jnp.where(even, low, high))


def pack_x(even, xa, xb, wave, born):
    start_a = jnp.where(even, CX - 4, 0)
    start_b = jnp.where(even, 0, CX - 4)
    for i in range(4):
        xa[i] = wave[start_a + i]
        xa[i + 4] = born[start_a + i]
        xb[i] = wave[start_b + i]
        xb[i + 4] = born[start_b + i]


def pack_kernel(place, wave_in, born_in, wave_rows, born_rows, xa, xb, ya, yb, wave, born, sems):
    sub, _ = iotas()
    even_y = place[1] == 0
    parts = 4
    each = CX // parts

    def copies(c):
        part = pl.ds(c * each, each)
        return (
            pltpu.make_async_copy(wave_in.at[part], wave.at[part], sems.at[0, c]),
            pltpu.make_async_copy(born_in.at[part], born.at[part], sems.at[1, c]),
        )

    for c in range(parts):
        for copy in copies(c):
            copy.start()
    clear(wave_rows, born_rows)
    for c in range(parts):
        for copy in copies(c):
            copy.wait()

        def step(x, carry):
            for z in range(TZ):
                w0, w1, b0, b1 = tile(wave, x, 0, z), tile(wave, x, 1, z), tile(born, x, 0, z), tile(born, x, 1, z)
                pack_y(sub, even_y, ya, yb, x, z, w0, w1, b0, b1)
                wave_rows[strip(x, 0, z), :] = w0
                wave_rows[strip(x, 1, z), :] = w1
                born_rows[strip(x, 0, z), :] = b0
                born_rows[strip(x, 1, z), :] = b1
            return carry

        lax.fori_loop(c * each, (c + 1) * each, step, 0)
    pack_x(place[0] == 0, xa, xb, wave, born)


def along_z(ref, high, low, table, out):
    zero = jnp.zeros((CX * CY, 128), BF16)
    for half in (high, low):
        half[:, 0:128] = zero
        half[:, 128 + NZ : 256 + NZ] = zero

    def split(x, carry):
        rows = pl.ds(pl.multiple_of(x * CY, CY), CY)
        for z in range(TZ):
            value = ref[pl.ds(pl.multiple_of(x * LAYER + (4 * LAYER + z * STRIP + 8), 8), CY), :]
            top = value.astype(BF16)
            high[rows, 128 + z * 128 : 256 + z * 128] = top
            low[rows, 128 + z * 128 : 256 + z * 128] = (value - top.astype(F32)).astype(BF16)
        return carry

    lax.fori_loop(0, CX, split, 0, unroll=2)
    for c in range(NZ // 256):
        window = slice(c * 256, c * 256 + 512)
        both = jnp.concatenate([high[:, window], low[:, window]], axis=1)
        out[:, c * 256 : c * 256 + 256] = jnp.dot(both, table[...], preferred_element_type=F32)


def spread(ref, z_sum, x, t, z):
    here = ref[strip(x, t, z), :]
    total = CENTER * here + z_sum[pl.ds(pl.multiple_of(x * CY + t * 8, 8), 8), z * 128 : z * 128 + 128]
    for k in range(1, 5):
        flat = ref[strip(x, t, z, k), :] + ref[strip(x, t, z, -k), :]
        deep = ref[strip(x, t, z, k * LAYER), :] + ref[strip(x, t, z, -k * LAYER), :]
        total = total + WEIGHTS[k - 1] * (flat + deep)
    return here, total


def add_sources(cells, amps, contrast, wave_part, born_part):
    sub, lane = iotas()
    for i in range(4):
        cell = cells[i]
        x = lax.shift_right_logical(cell, 14)
        y = lax.bitwise_and(lax.shift_right_logical(cell, 10), 15)
        z = lax.bitwise_and(cell, NZ - 1)
        row = pl.multiple_of(lax.bitwise_and(y, 8), 8)
        col = pl.multiple_of(lax.bitwise_and(z, NZ - 128), 128)
        here = (sub == lax.bitwise_and(y, 7)) & (lane == lax.bitwise_and(z, 127))
        added = jnp.where(here, amps[i], 0.0)
        at = (x, pl.ds(row, 8), pl.ds(col, 128))
        wave_part[at] = wave_part[at] + added
        born_part[at] = born_part[at] + contrast[at] * added


def inner_first(
    cells, amps, wave, born, table, wave_old_in, born_old_in, courant_in, contrast_in,
    wave_part, born_part, courant, contrast, wave_old, born_old, high, low, wave_z, born_z, sems,
):
    copies = [
        pltpu.make_async_copy(a, b, sems.at[i])
        for i, (a, b) in enumerate(
            ((wave_old_in, wave_old), (born_old_in, born_old), (courant_in, courant), (contrast_in, contrast))
        )
    ]
    for copy in copies:
        copy.start()
    along_z(wave, high, low, table, wave_z)
    along_z(born, high, low, table, born_z)
    for copy in copies:
        copy.wait()

    def step(x, carry):
        for z in range(TZ):
            for t in range(2):
                speed = tile(courant, x, t, z) * (1.0 / SCALE)
                put(courant, x, t, z, speed)
                here, total = spread(wave, wave_z, x, t, z)
                moved = speed * total
                put(wave_part, x, t, z, (2.0 * here - tile(wave_old, x, t, z)) + moved)
                here, total = spread(born, born_z, x, t, z)
                moved = speed * total + tile(contrast, x, t, z) * moved
                put(born_part, x, t, z, (2.0 * here - tile(born_old, x, t, z)) + moved)
        return carry

    lax.fori_loop(0, CX, step, 0)
    add_sources(cells, amps, contrast, wave_part, born_part)


def inner_second(
    cells, amps, rows_at, wave, born, table, wave_old, born_old, courant, contrast, picks, wave_now, born_now,
    wave_part, born_part, first, wave_out, born_out, high, low, wave_z, born_z, rows, sems,
):
    copies = [
        pltpu.make_async_copy(wave_now, wave_out, sems.at[0]),
        pltpu.make_async_copy(born_now, born_out, sems.at[1]),
    ]
    for copy in copies:
        copy.start()
    along_z(wave, high, low, table, wave_z)
    along_z(born, high, low, table, born_z)

    def step(x, carry):
        for z in range(TZ):
            for t in range(2):
                speed = tile(courant, x, t, z)
                here, total = spread(wave, wave_z, x, t, z)
                moved = speed * total
                put(wave_part, x, t, z, (2.0 * here - wave_old[strip(x, t, z), :]) + moved)
                here, total = spread(born, born_z, x, t, z)
                moved = speed * total + tile(contrast, x, t, z) * moved
                put(born_part, x, t, z, (2.0 * here - born_old[strip(x, t, z), :]) + moved)
        return carry

    lax.fori_loop(0, CX, step, 0)
    add_sources(cells, amps, contrast, wave_part, born_part)
    take(rows_at, born, picks, rows, first)
    for copy in copies:
        copy.wait()


def fix(place, wave_part, born_part, courant, contrast, xa, xb, ya, yb, wave, born, wave_rows, born_rows, faces):
    sub, _ = iotas()
    even_x = place[0] == 0
    even_y = place[1] == 0
    part = lax.bitwise_and(sub, 3)
    low_weights = [jnp.where(part < k, WEIGHTS[k - 1], 0.0) for k in range(1, 4)]
    high_weights = [jnp.where(part >= 4 - k, WEIGHTS[k - 1], 0.0) for k in range(1, 4)]

    def one(x, side, offset):
        for z in range(TZ):
            from_a, from_b = tile(ya, x, 0, z), tile(yb, x, 0, z)
            low = jnp.where(even_y, from_b, from_a)
            high = jnp.where(even_y, from_a, from_b)
            low_sum, high_sum = WEIGHTS[3] * low, WEIGHTS[3] * high
            for k in range(1, 4):
                low_sum = low_sum + low_weights[k - 1] * pltpu.roll(low, 4 + k, 0)
                high_sum = high_sum + high_weights[k - 1] * pltpu.roll(high, 4 - k, 0)
            wave_sums = [
                jnp.where(sub < 4, low_sum, 0.0),
                jnp.where(sub < 4, 0.0, pltpu.roll(high_sum, 4, 0)),
            ]
            born_sums = [
                jnp.where(sub < 4, pltpu.roll(low_sum, 4, 0), 0.0),
                jnp.where(sub < 4, 0.0, high_sum),
            ]
            finals = []
            for t in range(2):
                wave_sum, born_sum = wave_sums[t], born_sums[t]
                if side:
                    for m in range(4):
                        reach = offset + 4 - m if side < 0 else 4 - offset + m
                        if 1 <= reach <= 4:
                            lone, other = (xb, xa) if side < 0 else (xa, xb)
                            w = WEIGHTS[reach - 1]
                            wave_sum = wave_sum + w * jnp.where(even_x, tile(lone, m, t, z), tile(other, m, t, z))
                            born_sum = born_sum + w * jnp.where(even_x, tile(lone, m + 4, t, z), tile(other, m + 4, t, z))
                speed = tile(courant, x, t, z)
                moved = speed * wave_sum
                wave_value = tile(wave_part, x, t, z) + moved
                born_value = tile(born_part, x, t, z) + (tile(contrast, x, t, z) * moved + speed * born_sum)
                put(wave, x, t, z, wave_value)
                put(born, x, t, z, born_value)
                if wave_rows is not None:
                    wave_rows[strip(x, t, z), :] = wave_value
                born_rows[strip(x, t, z), :] = born_value
                finals.append((wave_value, born_value))
            if faces is not None:
                (w0, b0), (w1, b1) = finals
                pack_y(sub, even_y, faces[2], faces[3], x, z, w0, w1, b0, b1)

    for x in range(4):
        one(x, -1, x)
    lax.fori_loop(4, CX - 4, lambda x, carry: (one(x, 0, 0), carry)[1], 0)
    for x in range(CX - 4, CX):
        one(x, 1, x - (CX - 4))
    if faces is not None:
        pack_x(even_x, faces[0], faces[1], wave, born)


def fix_kernel(
    place, wave_part, born_part, courant, contrast, rxa, rxb, rya, ryb,
    wave, born, wave_rows, born_rows, xa, xb, ya, yb,
):
    clear(wave_rows, born_rows)
    fix(
        place, wave_part, born_part, courant, contrast, rxa, rxb, rya, ryb,
        wave, born, wave_rows, born_rows, (xa, xb, ya, yb),
    )


def take(rows_at, grid, picks, rows, out):
    def step(g, carry):
        for j in range(4):
            r = g * 4 + j
            for t in range(8):
                rows[pl.ds(r * 8 + t, 1), :] = grid[pl.ds(rows_at[t, r], 1), :]
        return carry

    lax.fori_loop(0, 64, step, 0)

    def total(g, carry):
        part = pl.ds(pl.multiple_of(g * 256, 256), 256)
        value = (rows[part, :] * picks[part, :]).reshape(32, 8, 128)
        out[pl.ds(pl.multiple_of(g * 32, 32), 32), :] = jnp.sum(value, axis=1)
        return carry

    lax.fori_loop(0, 8, total, 0)


def last_kernel(
    place, rows_at, wave_part, born_part, courant, contrast, rxa, rxb, rya, ryb,
    picks, first, slots, dest, wave_out, born_out, packed, wave, born, grid, rows, sums, sems,
):
    fix(place, wave_part, born_part, courant, contrast, rxa, rxb, rya, ryb, wave, born, None, grid, None)
    copies = [
        pltpu.make_async_copy(wave, wave_out, sems.at[0]),
        pltpu.make_async_copy(born, born_out, sems.at[1]),
    ]
    for copy in copies:
        copy.start()
    take(rows_at, grid, picks, rows, sums)
    one = jnp.sum(first[...], axis=1, keepdims=True)
    two = jnp.sum(sums[...], axis=1, keepdims=True)
    lane = lax.broadcasted_iota(jnp.int32, (256, 128), 1)
    spread_out = jnp.where(lane < 4, one, two) * slots[...]
    owner = lax.broadcasted_iota(jnp.int32, (128, 256), 0)
    chosen = jnp.where(owner == dest[...], 1.0, 0.0).astype(F32)
    packed[...] = jnp.dot(chosen, spread_out, precision=lax.Precision.HIGHEST, preferred_element_type=F32)
    for copy in copies:
        copy.wait()


def pairs(count, first):
    found = []
    for i in range(first, count - 1, 2):
        found += [(i, i + 1), (i + 1, i)]
    return found


VM = pl.BlockSpec(memory_space=pltpu.VMEM)
SM = pl.BlockSpec(memory_space=pltpu.SMEM)
HB = pl.BlockSpec(memory_space=pltpu.HBM)


def kept(shape):
    return VM, pltpu.VMEM(shape, F32)


def plain(shape):
    return VM, jax.ShapeDtypeStruct(shape, F32)


def away(shape):
    return HB, jax.ShapeDtypeStruct(shape, F32)


def call(kernel, name, args, specs, outs, scratch, mib, us):
    return pl.pallas_call(
        kernel,
        name=name,
        out_shape=tuple(o[1] for o in outs),
        in_specs=specs,
        out_specs=tuple(o[0] for o in outs),
        scratch_shapes=list(scratch),
        compiler_params=pltpu.CompilerParams(vmem_limit_bytes=mib * 1024 * 1024),
        cost_estimate=pl.CostEstimate(flops=0, bytes_accessed=us * 3_000_000, transcendentals=0),
    )(*args)


def exchange(faces):
    xa, xb, ya, yb = faces
    ryb = lax.ppermute(yb, "gy", pairs(16, 1))
    rxb = lax.ppermute(xb, "gx", pairs(8, 1))
    rxa = lax.ppermute(xa, "gx", pairs(8, 0))
    rya = lax.ppermute(ya, "gy", pairs(16, 0))
    return rxa, rxb, rya, ryb


def z_table():
    source = lax.broadcasted_iota(jnp.int32, (1024, 256), 0) % 512 - 128
    target = lax.broadcasted_iota(jnp.int32, (1024, 256), 1)
    gap = jnp.abs(source - target)
    table = jnp.zeros((1024, 256), F32)
    for k in range(1, 5):
        table = jnp.where(gap == k, WEIGHTS[k - 1], table)
    return table.astype(BF16)


def body(
    wave_old,
    wave_now,
    born_old,
    born_now,
    courant,
    contrast,
    src_cell,
    src_amp,
    rcv_cell,
    rcv_weight,
    rcv_dest,
):
    place = jnp.stack([lax.axis_index("gx") % 2, lax.axis_index("gy") % 2]).astype(jnp.int32)
    field = pltpu.VMEM(BLOCK, F32)
    halves = [pltpu.VMEM((CX * CY, NZ + 256), BF16)] * 2 + [pltpu.VMEM((CX * CY, NZ), F32)] * 2
    face_outs = [plain(XFACE), plain(XFACE), plain(YFACE), plain(YFACE)]

    wave_rows, born_rows, *faces = call(
        pack_kernel, "pack", (place, wave_now, born_now), [SM, HB, HB],
        [kept((ROWS, 128))] * 2 + face_outs, [field, field, pltpu.SemaphoreType.DMA((2, 4))], 10, 2,
    )
    halo = exchange(faces)
    table = z_table()
    wave_part, born_part, speed, factor = call(
        inner_first, "inner1",
        (src_cell, src_amp[:, 0], wave_rows, born_rows, table, wave_old, born_old, courant, contrast),
        [SM, SM, VM, VM, VM, HB, HB, HB, HB],
        [kept(BLOCK)] * 4, [field, field, *halves, pltpu.SemaphoreType.DMA((4,))], 14, 8,
    )

    cell = rcv_cell.T
    rows_at = ((cell >> 14) + 4) * LAYER + ((cell >> 7) & 7) * STRIP + 8 + ((cell >> 10) & 15)
    lane = lax.broadcasted_iota(jnp.int32, (256, 8, 128), 2)
    picks = jnp.where(lane == (rcv_cell & 127)[:, :, None], rcv_weight[:, :, None], 0.0).reshape(2048, 128)
    dest = rcv_dest[:, 0]
    order = jnp.arange(256, dtype=jnp.int32)
    earlier = (dest[:, None] == dest[None, :]) & (order[None, :] < order[:, None])
    slot = jnp.sum(earlier.astype(jnp.int32), axis=1)
    lane = lax.broadcasted_iota(jnp.int32, (256, 128), 1)
    slots = jnp.where((lane < 8) & (lane % 4 == slot[:, None]), 1.0, 0.0).astype(F32)

    wave_mid, born_mid, wave_mid_rows, born_mid_rows, *faces = call(
        fix_kernel, "fix1", (place, wave_part, born_part, speed, factor, *halo), [SM] + [VM] * 8,
        [kept(BLOCK)] * 2 + [kept((ROWS, 128))] * 2 + face_outs, [], 10, 3,
    )
    halo = exchange(faces)
    wave_part, born_part, first, wave_next, born_next = call(
        inner_second, "inner2",
        (
            src_cell, src_amp[:, 1], rows_at, wave_mid_rows, born_mid_rows, table, wave_rows, born_rows,
            speed, factor, picks, wave_mid, born_mid,
        ),
        [SM] * 3 + [VM] * 10,
        [kept(BLOCK)] * 2 + [plain((256, 128)), away(BLOCK), away(BLOCK)],
        [*halves, pltpu.VMEM((2048, 128), F32), pltpu.SemaphoreType.DMA((2,))], 12, 10,
    )
    wave_last, born_last, packed = call(
        last_kernel, "last",
        (place, rows_at, wave_part, born_part, speed, factor, *halo, picks, first, slots, dest[None, :]),
        [SM, SM] + [VM] * 12,
        [away(BLOCK), away(BLOCK), plain((128, 128))],
        [
            field, field, pltpu.VMEM((ROWS, 128), F32), pltpu.VMEM((2048, 128), F32),
            pltpu.VMEM((256, 128), F32), pltpu.SemaphoreType.DMA((2,)),
        ], 16, 5,
    )
    arrived = lax.all_to_all(
        packed.reshape(128, 1, 128), ("gx", "gy"), split_axis=0, concat_axis=0, tiled=True
    )
    gathers = arrived[:, 0, :8].reshape(1, 128, 2, CAP)
    return (wave_next, wave_last, born_next, born_last, gathers)


def solution(mesh):
    placed = (P("gx", "gy", None),) * 6 + (
        P(("gx", "gy")),
        P(("gx", "gy"), None),
        P(("gx", "gy"), None),
        P(("gx", "gy"), None),
        P(("gx", "gy"), None),
    )
    return jax.shard_map(
        body,
        mesh=mesh,
        in_specs=placed,
        out_specs=(P("gx", "gy", None),) * 4 + (P(("gx", "gy"), None, None, None),),
        check_vma=False,
    )
```

time: 108 us -> 112 us (1.037)
  local copies, waits for them, and re-layouts: 9 us -> 27.2 us
  Pallas kernels: 57.5 us -> 40.5 us
    unnamed x26 -> x54, local copies, waits for them, and re-layouts: 8.65 us -> 26.8 us
    pallas_call x6 -> x5, Pallas kernels: 57.5 us -> 40.5 us  [call(): pl.pallas_call(kernel, name=name, out_shape=tuple((o[1] for o in outs)),...]
  transfers between devices with their start and end apart: 8 -> 8, of which waited for: 0 -> 0; matrix products, arithmetic and copies ran while one was open for 1% -> 2% of each run, Pallas kernels for 32% -> 24%
where the time goes in v2:
time: 112 us; the launch traced here: 111 us
  Pallas kernels  40.5 us (36%)
  local copies, waits for them, and re-layouts  27.2 us (24%)
  blocking collectives  24.6 us (22%)
  starting transfers between devices  15.8 us (14%)
  other arithmetic  1.94 us (2%)
    pallas_call x5, Pallas kernels, call(): pl.pallas_call(kernel, name=name, out_shape=tuple((o[1] for o in outs)),...  40.5 us
    unnamed x54, local copies, waits for them, and re-layouts  26.8 us
    all_to_all x1, blocking collectives, body(): lax.all_to_all(packed.reshape(128, 1, 128), ('gx', 'gy'), split_axis=0, c...  24.6 us
    ppermute x2, starting transfers between devices, exchange(): ryb = lax.ppermute(yb, 'gy', pairs(16, 1))  7.48 us
    ppermute x2, starting transfers between devices, exchange(): rxa = lax.ppermute(xa, 'gx', pairs(8, 0))  4.71 us
  transfers between devices with their start and end apart: 8, of which 0 were waited for; matrix products, arithmetic and copies ran while one was open for 2% of the time, Pallas kernels for 24%

profile of v2, /device:TPU:1, one launch (start us, length us, event | category | flops | bytes accessed | tf_op | source)
XLA Modules:
  0.0 111.1 jit_solution(5534699245995045362)
XLA Ops:
  0.6 0.1 pad_add_fusion.place
  0.7 1.6 %copy-done.11 = f32[32,16,1024]{2,1,0:T(8,128)S(1)} copy-done((f32[32,16,1024]{2,1,0:T(8,128)S(1)}, f32[32,16,1024]{2,1,0:T(8,128)}, u32[]{:S(2)}) %copy-start.11) | copy-done | bytes 2097176
  2.3 1.6 %copy-done.12 = f32[32,16,1024]{2,1,0:T(8,128)S(1)} copy-done((f32[32,16,1024]{2,1,0:T(8,128)S(1)}, f32[32,16,1024]{2,1,0:T(8,128)}, u32[]{:S(2)}) %copy-start.12) | copy-done | bytes 2097176
  3.9 1.8 %pack.1 = (f32[7688,128]{1,0:T(8,128)S(1)}, f32[7688,128]{1,0:T(8,128)S(1)}, f32[8,16,1024]{2,1,0:T(8,128)S(1)}, f32[8,16,1024]{2,1,0:T(8,128)S(1)}, f32[32,8,10...) custom-call(s32[2]{0:T(128)S(1)} %pad_add_fusion.place, f32[32,16,1024]{2,1,0:T(8,128)S(1)} %copy-done.11, ...), custom_call_target="tpu_custom_call" | custom-call | bytes 6000000 | tf_op jit(solution)/shard_map/pack/pallas_call | solution.py:368
  5.8 1.5 %collective-permute-start.2 = (f32[32,8,1024]{2,1,0:T(8,128)S(1)}, f32[32,8,1024]{2,1,0:T(8,128)S(1)}, u32[]{:S(2)}, u32[]{:S(2)}) collective-permute-start(f32[32,8,1024]{2,1,0:T(8,128)S(1)} %get-tuple-element.39), channel_id=1, source_target_pairs={{0,1},{1,0},{2,3},{3,2},{4,5},{5,4},{6,7},{7,6},{8,9},{9,8},{10,11... | collective-permute-start | bytes 3145736 | tf_op jit(solution)/shard_map/ppermute | solution.py:385
  7.2 3.6 %collective-permute-start.3 = (f32[32,8,1024]{2,1,0:T(8,128)S(1)}, f32[32,8,1024]{2,1,0:T(8,128)S(1)}, u32[]{:S(2)}, u32[]{:S(2)}) collective-permute-start(f32[32,8,1024]{2,1,0:T(8,128)S(1)} %get-tuple-element.40), channel_id=1, source_target_pairs={{1,2},{2,1},{3,4},{4,3},{5,6},{6,5},{7,8},{8,7},{9,10},{10,9},{11,... | collective-permute-start | bytes 3145736 | tf_op jit(solution)/shard_map/ppermute | solution.py:382
  10.8 1.3 %collective-permute-start = (f32[8,16,1024]{2,1,0:T(8,128)S(1)}, f32[8,16,1024]{2,1,0:T(8,128)S(1)}, u32[]{:S(2)}, u32[]{:S(2)}) collective-permute-start(f32[8,16,1024]{2,1,0:T(8,128)S(1)} %get-tuple-element.37), channel_id=1, source_target_pairs={{0,16},{16,0},{32,48},{48,32},{64,80},{80,64},{96,112},{112,96},{1... | collective-permute-start | bytes 1572872 | tf_op jit(solution)/shard_map/ppermute | solution.py:384
  12.1 0.7 collective-permute-start.1
  12.8 0.9 select_convert_fusion.table
  13.8 0.0 copy-start.15
  13.8 1.6 %copy-done.15 = f32[32,16,1024]{2,1,0:T(8,128)S(1)} copy-done((f32[32,16,1024]{2,1,0:T(8,128)S(1)}, f32[32,16,1024]{2,1,0:T(8,128)}, u32[]{:S(2)}) %copy-start.15) | copy-done | bytes 2097176
  15.4 1.6 %copy-done.16 = f32[32,16,1024]{2,1,0:T(8,128)S(1)} copy-done((f32[32,16,1024]{2,1,0:T(8,128)S(1)}, f32[32,16,1024]{2,1,0:T(8,128)}, u32[]{:S(2)}) %copy-start.16) | copy-done | bytes 2097176
  17.0 12.5 %inner1.1 = (f32[32,16,1024]{2,1,0:T(8,128)S(1)}, f32[32,16,1024]{2,1,0:T(8,128)S(1)}, f32[32,16,1024]{2,1,0:T(8,128)S(1)}, f32[32,16,1024]{2,1,0:T(8,128)S(1)}) custom-call(s32[4]{0:T(128)S(1)} %copy-done.22, f32[4]{0:T(128)S(1)} %get-tuple-element.64.amps, f32[7688,128]{1,0:T(8,128)S(1)} %get-tuple-element.31.wave.wave_old, ...), custom_call_target="tpu_custom_call" | custom-call | bytes 24000000 | tf_op jit(solution)/shard_map/inner1/pallas_call | solution.py:368
  29.5 0.0 copy-start
  29.6 0.0 collective-permute-done.1.rxb
  29.6 0.0 copy-start.21
  29.6 0.0 copy-start.23
  29.6 0.0 copy-start.24
  29.6 4.7 %fix1.1 = (f32[32,16,1024]{2,1,0:T(8,128)S(1)}, f32[32,16,1024]{2,1,0:T(8,128)S(1)}, f32[7688,128]{1,0:T(8,128)S(1)}, f32[7688,128]{1,0:T(8,128)S(1)}, f32[8,16,...) custom-call(s32[2]{0:T(128)S(1)} %pad_add_fusion.place, ...), custom_call_target="tpu_custom_call" | custom-call | bytes 9000000 | tf_op jit(solution)/shard_map/fix1/pallas_call | solution.py:368
  34.3 1.9 %copy-done.7 = f32[7688,128]{1,0:T(8,128)} copy-done((f32[7688,128]{1,0:T(8,128)}, f32[7688,128]{1,0:T(8,128)S(1)}, u32[]{:S(2)}) %copy-start.7) | copy-done | bytes 3936280
  36.2 1.9 %copy-done.9 = f32[7688,128]{1,0:T(8,128)} copy-done((f32[7688,128]{1,0:T(8,128)}, f32[7688,128]{1,0:T(8,128)S(1)}, u32[]{:S(2)}) %copy-start.9) | copy-done | bytes 3936280
  38.1 1.3 %copy-done.17 = f32[32,16,1024]{2,1,0:T(8,128)} copy-done((f32[32,16,1024]{2,1,0:T(8,128)}, f32[32,16,1024]{2,1,0:T(8,128)S(1)}, u32[]{:S(2)}) %copy-start.17) | copy-done | bytes 2097176
  39.5 1.3 %copy-done.19 = f32[32,16,1024]{2,1,0:T(8,128)} copy-done((f32[32,16,1024]{2,1,0:T(8,128)}, f32[32,16,1024]{2,1,0:T(8,128)S(1)}, u32[]{:S(2)}) %copy-start.19) | copy-done | bytes 2097176
  40.8 3.9 %collective-permute-start.7 = (f32[32,8,1024]{2,1,0:T(8,128)}, f32[32,8,1024]{2,1,0:T(8,128)}, u32[]{:S(2)}, u32[]{:S(2)}) collective-permute-start(f32[32,8,1024]{2,1,0:T(8,128)} %get-tuple-element.51), channel_id=1, source_target_pairs={{1,2},{2,1},{3,4},{4,3},{5,6},{6,5},{7,8},{8,7},{9,10},{10,9},{11,... | collective-permute-start | bytes 3145736 | tf_op jit(solution)/shard_map/ppermute | solution.py:382
  44.7 0.2 convert_reduce_fusion
  44.9 0.1 fusion.7.slots
  45.0 3.4 %collective-permute-start.4 = (f32[8,16,1024]{2,1,0:T(8,128)}, f32[8,16,1024]{2,1,0:T(8,128)S(1)}, u32[]{:S(2)}, u32[]{:S(2)}) collective-permute-start(f32[8,16,1024]{2,1,0:T(8,128)} %get-tuple-element.48), channel_id=1, source_target_pairs={{0,16},{16,0},{32,48},{48,32},{64,80},{80,64},{96,112},{112,96},{1... | collective-permute-start | bytes 1572872 | tf_op jit(solution)/shard_map/ppermute | solution.py:384
  48.5 1.5 %collective-permute-start.5 = (f32[8,16,1024]{2,1,0:T(8,128)}, f32[8,16,1024]{2,1,0:T(8,128)}, u32[]{:S(2)}, u32[]{:S(2)}) collective-permute-start(f32[8,16,1024]{2,1,0:T(8,128)} %get-tuple-element.49), channel_id=1, source_target_pairs={{16,32},{32,16},{48,64},{64,48},{80,96},{96,80},{17,33},{33,17},{4... | collective-permute-start | bytes 1572872 | tf_op jit(solution)/shard_map/ppermute | solution.py:383
  49.9 0.1 copy.24
  50.1 0.1 eq.81
  50.2 0.1 copy.25
  50.3 0.1 broadcast_in_dim.48
  50.4 0.6 fusion.4.picks
  51.0 0.0 copy-start.1
  51.1 1.6 %copy-done.1 = f32[32,16,1024]{2,1,0:T(8,128)S(1)} copy-done((f32[32,16,1024]{2,1,0:T(8,128)S(1)}, f32[32,16,1024]{2,1,0:T(8,128)}, u32[]{:S(2)}) %copy-start.1) | copy-done | bytes 2097176
  52.6 2.1 %copy-done.4 = f32[7688,128]{1,0:T(8,128)S(1)} copy-done((f32[7688,128]{1,0:T(8,128)S(1)}, f32[7688,128]{1,0:T(8,128)}, u32[]{:S(2)}) %copy-start.4) | copy-done | bytes 3936280
  54.8 2.1 %copy-done.6 = f32[7688,128]{1,0:T(8,128)S(1)} copy-done((f32[7688,128]{1,0:T(8,128)S(1)}, f32[7688,128]{1,0:T(8,128)}, u32[]{:S(2)}) %copy-start.6) | copy-done | bytes 3936280
  56.9 2.1 %copy-done.8 = f32[7688,128]{1,0:T(8,128)S(1)} copy-done((f32[7688,128]{1,0:T(8,128)S(1)}, f32[7688,128]{1,0:T(8,128)}, u32[]{:S(2)}) %copy-start.8) | copy-done | bytes 3936280
  59.0 2.1 %copy-done.10 = f32[7688,128]{1,0:T(8,128)S(1)} copy-done((f32[7688,128]{1,0:T(8,128)S(1)}, f32[7688,128]{1,0:T(8,128)}, u32[]{:S(2)}) %copy-start.10) | copy-done | bytes 3936280
  61.1 1.6 %copy-done.18 = f32[32,16,1024]{2,1,0:T(8,128)S(1)} copy-done((f32[32,16,1024]{2,1,0:T(8,128)S(1)}, f32[32,16,1024]{2,1,0:T(8,128)}, u32[]{:S(2)}) %copy-start.18) | copy-done | bytes 2097176
  62.7 1.6 %copy-done.20 = f32[32,16,1024]{2,1,0:T(8,128)S(1)} copy-done((f32[32,16,1024]{2,1,0:T(8,128)S(1)}, f32[32,16,1024]{2,1,0:T(8,128)}, u32[]{:S(2)}) %copy-start.20) | copy-done | bytes 2097176
  64.3 14.5 %inner2.1 = (f32[32,16,1024]{2,1,0:T(8,128)S(1)}, f32[32,16,1024]{2,1,0:T(8,128)S(1)}, f32[256,128]{1,0:T(8,128)S(1)}, f32[32,16,1024]{2,1,0:T(8,128)}, f32[32,16,1024]{2,1,0:T(8,128)}) custom-call(s32[4]{0:T(128)S(1)} %copy-done.22, f32[4]{0:T(128)S(1)} %get-tuple-element.65.amps, s32[8,256]{1,0:T(8,128)S(1)} %get-tuple-element.63.rows_at, ...), custom_call_target="tpu_custom_call" | custom-call | bytes 30000000 | tf_op jit(solution)/shard_map/inner2/pallas_call | solution.py:368
  78.8 0.0 collective-permute-done.4.rxa
  78.8 0.0 collective-permute-done.5.rxb
  78.8 0.0 collective-permute-done.7.ryb
  78.9 7.0 %last.1 = (f32[32,16,1024]{2,1,0:T(8,128)}, f32[32,16,1024]{2,1,0:T(8,128)}, f32[128,128]{1,0:T(8,128)S(1)}) custom-call(s32[2]{0:T(128)S(1)} %pad_add_fusion.place, s32[8,256]{1,0:T(8,128)S(1)} %get-tuple-element.63.rows_at, f32[32,16,1024]{2,1,0:T(8,128)S(1)} %get-tuple-element.46.wave_part, f32[32,16,1024]{2,1,0:T(8,128)S(1)} %get-tuple-element.47.born_part, ...), custom_call_target="tpu_custom_call" | custom-call | bytes 15000000 | tf_op jit(solution)/shard_map/last/pallas_call | solution.py:368
  85.9 24.6 %all_to_all.5 = f32[128,1,128]{2,1,0:T(1,128)S(1)} all-to-all(f32[128,1,128]{2,1,0:T(1,128)S(1)} %bitcast.15), channel_id=1, replica_groups=mesh['gx'=8,'gy'=16] {'gx','gy'}, dimensions={0} | all-to-all | bytes 131072 | tf_op jit(solution)/shard_map/all_to_all | solution.py:466
  110.4 0.7 copy.28
  (42 shorter events, 0.1 us)
Async XLA Ops:
  0.7 1.6 %copy-start.11 = (f32[32,16,1024]{2,1,0:T(8,128)S(1)}, f32[32,16,1024]{2,1,0:T(8,128)}, u32[]{:S(2)}) copy-start(f32[32,16,1024]{2,1,0:T(8,128)} %wave_in.1) | copy-start | bytes 6291460
  2.3 1.6 %copy-start.12 = (f32[32,16,1024]{2,1,0:T(8,128)S(1)}, f32[32,16,1024]{2,1,0:T(8,128)}, u32[]{:S(2)}) copy-start(f32[32,16,1024]{2,1,0:T(8,128)} %born_in.1) | copy-start | bytes 6291460
  3.9 8.9 %copy-start.25 = (f32[4,2]{0,1:T(2,128)S(1)}, f32[4,2]{0,1:T(2,128)}, u32[]{:S(2)}) copy-start(f32[4,2]{0,1:T(2,128)} %param.18) | copy-start | bytes 100
  3.9 9.8 %copy-start.13 = (f32[32,16,1024]{2,1,0:T(8,128)S(1)}, f32[32,16,1024]{2,1,0:T(8,128)}, u32[]{:S(2)}) copy-start(f32[32,16,1024]{2,1,0:T(8,128)} %wave_old_in.1) | copy-start | bytes 6291460
  3.9 9.9 %copy-start.14 = (f32[32,16,1024]{2,1,0:T(8,128)S(1)}, f32[32,16,1024]{2,1,0:T(8,128)}, u32[]{:S(2)}) copy-start(f32[32,16,1024]{2,1,0:T(8,128)} %born_old_in.1) | copy-start | bytes 6291460
  3.9 9.9 %copy-start.22 = (s32[4]{0:T(128)S(1)}, s32[4]{0:T(128)}, u32[]{:S(2)}) copy-start(s32[4]{0:T(128)} %cells.3) | copy-start | bytes 52
  5.7 23.8 %copy-start.3 = (f32[7688,128]{1,0:T(8,128)}, f32[7688,128]{1,0:T(8,128)S(1)}, u32[]{:S(2)}) copy-start(f32[7688,128]{1,0:T(8,128)S(1)} %get-tuple-element.31.wave.wave_old) | copy-start | bytes 11808772
  5.7 23.8 %copy-start.5 = (f32[7688,128]{1,0:T(8,128)}, f32[7688,128]{1,0:T(8,128)S(1)}, u32[]{:S(2)}) copy-start(f32[7688,128]{1,0:T(8,128)S(1)} %get-tuple-element.32.born.born_old) | copy-start | bytes 11808772
  5.8 23.8 %collective-permute-start.2 = (f32[32,8,1024]{2,1,0:T(8,128)S(1)}, f32[32,8,1024]{2,1,0:T(8,128)S(1)}, u32[]{:S(2)}, u32[]{:S(2)}) collective-permute-start(f32[32,8,1024]{2,1,0:T(8,128)S(1)} %get-tuple-element.39), channel_id=1, source_target_pairs={{0,1},{1,0},{2,3},{3,2},{4,5},{5,4},{6,7},{7,6},{8,9},{9,8},{10,11... | collective-permute-start | bytes 3145736 | tf_op jit(solution)/shard_map/ppermute | solution.py:385
  7.2 22.4 %collective-permute-start.3 = (f32[32,8,1024]{2,1,0:T(8,128)S(1)}, f32[32,8,1024]{2,1,0:T(8,128)S(1)}, u32[]{:S(2)}, u32[]{:S(2)}) collective-permute-start(f32[32,8,1024]{2,1,0:T(8,128)S(1)} %get-tuple-element.40), channel_id=1, source_target_pairs={{1,2},{2,1},{3,4},{4,3},{5,6},{6,5},{7,8},{8,7},{9,10},{10,9},{11,... | collective-permute-start | bytes 3145736 | tf_op jit(solution)/shard_map/ppermute | solution.py:382
  10.8 18.8 %collective-permute-start = (f32[8,16,1024]{2,1,0:T(8,128)S(1)}, f32[8,16,1024]{2,1,0:T(8,128)S(1)}, u32[]{:S(2)}, u32[]{:S(2)}) collective-permute-start(f32[8,16,1024]{2,1,0:T(8,128)S(1)} %get-tuple-element.37), channel_id=1, source_target_pairs={{0,16},{16,0},{32,48},{48,32},{64,80},{80,64},{96,112},{112,96},{1... | collective-permute-start | bytes 1572872 | tf_op jit(solution)/shard_map/ppermute | solution.py:384
  12.1 17.5 %collective-permute-start.1 = (f32[8,16,1024]{2,1,0:T(8,128)S(1)}, f32[8,16,1024]{2,1,0:T(8,128)S(1)}, u32[]{:S(2)}, u32[]{:S(2)}) collective-permute-start(f32[8,16,1024]{2,1,0:T(8,128)S(1)} %get-tuple-element.38), channel_id=1, source_target_pairs={{16,32},{32,16},{48,64},{64,48},{80,96},{96,80},{17,33},{33,17},{4... | collective-permute-start | bytes 1572872 | tf_op jit(solution)/shard_map/ppermute | solution.py:383
  13.8 1.6 %copy-start.15 = (f32[32,16,1024]{2,1,0:T(8,128)S(1)}, f32[32,16,1024]{2,1,0:T(8,128)}, u32[]{:S(2)}) copy-start(f32[32,16,1024]{2,1,0:T(8,128)} %courant_in.1) | copy-start | bytes 6291460
  15.4 1.6 %copy-start.16 = (f32[32,16,1024]{2,1,0:T(8,128)S(1)}, f32[32,16,1024]{2,1,0:T(8,128)}, u32[]{:S(2)}) copy-start(f32[32,16,1024]{2,1,0:T(8,128)} %contrast_in.1) | copy-start | bytes 6291460
  29.5 4.8 %copy-start = (f32[32,16,1024]{2,1,0:T(8,128)}, f32[32,16,1024]{2,1,0:T(8,128)S(1)}, u32[]{:S(2)}) copy-start(f32[32,16,1024]{2,1,0:T(8,128)S(1)} %get-tuple-element.36.contrast) | copy-start | bytes 6291460
  29.6 15.1 %copy-start.21 = (s32[256,1]{0,1:T(1,128)S(1)}, s32[256,1]{0,1:T(1,128)}, u32[]{:S(2)}) copy-start(s32[256,1]{0,1:T(1,128)} %param.21) | copy-start | bytes 3076
  29.6 20.3 %copy-start.23 = (s32[256,8]{0,1:T(8,128)S(1)}, s32[256,8]{0,1:T(8,128)}, u32[]{:S(2)}) copy-start(s32[256,8]{0,1:T(8,128)} %param.19) | copy-start | bytes 24580
  29.6 20.6 %copy-start.24 = (f32[256,8]{0,1:T(8,128)S(1)}, f32[256,8]{0,1:T(8,128)}, u32[]{:S(2)}) copy-start(f32[256,8]{0,1:T(8,128)} %param.20) | copy-start | bytes 24580
  34.3 1.9 %copy-start.7 = (f32[7688,128]{1,0:T(8,128)}, f32[7688,128]{1,0:T(8,128)S(1)}, u32[]{:S(2)}) copy-start(f32[7688,128]{1,0:T(8,128)S(1)} %get-tuple-element.41.wave) | copy-start | bytes 11808772
  36.2 1.9 %copy-start.9 = (f32[7688,128]{1,0:T(8,128)}, f32[7688,128]{1,0:T(8,128)S(1)}, u32[]{:S(2)}) copy-start(f32[7688,128]{1,0:T(8,128)S(1)} %get-tuple-element.42.born) | copy-start | bytes 11808772
  38.1 1.3 %copy-start.17 = (f32[32,16,1024]{2,1,0:T(8,128)}, f32[32,16,1024]{2,1,0:T(8,128)S(1)}, u32[]{:S(2)}) copy-start(f32[32,16,1024]{2,1,0:T(8,128)S(1)} %get-tuple-element.43.wave_now) | copy-start | bytes 6291460
  39.5 1.3 %copy-start.19 = (f32[32,16,1024]{2,1,0:T(8,128)}, f32[32,16,1024]{2,1,0:T(8,128)S(1)}, u32[]{:S(2)}) copy-start(f32[32,16,1024]{2,1,0:T(8,128)S(1)} %get-tuple-element.44.born_now) | copy-start | bytes 6291460
  40.8 38.1 %collective-permute-start.6 = (f32[32,8,1024]{2,1,0:T(8,128)}, f32[32,8,1024]{2,1,0:T(8,128)}, u32[]{:S(2)}, u32[]{:S(2)}) collective-permute-start(f32[32,8,1024]{2,1,0:T(8,128)} %get-tuple-element.50), channel_id=1, source_target_pairs={{0,1},{1,0},{2,3},{3,2},{4,5},{5,4},{6,7},{7,6},{8,9},{9,8},{10,11... | collective-permute-start | bytes 3145736 | tf_op jit(solution)/shard_map/ppermute | solution.py:385
  40.8 38.1 %collective-permute-start.7 = (f32[32,8,1024]{2,1,0:T(8,128)}, f32[32,8,1024]{2,1,0:T(8,128)}, u32[]{:S(2)}, u32[]{:S(2)}) collective-permute-start(f32[32,8,1024]{2,1,0:T(8,128)} %get-tuple-element.51), channel_id=1, source_target_pairs={{1,2},{2,1},{3,4},{4,3},{5,6},{6,5},{7,8},{8,7},{9,10},{10,9},{11,... | collective-permute-start | bytes 3145736 | tf_op jit(solution)/shard_map/ppermute | solution.py:382
  45.0 33.8 %collective-permute-start.4 = (f32[8,16,1024]{2,1,0:T(8,128)}, f32[8,16,1024]{2,1,0:T(8,128)S(1)}, u32[]{:S(2)}, u32[]{:S(2)}) collective-permute-start(f32[8,16,1024]{2,1,0:T(8,128)} %get-tuple-element.48), channel_id=1, source_target_pairs={{0,16},{16,0},{32,48},{48,32},{64,80},{80,64},{96,112},{112,96},{1... | collective-permute-start | bytes 1572872 | tf_op jit(solution)/shard_map/ppermute | solution.py:384
  48.5 30.4 %collective-permute-start.5 = (f32[8,16,1024]{2,1,0:T(8,128)}, f32[8,16,1024]{2,1,0:T(8,128)}, u32[]{:S(2)}, u32[]{:S(2)}) collective-permute-start(f32[8,16,1024]{2,1,0:T(8,128)} %get-tuple-element.49), channel_id=1, source_target_pairs={{16,32},{32,16},{48,64},{64,48},{80,96},{96,80},{17,33},{33,17},{4... | collective-permute-start | bytes 1572872 | tf_op jit(solution)/shard_map/ppermute | solution.py:383
  51.0 1.6 %copy-start.1 = (f32[32,16,1024]{2,1,0:T(8,128)S(1)}, f32[32,16,1024]{2,1,0:T(8,128)}, u32[]{:S(2)}) copy-start(f32[32,16,1024]{2,1,0:T(8,128)} %copy-done) | copy-start | bytes 6291460
  52.6 2.1 %copy-start.4 = (f32[7688,128]{1,0:T(8,128)S(1)}, f32[7688,128]{1,0:T(8,128)}, u32[]{:S(2)}) copy-start(f32[7688,128]{1,0:T(8,128)} %copy-done.3) | copy-start | bytes 11808772
  54.8 2.1 %copy-start.6 = (f32[7688,128]{1,0:T(8,128)S(1)}, f32[7688,128]{1,0:T(8,128)}, u32[]{:S(2)}) copy-start(f32[7688,128]{1,0:T(8,128)} %copy-done.5) | copy-start | bytes 11808772
  56.9 2.1 %copy-start.8 = (f32[7688,128]{1,0:T(8,128)S(1)}, f32[7688,128]{1,0:T(8,128)}, u32[]{:S(2)}) copy-start(f32[7688,128]{1,0:T(8,128)} %copy-done.7) | copy-start | bytes 11808772
  59.0 2.1 %copy-start.10 = (f32[7688,128]{1,0:T(8,128)S(1)}, f32[7688,128]{1,0:T(8,128)}, u32[]{:S(2)}) copy-start(f32[7688,128]{1,0:T(8,128)} %copy-done.9) | copy-start | bytes 11808772
  61.1 1.6 %copy-start.18 = (f32[32,16,1024]{2,1,0:T(8,128)S(1)}, f32[32,16,1024]{2,1,0:T(8,128)}, u32[]{:S(2)}) copy-start(f32[32,16,1024]{2,1,0:T(8,128)} %copy-done.17) | copy-start | bytes 6291460
  62.7 1.6 %copy-start.20 = (f32[32,16,1024]{2,1,0:T(8,128)S(1)}, f32[32,16,1024]{2,1,0:T(8,128)}, u32[]{:S(2)}) copy-start(f32[32,16,1024]{2,1,0:T(8,128)} %copy-done.19) | copy-start | bytes 6291460
  64.3 14.6 %copy-start.2 = (f32[32,16,1024]{2,1,0:T(8,128)S(1)}, f32[32,16,1024]{2,1,0:T(8,128)}, u32[]{:S(2)}) copy-start(f32[32,16,1024]{2,1,0:T(8,128)} %copy-done) | copy-start | bytes 6291460

commit v3 on v2

--- a/solution.py
+++ b/solution.py
@@ -162,9 +162,25 @@
         born_part[at] = born_part[at] + contrast[at] * added
 
 
+def make_picks(taps, weights, picks):
+    lane = lax.broadcasted_iota(jnp.int32, (8, 128), 1)
+    for half in range(2):
+        spots = lax.bitwise_and(taps[:, half * 128 : half * 128 + 128], 127)
+        gains = weights[:, half * 128 : half * 128 + 128]
+
+        def group(g, carry):
+            spots, gains = carry
+            for j in range(16):
+                row = pl.multiple_of((half * 128 + g * 16 + j) * 8, 8)
+                picks[pl.ds(row, 8), :] = jnp.where(lane == spots[:, j : j + 1], gains[:, j : j + 1], 0.0)
+            return pltpu.roll(spots, 112, 1), pltpu.roll(gains, 112, 1)
+
+        lax.fori_loop(0, 8, group, (spots, gains))
+
+
 def inner_first(
-    cells, amps, wave, born, table, wave_old_in, born_old_in, courant_in, contrast_in,
-    wave_part, born_part, courant, contrast, wave_old, born_old, high, low, wave_z, born_z, sems,
+    cells, amps, wave, born, table, taps, weights, wave_old_in, born_old_in, courant_in, contrast_in,
+    wave_part, born_part, courant, contrast, picks, wave_old, born_old, high, low, wave_z, born_z, sems,
 ):
     copies = [
         pltpu.make_async_copy(a, b, sems.at[i])
@@ -176,6 +192,7 @@
         copy.start()
     along_z(wave, high, low, table, wave_z)
     along_z(born, high, low, table, born_z)
+    make_picks(taps, weights, picks)
     for copy in copies:
         copy.wait()
 
@@ -364,6 +381,10 @@
     return HB, jax.ShapeDtypeStruct(shape, F32)
 
 
+def still(value):
+    return pltpu.with_memory_space_constraint(value, pltpu.HBM)
+
+
 def call(kernel, name, args, specs, outs, scratch, mib, us):
     return pl.pallas_call(
         kernel,
@@ -415,22 +436,23 @@
     face_outs = [plain(XFACE), plain(XFACE), plain(YFACE), plain(YFACE)]
 
     wave_rows, born_rows, *faces = call(
-        pack_kernel, "pack", (place, wave_now, born_now), [SM, HB, HB],
+        pack_kernel, "pack", (place, still(wave_now), still(born_now)), [SM, HB, HB],
         [kept((ROWS, 128))] * 2 + face_outs, [field, field, pltpu.SemaphoreType.DMA((2, 4))], 10, 2,
     )
     halo = exchange(faces)
     table = z_table()
-    wave_part, born_part, speed, factor = call(
+    wave_part, born_part, speed, factor, picks = call(
         inner_first, "inner1",
-        (src_cell, src_amp[:, 0], wave_rows, born_rows, table, wave_old, born_old, courant, contrast),
-        [SM, SM, VM, VM, VM, HB, HB, HB, HB],
-        [kept(BLOCK)] * 4, [field, field, *halves, pltpu.SemaphoreType.DMA((4,))], 14, 8,
+        (
+            src_cell, src_amp[:, 0], wave_rows, born_rows, table, rcv_cell.T, rcv_weight.T,
+            still(wave_old), still(born_old), still(courant), still(contrast),
+        ),
+        [SM, SM] + [VM] * 5 + [HB] * 4,
+        [kept(BLOCK)] * 4 + [kept((2048, 128))], [field, field, *halves, pltpu.SemaphoreType.DMA((4,))], 14, 8,
     )
 
     cell = rcv_cell.T
     rows_at = ((cell >> 14) + 4) * LAYER + ((cell >> 7) & 7) * STRIP + 8 + ((cell >> 10) & 15)
-    lane = lax.broadcasted_iota(jnp.int32, (256, 8, 128), 2)
-    picks = jnp.where(lane == (rcv_cell & 127)[:, :, None], rcv_weight[:, :, None], 0.0).reshape(2048, 128)
     dest = rcv_dest[:, 0]
     order = jnp.arange(256, dtype=jnp.int32)
     earlier = (dest[:, None] == dest[None, :]) & (order[None, :] < order[:, None])

time: 112 us -> 91.9 us (0.82)
  local copies, waits for them, and re-layouts: 27.2 us -> 0.69 us
  blocking collectives: 24.6 us -> 33 us
    unnamed x54 -> x11, local copies, waits for them, and re-layouts: 26.8 us -> 0.68 us
    all_to_all x1, blocking collectives: 24.6 us -> 33 us  [body(): lax.all_to_all(packed.reshape(128, 1, 128), ('gx', 'gy'), split_axis=0, c...]
  transfers between devices with their start and end apart: 8 -> 8, of which waited for: 0 -> 0; matrix products, arithmetic and copies ran while one was open for 2% -> 1% of each run, Pallas kernels for 24% -> 31%
where the time goes in v3:
time: 91.9 us; the launch traced here: 91.7 us
  Pallas kernels  40.7 us (44%)
  blocking collectives  33 us (36%)
  starting transfers between devices  15.1 us (16%)
  other arithmetic  1.32 us (1%)
    pallas_call x5, Pallas kernels, call(): pl.pallas_call(kernel, name=name, out_shape=tuple((o[1] for o in outs)),...  40.7 us
    all_to_all x1, blocking collectives, body(): lax.all_to_all(packed.reshape(128, 1, 128), ('gx', 'gy'), split_axis=0, c...  33 us
    ppermute x2, starting transfers between devices, exchange(): ryb = lax.ppermute(yb, 'gy', pairs(16, 1))  7.47 us
    ppermute x2, starting transfers between devices, exchange(): rxa = lax.ppermute(xa, 'gx', pairs(8, 0))  4.72 us
  transfers between devices with their start and end apart: 8, of which 0 were waited for; matrix products, arithmetic and copies ran while one was open for 1% of the time, Pallas kernels for 31%

profile of v3, /device:TPU:1, one launch (start us, length us, event | category | flops | bytes accessed | tf_op | source)
XLA Modules:
  0.0 91.7 jit_solution(15300244294138889782)
XLA Ops:
  0.6 0.1 pad_add_fusion.place
  0.7 0.0 copy-start.4
  0.7 0.0 copy-start
  0.7 0.0 copy-start.2
  0.7 0.0 copy-start.3
  0.7 3.0 %pack.1 = (f32[7688,128]{1,0:T(8,128)S(1)}, f32[7688,128]{1,0:T(8,128)S(1)}, f32[8,16,1024]{2,1,0:T(8,128)S(1)}, f32[8,16,1024]{2,1,0:T(8,128)S(1)}, f32[32,8,10...) custom-call(s32[2]{0:T(128)S(1)} %pad_add_fusion.place, f32[32,16,1024]{2,1,0:T(8,128)} %wave_in.1, f32[32,16,1024]{2,1,0:T(8,128)} %born_in.1), custom_call_target="tpu_custom_call" | custom-call | bytes 6000000 | tf_op jit(solution)/shard_map/pack/pallas_call | solution.py:389
  3.7 1.5 %collective-permute-start.2 = (f32[32,8,1024]{2,1,0:T(8,128)S(1)}, f32[32,8,1024]{2,1,0:T(8,128)S(1)}, u32[]{:S(2)}, u32[]{:S(2)}) collective-permute-start(f32[32,8,1024]{2,1,0:T(8,128)S(1)} %get-tuple-element.40), channel_id=1, source_target_pairs={{0,1},{1,0},{2,3},{3,2},{4,5},{5,4},{6,7},{7,6},{8,9},{9,8},{10,11... | collective-permute-start | bytes 3145736 | tf_op jit(solution)/shard_map/ppermute | solution.py:406
  5.2 3.6 %collective-permute-start.3 = (f32[32,8,1024]{2,1,0:T(8,128)S(1)}, f32[32,8,1024]{2,1,0:T(8,128)S(1)}, u32[]{:S(2)}, u32[]{:S(2)}) collective-permute-start(f32[32,8,1024]{2,1,0:T(8,128)S(1)} %get-tuple-element.41), channel_id=1, source_target_pairs={{1,2},{2,1},{3,4},{4,3},{5,6},{6,5},{7,8},{8,7},{9,10},{10,9},{11,... | collective-permute-start | bytes 3145736 | tf_op jit(solution)/shard_map/ppermute | solution.py:403
  8.7 1.3 %collective-permute-start = (f32[8,16,1024]{2,1,0:T(8,128)S(1)}, f32[8,16,1024]{2,1,0:T(8,128)S(1)}, u32[]{:S(2)}, u32[]{:S(2)}) collective-permute-start(f32[8,16,1024]{2,1,0:T(8,128)S(1)} %get-tuple-element.38), channel_id=1, source_target_pairs={{0,16},{16,0},{32,48},{48,32},{64,80},{80,64},{96,112},{112,96},{1... | collective-permute-start | bytes 1572872 | tf_op jit(solution)/shard_map/ppermute | solution.py:405
  10.0 0.7 collective-permute-start.1
  10.7 0.0 copy-done.4
  10.7 0.9 %select_convert_fusion.table = bf16[1024,256]{1,0:T(8,128)(2,1)S(1)} fusion(s32[1024]{0:T(1024)S(1)} %get-tuple-element.66, s32[1024]{0:T(1024)S(1)} %get-tuple-element.67, pred[1024]{0:T(1024)(128)(4,1)S(1)} %fusion.10), kind=kLoop, calls=%fused_computation | loop fusion | flops 3407872 | bytes 533504 | tf_op jit(solution)/shard_map/convert_element_type | solution.py:417
  11.7 0.0 copy-done
  11.7 0.0 copy-done.2
  11.7 0.0 copy-done.3
  11.7 13.8 %inner1.1 = (f32[32,16,1024]{2,1,0:T(8,128)S(1)}, f32[32,16,1024]{2,1,0:T(8,128)S(1)}, f32[32,16,1024]{2,1,0:T(8,128)S(1)}, f32[32,16,1024]{2,1,0:T(8,128)S(1)}, f32[2048,128]{1,0:T(8,128)S(1)}) custom-call(s32[4]{0:T(128)S(1)} %copy-done.3, f32[4]{0:T(128)S(1)} %get-tuple-element.64.amps, f32[7688,128]{1,0:T(8,128)S(1)} %get-tuple-element.32.wave.wave_old, ...), custom_call_target="tpu_custom_call" | custom-call | bytes 24000000 | tf_op jit(solution)/shard_map/inner1/pallas_call | solution.py:389
  25.5 0.0 collective-permute-done.rxa
  25.5 0.0 collective-permute-done.1.rxb
  25.6 0.0 collective-permute-done.2.rya
  25.6 0.0 collective-permute-done.3.ryb
  25.6 0.0 copy-start.1
  25.6 3.0 %fix1.1 = (f32[32,16,1024]{2,1,0:T(8,128)S(1)}, f32[32,16,1024]{2,1,0:T(8,128)S(1)}, f32[7688,128]{1,0:T(8,128)S(1)}, f32[7688,128]{1,0:T(8,128)S(1)}, f32[8,16,...) custom-call(s32[2]{0:T(128)S(1)} %pad_add_fusion.place, ...), custom_call_target="tpu_custom_call" | custom-call | bytes 9000000 | tf_op jit(solution)/shard_map/fix1/pallas_call | solution.py:389
  28.6 0.1 collective-permute-start.6
  28.7 3.9 %collective-permute-start.7 = (f32[32,8,1024]{2,1,0:T(8,128)S(1)}, f32[32,8,1024]{2,1,0:T(8,128)S(1)}, u32[]{:S(2)}, u32[]{:S(2)}) collective-permute-start(f32[32,8,1024]{2,1,0:T(8,128)S(1)} %get-tuple-element.53), channel_id=1, source_target_pairs={{1,2},{2,1},{3,4},{4,3},{5,6},{6,5},{7,8},{8,7},{9,10},{10,9},{11,... | collective-permute-start | bytes 3145736 | tf_op jit(solution)/shard_map/ppermute | solution.py:403
  32.6 0.0 copy-done.1
  32.6 0.2 convert_reduce_fusion
  32.8 3.4 %collective-permute-start.4 = (f32[8,16,1024]{2,1,0:T(8,128)S(1)}, f32[8,16,1024]{2,1,0:T(8,128)S(1)}, u32[]{:S(2)}, u32[]{:S(2)}) collective-permute-start(f32[8,16,1024]{2,1,0:T(8,128)S(1)} %get-tuple-element.50), channel_id=1, source_target_pairs={{0,16},{16,0},{32,48},{48,32},{64,80},{80,64},{96,112},{112,96},{1... | collective-permute-start | bytes 1572872 | tf_op jit(solution)/shard_map/ppermute | solution.py:405
  36.3 0.7 collective-permute-start.5
  37.0 0.1 fusion.6.slots
  37.1 14.9 %inner2.1 = (f32[32,16,1024]{2,1,0:T(8,128)S(1)}, f32[32,16,1024]{2,1,0:T(8,128)S(1)}, f32[256,128]{1,0:T(8,128)S(1)}, f32[32,16,1024]{2,1,0:T(8,128)}, f32[32,16,1024]{2,1,0:T(8,128)}) custom-call(s32[4]{0:T(128)S(1)} %copy-done.3, f32[4]{0:T(128)S(1)} %get-tuple-element.65.amps, s32[8,256]{1,0:T(8,128)S(1)} %and_add_fusion.rows_at, ...), custom_call_target="tpu_custom_call" | custom-call | bytes 30000000 | tf_op jit(solution)/shard_map/inner2/pallas_call | solution.py:389
  52.0 0.0 collective-permute-done.4.rxa
  52.0 0.0 collective-permute-done.5.rxb
  52.0 0.0 collective-permute-done.6.rya
  52.0 0.0 collective-permute-done.7.ryb
  52.0 6.1 %last.1 = (f32[32,16,1024]{2,1,0:T(8,128)}, f32[32,16,1024]{2,1,0:T(8,128)}, f32[128,128]{1,0:T(8,128)S(1)}) custom-call(s32[2]{0:T(128)S(1)} %pad_add_fusion.place, s32[8,256]{1,0:T(8,128)S(1)} %and_add_fusion.rows_at, f32[32,16,1024]{2,1,0:T(8,128)S(1)} %get-tuple-element.48.wave_part, f32[32,16,1024]{2,1,0:T(8,128)S(1)} %get-tuple-element.49.born_part, ...), custom_call_target="tpu_custom_call" | custom-call | bytes 15000000 | tf_op jit(solution)/shard_map/last/pallas_call | solution.py:389
  58.1 33.0 %all_to_all.5 = f32[128,1,128]{2,1,0:T(1,128)S(1)} all-to-all(f32[128,1,128]{2,1,0:T(1,128)S(1)} %bitcast.16), channel_id=1, replica_groups=mesh['gx'=8,'gy'=16] {'gx','gy'}, dimensions={0} | all-to-all | bytes 131072 | tf_op jit(solution)/shard_map/all_to_all | solution.py:488
  91.0 0.7 copy.22
  (6 shorter events, 0.0 us)
Async XLA Ops:
  0.7 10.0 %copy-start.4 = (f32[4,2]{0,1:T(2,128)S(1)}, f32[4,2]{0,1:T(2,128)}, u32[]{:S(2)}) copy-start(f32[4,2]{0,1:T(2,128)} %param.18) | copy-start | bytes 100
  0.7 11.0 %copy-start = (s32[256,8]{0,1:T(8,128)S(1)}, s32[256,8]{0,1:T(8,128)}, u32[]{:S(2)}) copy-start(s32[256,8]{0,1:T(8,128)} %param.19) | copy-start | bytes 24580
  0.7 11.0 %copy-start.2 = (f32[256,8]{0,1:T(8,128)S(1)}, f32[256,8]{0,1:T(8,128)}, u32[]{:S(2)}) copy-start(f32[256,8]{0,1:T(8,128)} %param.20) | copy-start | bytes 24580
  0.7 11.0 %copy-start.3 = (s32[4]{0:T(128)S(1)}, s32[4]{0:T(128)}, u32[]{:S(2)}) copy-start(s32[4]{0:T(128)} %cells.3) | copy-start | bytes 52
  3.7 21.9 %collective-permute-start.2 = (f32[32,8,1024]{2,1,0:T(8,128)S(1)}, f32[32,8,1024]{2,1,0:T(8,128)S(1)}, u32[]{:S(2)}, u32[]{:S(2)}) collective-permute-start(f32[32,8,1024]{2,1,0:T(8,128)S(1)} %get-tuple-element.40), channel_id=1, source_target_pairs={{0,1},{1,0},{2,3},{3,2},{4,5},{5,4},{6,7},{7,6},{8,9},{9,8},{10,11... | collective-permute-start | bytes 3145736 | tf_op jit(solution)/shard_map/ppermute | solution.py:406
  5.2 20.4 %collective-permute-start.3 = (f32[32,8,1024]{2,1,0:T(8,128)S(1)}, f32[32,8,1024]{2,1,0:T(8,128)S(1)}, u32[]{:S(2)}, u32[]{:S(2)}) collective-permute-start(f32[32,8,1024]{2,1,0:T(8,128)S(1)} %get-tuple-element.41), channel_id=1, source_target_pairs={{1,2},{2,1},{3,4},{4,3},{5,6},{6,5},{7,8},{8,7},{9,10},{10,9},{11,... | collective-permute-start | bytes 3145736 | tf_op jit(solution)/shard_map/ppermute | solution.py:403
  8.7 16.8 %collective-permute-start = (f32[8,16,1024]{2,1,0:T(8,128)S(1)}, f32[8,16,1024]{2,1,0:T(8,128)S(1)}, u32[]{:S(2)}, u32[]{:S(2)}) collective-permute-start(f32[8,16,1024]{2,1,0:T(8,128)S(1)} %get-tuple-element.38), channel_id=1, source_target_pairs={{0,16},{16,0},{32,48},{48,32},{64,80},{80,64},{96,112},{112,96},{1... | collective-permute-start | bytes 1572872 | tf_op jit(solution)/shard_map/ppermute | solution.py:405
  10.0 15.5 %collective-permute-start.1 = (f32[8,16,1024]{2,1,0:T(8,128)S(1)}, f32[8,16,1024]{2,1,0:T(8,128)S(1)}, u32[]{:S(2)}, u32[]{:S(2)}) collective-permute-start(f32[8,16,1024]{2,1,0:T(8,128)S(1)} %get-tuple-element.39), channel_id=1, source_target_pairs={{16,32},{32,16},{48,64},{64,48},{80,96},{96,80},{17,33},{33,17},{4... | collective-permute-start | bytes 1572872 | tf_op jit(solution)/shard_map/ppermute | solution.py:404
  25.6 7.1 %copy-start.1 = (s32[256,1]{0,1:T(1,128)S(1)}, s32[256,1]{0,1:T(1,128)}, u32[]{:S(2)}) copy-start(s32[256,1]{0,1:T(1,128)} %param.21) | copy-start | bytes 3076
  28.6 23.4 %collective-permute-start.6 = (f32[32,8,1024]{2,1,0:T(8,128)S(1)}, f32[32,8,1024]{2,1,0:T(8,128)S(1)}, u32[]{:S(2)}, u32[]{:S(2)}) collective-permute-start(f32[32,8,1024]{2,1,0:T(8,128)S(1)} %get-tuple-element.52), channel_id=1, source_target_pairs={{0,1},{1,0},{2,3},{3,2},{4,5},{5,4},{6,7},{7,6},{8,9},{9,8},{10,11... | collective-permute-start | bytes 3145736 | tf_op jit(solution)/shard_map/ppermute | solution.py:406
  28.7 23.3 %collective-permute-start.7 = (f32[32,8,1024]{2,1,0:T(8,128)S(1)}, f32[32,8,1024]{2,1,0:T(8,128)S(1)}, u32[]{:S(2)}, u32[]{:S(2)}) collective-permute-start(f32[32,8,1024]{2,1,0:T(8,128)S(1)} %get-tuple-element.53), channel_id=1, source_target_pairs={{1,2},{2,1},{3,4},{4,3},{5,6},{6,5},{7,8},{8,7},{9,10},{10,9},{11,... | collective-permute-start | bytes 3145736 | tf_op jit(solution)/shard_map/ppermute | solution.py:403
  32.8 19.1 %collective-permute-start.4 = (f32[8,16,1024]{2,1,0:T(8,128)S(1)}, f32[8,16,1024]{2,1,0:T(8,128)S(1)}, u32[]{:S(2)}, u32[]{:S(2)}) collective-permute-start(f32[8,16,1024]{2,1,0:T(8,128)S(1)} %get-tuple-element.50), channel_id=1, source_target_pairs={{0,16},{16,0},{32,48},{48,32},{64,80},{80,64},{96,112},{112,96},{1... | collective-permute-start | bytes 1572872 | tf_op jit(solution)/shard_map/ppermute | solution.py:405
  36.3 15.7 %collective-permute-start.5 = (f32[8,16,1024]{2,1,0:T(8,128)S(1)}, f32[8,16,1024]{2,1,0:T(8,128)S(1)}, u32[]{:S(2)}, u32[]{:S(2)}) collective-permute-start(f32[8,16,1024]{2,1,0:T(8,128)S(1)} %get-tuple-element.51), channel_id=1, source_target_pairs={{16,32},{32,16},{48,64},{64,48},{80,96},{96,80},{17,33},{33,17},{4... | collective-permute-start | bytes 1572872 | tf_op jit(solution)/shard_map/ppermute | solution.py:404

commit v4 on v3

--- a/solution.py
+++ b/solution.py
@@ -4,6 +4,7 @@
 from jax.experimental import pallas as pl
 from jax.experimental.pallas import tpu as pltpu
 from jax.sharding import PartitionSpec as P
+
 
 CAP = 4
 SCALE = 5040.0
@@ -79,7 +80,24 @@
         xb[i + 4] = born[start_b + i]
 
 
-def pack_kernel(place, wave_in, born_in, wave_rows, born_rows, xa, xb, ya, yb, wave, born, sems):
+def edge_kernel(place, ends, wave, born, xa, xb, place_out, ends_out, sems):
+    for i in range(2):
+        place_out[i] = place[i]
+        ends_out[i] = ends[i]
+    even = place[0] == 0
+    starts = (jnp.where(even, CX - 4, 0), jnp.where(even, 0, CX - 4))
+    copies = [
+        pltpu.make_async_copy(field.at[pl.ds(start, 4)], face.at[pl.ds(4 * i, 4)], sems.at[j, i])
+        for j, (start, face) in enumerate(zip(starts, (xa, xb)))
+        for i, field in enumerate((wave, born))
+    ]
+    for copy in copies:
+        copy.start()
+    for copy in copies:
+        copy.wait()
+
+
+def pack_kernel(place, wave_in, born_in, wave_rows, born_rows, ya, yb, wave, born, sems):
     sub, _ = iotas()
     even_y = place[1] == 0
     parts = 4
@@ -111,7 +129,6 @@
             return carry
 
         lax.fori_loop(c * each, (c + 1) * each, step, 0)
-    pack_x(place[0] == 0, xa, xb, wave, born)
 
 
 def along_z(ref, high, low, table, out):
@@ -180,7 +197,8 @@
 
 def inner_first(
     cells, amps, wave, born, table, taps, weights, wave_old_in, born_old_in, courant_in, contrast_in,
-    wave_part, born_part, courant, contrast, picks, wave_old, born_old, high, low, wave_z, born_z, sems,
+    wave_part, born_part, courant, contrast, picks, wave_next, born_next,
+    wave_old, born_old, high, low, wave_z, born_z, sems,
 ):
     copies = [
         pltpu.make_async_copy(a, b, sems.at[i])
@@ -193,6 +211,7 @@
     along_z(wave, high, low, table, wave_z)
     along_z(born, high, low, table, born_z)
     make_picks(taps, weights, picks)
+    clear(wave_next, born_next)
     for copy in copies:
         copy.wait()
 
@@ -245,7 +264,10 @@
         copy.wait()
 
 
-def fix(place, wave_part, born_part, courant, contrast, xa, xb, ya, yb, wave, born, wave_rows, born_rows, faces):
+def fix(
+    place, ends, wave_part, born_part, courant, contrast, xa, xb, ya, yb, wave, born, wave_rows, born_rows, y_faces,
+    edges, middle,
+):
     sub, _ = iotas()
     even_x = place[0] == 0
     even_y = place[1] == 0
@@ -278,7 +300,7 @@
                         reach = offset + 4 - m if side < 0 else 4 - offset + m
                         if 1 <= reach <= 4:
                             lone, other = (xb, xa) if side < 0 else (xa, xb)
-                            w = WEIGHTS[reach - 1]
+                            w = WEIGHTS[reach - 1] * ends[0 if side < 0 else 1]
                             wave_sum = wave_sum + w * jnp.where(even_x, tile(lone, m, t, z), tile(other, m, t, z))
                             born_sum = born_sum + w * jnp.where(even_x, tile(lone, m + 4, t, z), tile(other, m + 4, t, z))
                 speed = tile(courant, x, t, z)
@@ -291,39 +313,61 @@
                     wave_rows[strip(x, t, z), :] = wave_value
                 born_rows[strip(x, t, z), :] = born_value
                 finals.append((wave_value, born_value))
-            if faces is not None:
+            if y_faces is not None:
                 (w0, b0), (w1, b1) = finals
-                pack_y(sub, even_y, faces[2], faces[3], x, z, w0, w1, b0, b1)
-
-    for x in range(4):
-        one(x, -1, x)
-    lax.fori_loop(4, CX - 4, lambda x, carry: (one(x, 0, 0), carry)[1], 0)
-    for x in range(CX - 4, CX):
-        one(x, 1, x - (CX - 4))
-    if faces is not None:
-        pack_x(even_x, faces[0], faces[1], wave, born)
-
-
-def fix_kernel(
-    place, wave_part, born_part, courant, contrast, rxa, rxb, rya, ryb,
-    wave, born, wave_rows, born_rows, xa, xb, ya, yb,
-):
-    clear(wave_rows, born_rows)
+                pack_y(sub, even_y, *y_faces, x, z, w0, w1, b0, b1)
+
+    if edges:
+        for x in range(4):
+            one(x, -1, x)
+        for x in range(CX - 4, CX):
+            one(x, 1, x - (CX - 4))
+    if middle:
+        lax.fori_loop(4, CX - 4, lambda x, carry: (one(x, 0, 0), carry)[1], 0)
+
+
+def fix_edges(
+    place, ends, wave_part, born_part, courant, contrast, rxa, rxb, rya, ryb, rows_a, rows_b,
+    wave, born, wave_rows, born_rows, xa, xb,
+):
     fix(
-        place, wave_part, born_part, courant, contrast, rxa, rxb, rya, ryb,
-        wave, born, wave_rows, born_rows, (xa, xb, ya, yb),
-    )
+        place, ends, wave_part, born_part, courant, contrast, rxa, rxb, rya, ryb,
+        wave, born, wave_rows, born_rows, None, True, False,
+    )
+    pack_x(place[0] == 0, xa, xb, wave, born)
+
+
+def fix_middle(
+    place, ends, wave_part, born_part, courant, contrast, rya, ryb, wave_in, born_in, rows_a, rows_b,
+    wave, born, wave_rows, born_rows, ya, yb,
+):
+    fix(
+        place, ends, wave_part, born_part, courant, contrast, None, None, rya, ryb,
+        wave, born, wave_rows, born_rows, (ya, yb), False, True,
+    )
+    sub, _ = iotas()
+    even_y = place[1] == 0
+
+    def step(i, carry):
+        x = jnp.where(i < 4, i, i + CX - 8)
+        for z in range(TZ):
+            pack_y(
+                sub, even_y, ya, yb, x, z, tile(wave, x, 0, z), tile(wave, x, 1, z), tile(born, x, 0, z), tile(born, x, 1, z)
+            )
+        return carry
+
+    lax.fori_loop(0, 8, step, 0)
 
 
 def take(rows_at, grid, picks, rows, out):
     def step(g, carry):
-        for j in range(4):
-            r = g * 4 + j
+        for j in range(8):
+            r = g * 8 + j
             for t in range(8):
                 rows[pl.ds(r * 8 + t, 1), :] = grid[pl.ds(rows_at[t, r], 1), :]
         return carry
 
-    lax.fori_loop(0, 64, step, 0)
+    lax.fori_loop(0, 32, step, 0)
 
     def total(g, carry):
         part = pl.ds(pl.multiple_of(g * 256, 256), 256)
@@ -335,10 +379,13 @@
 
 
 def last_kernel(
-    place, rows_at, wave_part, born_part, courant, contrast, rxa, rxb, rya, ryb,
+    place, ends, rows_at, wave_part, born_part, courant, contrast, rxa, rxb, rya, ryb,
     picks, first, slots, dest, wave_out, born_out, packed, wave, born, grid, rows, sums, sems,
 ):
-    fix(place, wave_part, born_part, courant, contrast, rxa, rxb, rya, ryb, wave, born, None, grid, None)
+    fix(
+        place, ends, wave_part, born_part, courant, contrast, rxa, rxb, rya, ryb,
+        wave, born, None, grid, None, True, True,
+    )
     copies = [
         pltpu.make_async_copy(wave, wave_out, sems.at[0]),
         pltpu.make_async_copy(born, born_out, sems.at[1]),
@@ -385,26 +432,31 @@
     return pltpu.with_memory_space_constraint(value, pltpu.HBM)
 
 
-def call(kernel, name, args, specs, outs, scratch, mib, us):
+def call(kernel, args, specs, outs, scratch, mib, us, aliases=None):
     return pl.pallas_call(
         kernel,
-        name=name,
         out_shape=tuple(o[1] for o in outs),
         in_specs=specs,
         out_specs=tuple(o[0] for o in outs),
         scratch_shapes=list(scratch),
+        input_output_aliases=aliases or {},
         compiler_params=pltpu.CompilerParams(vmem_limit_bytes=mib * 1024 * 1024),
         cost_estimate=pl.CostEstimate(flops=0, bytes_accessed=us * 3_000_000, transcendentals=0),
     )(*args)
 
 
-def exchange(faces):
-    xa, xb, ya, yb = faces
+def swap_x(xa, xb):
+    flat = [(i * 16 + g, j * 16 + g) for i, j in pairs(8, 1) for g in range(16)]
+    flat += [(i * 16 + g, i * 16 + (g ^ 1)) for i in (0, 7) for g in range(16)]
+    rxb = lax.ppermute(xb, ("gx", "gy"), flat)
+    rxa = lax.ppermute(xa, "gx", pairs(8, 0))
+    return rxa, rxb
+
+
+def swap_y(ya, yb):
     ryb = lax.ppermute(yb, "gy", pairs(16, 1))
-    rxb = lax.ppermute(xb, "gx", pairs(8, 1))
-    rxa = lax.ppermute(xa, "gx", pairs(8, 0))
     rya = lax.ppermute(ya, "gy", pairs(16, 0))
-    return rxa, rxb, rya, ryb
+    return rya, ryb
 
 
 def z_table():
@@ -417,7 +469,7 @@
     return table.astype(BF16)
 
 
-def body(
+def steps(
     wave_old,
     wave_now,
     born_old,
@@ -430,25 +482,34 @@
     rcv_weight,
     rcv_dest,
 ):
-    place = jnp.stack([lax.axis_index("gx") % 2, lax.axis_index("gy") % 2]).astype(jnp.int32)
+    index_x, index_y = lax.axis_index("gx"), lax.axis_index("gy")
+    place = jnp.stack([index_x & 1, index_y & 1]).astype(jnp.int32)
+    ends = jnp.stack([index_x > 0, index_x < 7]).astype(F32)
     field = pltpu.VMEM(BLOCK, F32)
     halves = [pltpu.VMEM((CX * CY, NZ + 256), BF16)] * 2 + [pltpu.VMEM((CX * CY, NZ), F32)] * 2
-    face_outs = [plain(XFACE), plain(XFACE), plain(YFACE), plain(YFACE)]
-
-    wave_rows, born_rows, *faces = call(
-        pack_kernel, "pack", (place, still(wave_now), still(born_now)), [SM, HB, HB],
-        [kept((ROWS, 128))] * 2 + face_outs, [field, field, pltpu.SemaphoreType.DMA((2, 4))], 10, 2,
-    )
-    halo = exchange(faces)
+    x_faces, y_faces = [plain(XFACE)] * 2, [plain(YFACE)] * 2
+    fixed = [kept(BLOCK)] * 2 + [kept((ROWS, 128))] * 2
+
+    xa, xb, place, ends = call(
+        edge_kernel, (place, ends, still(wave_now), still(born_now)), [SM, SM, HB, HB],
+        x_faces + [(SM, jax.ShapeDtypeStruct((2,), jnp.int32)), (SM, jax.ShapeDtypeStruct((2,), F32))],
+        [pltpu.SemaphoreType.DMA((2, 2))], 4, 1,
+    )
+    halo_x = swap_x(xa, xb)
+    wave_rows, born_rows, ya, yb = call(
+        pack_kernel, (place, still(wave_now), still(born_now)), [SM, HB, HB],
+        [kept((ROWS, 128))] * 2 + y_faces, [field, field, pltpu.SemaphoreType.DMA((2, 4))], 10, 2,
+    )
+    halo_y = swap_y(ya, yb)
     table = z_table()
-    wave_part, born_part, speed, factor, picks = call(
-        inner_first, "inner1",
+    wave_part, born_part, speed, factor, picks, wave_mid_rows, born_mid_rows = call(
+        inner_first,
         (
             src_cell, src_amp[:, 0], wave_rows, born_rows, table, rcv_cell.T, rcv_weight.T,
             still(wave_old), still(born_old), still(courant), still(contrast),
         ),
         [SM, SM] + [VM] * 5 + [HB] * 4,
-        [kept(BLOCK)] * 4 + [kept((2048, 128))], [field, field, *halves, pltpu.SemaphoreType.DMA((4,))], 14, 8,
+        [kept(BLOCK)] * 4 + [kept((2048, 128))] + [kept((ROWS, 128))] * 2, [field, field, *halves, pltpu.SemaphoreType.DMA((4,))], 14, 8,
     )
 
     cell = rcv_cell.T
@@ -460,13 +521,19 @@
     lane = lax.broadcasted_iota(jnp.int32, (256, 128), 1)
     slots = jnp.where((lane < 8) & (lane % 4 == slot[:, None]), 1.0, 0.0).astype(F32)
 
-    wave_mid, born_mid, wave_mid_rows, born_mid_rows, *faces = call(
-        fix_kernel, "fix1", (place, wave_part, born_part, speed, factor, *halo), [SM] + [VM] * 8,
-        [kept(BLOCK)] * 2 + [kept((ROWS, 128))] * 2 + face_outs, [], 10, 3,
-    )
-    halo = exchange(faces)
+    shared = (wave_part, born_part, speed, factor)
+    *mid, xa, xb = call(
+        fix_edges, (place, ends, *shared, *halo_x, *halo_y, wave_mid_rows, born_mid_rows),
+        [SM] * 2 + [VM] * 10, fixed + x_faces, [], 4, 2, {10: 2, 11: 3},
+    )
+    next_x = swap_x(xa, xb)
+    wave_mid, born_mid, wave_mid_rows, born_mid_rows, ya, yb = call(
+        fix_middle, (place, ends, *shared, *halo_y, *mid),
+        [SM] * 2 + [VM] * 10, fixed + y_faces, [], 4, 2, {8: 0, 9: 1, 10: 2, 11: 3},
+    )
+    next_y = swap_y(ya, yb)
     wave_part, born_part, first, wave_next, born_next = call(
-        inner_second, "inner2",
+        inner_second,
         (
             src_cell, src_amp[:, 1], rows_at, wave_mid_rows, born_mid_rows, table, wave_rows, born_rows,
             speed, factor, picks, wave_mid, born_mid,
@@ -476,9 +543,9 @@
         [*halves, pltpu.VMEM((2048, 128), F32), pltpu.SemaphoreType.DMA((2,))], 12, 10,
     )
     wave_last, born_last, packed = call(
-        last_kernel, "last",
-        (place, rows_at, wave_part, born_part, speed, factor, *halo, picks, first, slots, dest[None, :]),
-        [SM, SM] + [VM] * 12,
+        last_kernel,
+        (place, ends, rows_at, wave_part, born_part, speed, factor, *next_x, *next_y, picks, first, slots, dest[None, :]),
+        [SM] * 3 + [VM] * 12,
         [away(BLOCK), away(BLOCK), plain((128, 128))],
         [
             field, field, pltpu.VMEM((ROWS, 128), F32), pltpu.VMEM((2048, 128), F32),
@@ -501,7 +568,7 @@
         P(("gx", "gy"), None),
     )
     return jax.shard_map(
-        body,
+        steps,
         mesh=mesh,
         in_specs=placed,
         out_specs=(P("gx", "gy", None),) * 4 + (P(("gx", "gy"), None, None, None),),

time: 91.9 us -> 91.3 us (level)
  Pallas kernels: 40.7 us -> 43.4 us
  starting transfers between devices: 15.1 us -> 12.5 us
    pallas_call x5 -> x7, Pallas kernels: 40.7 us -> 43.4 us  [call(): pl.pallas_call(kernel, out_shape=tuple((o[1] for o in outs)), in_specs=sp...]
    ppermute x8, starting transfers between devices: 15.1 us -> 12.5 us  [the longest x2 7 us: swap_y(): ryb = lax.ppermute(yb, 'gy', pairs(16, 1))]
  transfers between devices with their start and end apart: 8 -> 8, of which waited for: 0 -> 0; matrix products, arithmetic and copies ran while one was open for 1% -> 1% of each run, Pallas kernels for 31% -> 32%
where the time goes in v4:
time: 91.3 us; the launch traced here: 91.1 us
  Pallas kernels  43.4 us (48%)
  blocking collectives  32.2 us (35%)
  starting transfers between devices  12.5 us (14%)
  other arithmetic  1.4 us (2%)
    pallas_call x7, Pallas kernels, call(): pl.pallas_call(kernel, out_shape=tuple((o[1] for o in outs)), in_specs=sp...  43.4 us
    all_to_all x1, blocking collectives, steps(): lax.all_to_all(packed.reshape(128, 1, 128), ('gx', 'gy'), split_axis=0, c...  32.2 us
    ppermute x2, starting transfers between devices, swap_y(): ryb = lax.ppermute(yb, 'gy', pairs(16, 1))  7 us
    ppermute x2, starting transfers between devices, swap_x(): rxa = lax.ppermute(xa, 'gx', pairs(8, 0))  3.47 us
    ppermute x2, starting transfers between devices, swap_y(): rya = lax.ppermute(ya, 'gy', pairs(16, 0))  2.04 us
  transfers between devices with their start and end apart: 8, of which 0 were waited for; matrix products, arithmetic and copies ran while one was open for 1% of the time, Pallas kernels for 32%

profile of v4, /device:TPU:1, one launch (start us, length us, event | category | flops | bytes accessed | tf_op | source)
XLA Modules:
  0.0 91.1 jit_solution(16135075506692352890)
XLA Ops:
  0.6 0.1 add_convert_fusion.ends
  0.7 0.1 pad_add_fusion.place
  0.8 2.4 %shard_map.146 = (f32[8,16,1024]{2,1,0:T(8,128)S(1)}, f32[8,16,1024]{2,1,0:T(8,128)S(1)}, s32[2]{0:T(128)S(1)}, f32[2]{0:T(128)S(1)}) custom-call(s32[2]{0:T(128)S(1)} %pad_add_fusion.place, f32[2]{0:T(128)S(1)} %add_convert_fusion.ends, f32[32,16,1024]{2,1,0:T(8,128)} %wave_in.1, f32[32,16,1024]{2,1,0:T(8,128)} %born_in.1), custom_call_target="tpu_custom_call" | custom-call | bytes 3000000 | tf_op jit(solution)/shard_map/pallas_call | solution.py:436
  3.2 0.0 copy-start.4
  3.2 0.0 copy-start
  3.2 0.0 copy-start.2
  3.2 0.0 copy-start.3
  3.2 2.9 %shard_map.147 = (f32[7688,128]{1,0:T(8,128)S(1)}, f32[7688,128]{1,0:T(8,128)S(1)}, f32[32,8,1024]{2,1,0:T(8,128)S(1)}, f32[32,8,1024]{2,1,0:T(8,128)S(1)}) custom-call(s32[2]{0:T(128)S(1)} %get-tuple-element.40.place, f32[32,16,1024]{2,1,0:T(8,128)} %wave_in.1, f32[32,16,1024]{2,1,0:T(8,128)} %born_in.1), custom_call_target="tpu_custom_call" | custom-call | bytes 6000000 | tf_op jit(solution)/shard_map/pallas_call | solution.py:436
  6.1 1.5 %collective-permute-start = (f32[32,8,1024]{2,1,0:T(8,128)S(1)}, f32[32,8,1024]{2,1,0:T(8,128)S(1)}, u32[]{:S(2)}, u32[]{:S(2)}) collective-permute-start(f32[32,8,1024]{2,1,0:T(8,128)S(1)} %get-tuple-element.48), channel_id=1, source_target_pairs={{0,1},{1,0},{2,3},{3,2},{4,5},{5,4},{6,7},{7,6},{8,9},{9,8},{10,11... | collective-permute-start | bytes 3145736 | tf_op jit(solution)/shard_map/ppermute | solution.py:458
  7.6 3.6 %collective-permute-start.1 = (f32[32,8,1024]{2,1,0:T(8,128)S(1)}, f32[32,8,1024]{2,1,0:T(8,128)S(1)}, u32[]{:S(2)}, u32[]{:S(2)}) collective-permute-start(f32[32,8,1024]{2,1,0:T(8,128)S(1)} %get-tuple-element.49), channel_id=1, source_target_pairs={{1,2},{2,1},{3,4},{4,3},{5,6},{6,5},{7,8},{8,7},{9,10},{10,9},{11,... | collective-permute-start | bytes 3145736 | tf_op jit(solution)/shard_map/ppermute | solution.py:457
  11.1 1.3 %collective-permute-start.2 = (f32[8,16,1024]{2,1,0:T(8,128)S(1)}, f32[8,16,1024]{2,1,0:T(8,128)S(1)}, u32[]{:S(2)}, u32[]{:S(2)}) collective-permute-start(f32[8,16,1024]{2,1,0:T(8,128)S(1)} %get-tuple-element.50), channel_id=1, source_target_pairs={{0,16},{16,0},{32,48},{48,32},{64,80},{80,64},{96,112},{112,96},{1... | collective-permute-start | bytes 1572872 | tf_op jit(solution)/shard_map/ppermute | solution.py:452
  12.4 0.0 collective-permute-start.3
  12.4 0.0 copy-done.4
  12.5 0.9 %select_convert_fusion.table = bf16[1024,256]{1,0:T(8,128)(2,1)S(1)} fusion(s32[1024]{0:T(1024)S(1)} %get-tuple-element.82, s32[1024]{0:T(1024)S(1)} %get-tuple-element.83, pred[1024]{0:T(1024)(128)(4,1)S(1)} %fusion.10), kind=kLoop, calls=%fused_computation | loop fusion | flops 3407872 | bytes 533504 | tf_op jit(solution)/shard_map/convert_element_type | solution.py:469
  13.4 0.0 copy-done
  13.4 0.0 copy-done.2
  13.4 0.0 copy-done.3
  13.4 14.4 %shard_map.148 = (f32[32,16,1024]{2,1,0:T(8,128)S(1)}, f32[32,16,1024]{2,1,0:T(8,128)S(1)}, f32[32,16,1024]{2,1,0:T(8,128)S(1)}, f32[32,16,1024]{2,1,0:T(8,128)S...) custom-call(s32[4]{0:T(128)S(1)} %copy-done.3, f32[4]{0:T(128)S(1)} %get-tuple-element.80.amps, ...), custom_call_target="tpu_custom_call" | custom-call | bytes 24000000 | tf_op jit(solution)/shard_map/pallas_call | solution.py:436
  27.9 0.0 collective-permute-done.2.rxa
  27.9 0.0 collective-permute-done.3.rxb
  27.9 0.0 collective-permute-done.rya
  27.9 0.0 collective-permute-done.1.ryb
  27.9 1.3 %shard_map.149 = (f32[32,16,1024]{2,1,0:T(8,128)S(1)}, f32[32,16,1024]{2,1,0:T(8,128)S(1)}, f32[7688,128]{1,0:T(8,128)S(1)}, f32[7688,128]{1,0:T(8,128)S(1)}, f3...) custom-call(s32[2]{0:T(128)S(1)} %get-tuple-element.40.place, ...), custom_call_target="tpu_custom_call", output_to_operand_aliasing={{2}: (10, {}), {3}: (11, {})} | custom-call | bytes 6000000 | tf_op jit(solution)/shard_map/pallas_call | solution.py:436
  29.2 0.0 copy-start.1
  29.2 2.1 %shard_map.150 = (f32[32,16,1024]{2,1,0:T(8,128)S(1)}, f32[32,16,1024]{2,1,0:T(8,128)S(1)}, f32[7688,128]{1,0:T(8,128)S(1)}, f32[7688,128]{1,0:T(8,128)S(1)}, f3...) custom-call(s32[2]{0:T(128)S(1)} %get-tuple-element.40.place, ...), custom_call_target="tpu_custom_call", output_to_operand_aliasing={{0}: (8, {}), {1}: (9, {}), {2}: (10, {}), {3}: (11, {})} | custom-call | bytes 6000000 | tf_op jit(solution)/shard_map/pallas_call | solution.py:436
  31.3 0.6 collective-permute-start.6
  31.8 3.4 %collective-permute-start.7 = (f32[32,8,1024]{2,1,0:T(8,128)S(1)}, f32[32,8,1024]{2,1,0:T(8,128)S(1)}, u32[]{:S(2)}, u32[]{:S(2)}) collective-permute-start(f32[32,8,1024]{2,1,0:T(8,128)S(1)} %get-tuple-element.69), channel_id=1, source_target_pairs={{1,2},{2,1},{3,4},{4,3},{5,6},{6,5},{7,8},{8,7},{9,10},{10,9},{11,... | collective-permute-start | bytes 3145736 | tf_op jit(solution)/shard_map/ppermute | solution.py:457
  35.3 0.0 copy-done.1
  35.3 0.2 convert_reduce_fusion
  35.5 2.2 %collective-permute-start.4 = (f32[8,16,1024]{2,1,0:T(8,128)S(1)}, f32[8,16,1024]{2,1,0:T(8,128)S(1)}, u32[]{:S(2)}, u32[]{:S(2)}) collective-permute-start(f32[8,16,1024]{2,1,0:T(8,128)S(1)} %get-tuple-element.66), channel_id=1, source_target_pairs={{0,16},{16,0},{32,48},{48,32},{64,80},{80,64},{96,112},{112,96},{1... | collective-permute-start | bytes 1572872 | tf_op jit(solution)/shard_map/ppermute | solution.py:452
  37.7 0.0 collective-permute-start.5
  37.7 0.1 fusion.6.slots
  37.8 14.5 %shard_map.151 = (f32[32,16,1024]{2,1,0:T(8,128)S(1)}, f32[32,16,1024]{2,1,0:T(8,128)S(1)}, f32[256,128]{1,0:T(8,128)S(1)}, f32[32,16,1024]{2,1,0:T(8,128)}, f32[32,16,1024]{2,1,0:T(8,128)}) custom-call(s32[4]{0:T(128)S(1)} %copy-done.3, f32[4]{0:T(128)S(1)} %get-tuple-element.81.amps, s32[8,256]{1,0:T(8,128)S(1)} %and_add_fusion.rows_at, ...), custom_call_target="tpu_custom_call" | custom-call | bytes 30000000 | tf_op jit(solution)/shard_map/pallas_call | solution.py:436
  52.4 0.0 collective-permute-done.4.rxa
  52.4 0.0 collective-permute-done.5.rxb
  52.4 0.0 collective-permute-done.6.rya
  52.4 0.0 collective-permute-done.7.ryb
  52.4 5.8 %shard_map.152 = (f32[32,16,1024]{2,1,0:T(8,128)}, f32[32,16,1024]{2,1,0:T(8,128)}, f32[128,128]{1,0:T(8,128)S(1)}) custom-call(s32[2]{0:T(128)S(1)} %get-tuple-element.40.place, f32[2]{0:T(128)S(1)} %get-tuple-element.41.ends, s32[8,256]{1,0:T(8,128)S(1)} %and_add_fusion.rows_at, f32[32,16,1024]{2,1,0:T(8,128)S(1)} %get-tuple-element.64.wave_part, ...), custom_call_target="tpu_custom_call" | custom-call | bytes 15000000 | tf_op jit(solution)/shard_map/pallas_call | solution.py:436
  58.2 32.2 %all_to_all.5 = f32[128,1,128]{2,1,0:T(1,128)S(1)} all-to-all(f32[128,1,128]{2,1,0:T(1,128)S(1)} %bitcast.18), channel_id=1, replica_groups=mesh['gx'=8,'gy'=16] {'gx','gy'}, dimensions={0} | all-to-all | bytes 131072 | tf_op jit(solution)/shard_map/all_to_all | solution.py:555
  90.4 0.7 copy.28
  (6 shorter events, 0.0 us)
Async XLA Ops:
  3.2 9.3 %copy-start.4 = (f32[4,2]{0,1:T(2,128)S(1)}, f32[4,2]{0,1:T(2,128)}, u32[]{:S(2)}) copy-start(f32[4,2]{0,1:T(2,128)} %param.18) | copy-start | bytes 100
  3.2 10.2 %copy-start = (s32[256,8]{0,1:T(8,128)S(1)}, s32[256,8]{0,1:T(8,128)}, u32[]{:S(2)}) copy-start(s32[256,8]{0,1:T(8,128)} %param.19) | copy-start | bytes 24580
  3.2 10.2 %copy-start.2 = (f32[256,8]{0,1:T(8,128)S(1)}, f32[256,8]{0,1:T(8,128)}, u32[]{:S(2)}) copy-start(f32[256,8]{0,1:T(8,128)} %param.20) | copy-start | bytes 24580
  3.2 10.2 %copy-start.3 = (s32[4]{0:T(128)S(1)}, s32[4]{0:T(128)}, u32[]{:S(2)}) copy-start(s32[4]{0:T(128)} %cells.3) | copy-start | bytes 52
  6.1 21.8 %collective-permute-start = (f32[32,8,1024]{2,1,0:T(8,128)S(1)}, f32[32,8,1024]{2,1,0:T(8,128)S(1)}, u32[]{:S(2)}, u32[]{:S(2)}) collective-permute-start(f32[32,8,1024]{2,1,0:T(8,128)S(1)} %get-tuple-element.48), channel_id=1, source_target_pairs={{0,1},{1,0},{2,3},{3,2},{4,5},{5,4},{6,7},{7,6},{8,9},{9,8},{10,11... | collective-permute-start | bytes 3145736 | tf_op jit(solution)/shard_map/ppermute | solution.py:458
  7.6 20.3 %collective-permute-start.1 = (f32[32,8,1024]{2,1,0:T(8,128)S(1)}, f32[32,8,1024]{2,1,0:T(8,128)S(1)}, u32[]{:S(2)}, u32[]{:S(2)}) collective-permute-start(f32[32,8,1024]{2,1,0:T(8,128)S(1)} %get-tuple-element.49), channel_id=1, source_target_pairs={{1,2},{2,1},{3,4},{4,3},{5,6},{6,5},{7,8},{8,7},{9,10},{10,9},{11,... | collective-permute-start | bytes 3145736 | tf_op jit(solution)/shard_map/ppermute | solution.py:457
  11.1 16.8 %collective-permute-start.2 = (f32[8,16,1024]{2,1,0:T(8,128)S(1)}, f32[8,16,1024]{2,1,0:T(8,128)S(1)}, u32[]{:S(2)}, u32[]{:S(2)}) collective-permute-start(f32[8,16,1024]{2,1,0:T(8,128)S(1)} %get-tuple-element.50), channel_id=1, source_target_pairs={{0,16},{16,0},{32,48},{48,32},{64,80},{80,64},{96,112},{112,96},{1... | collective-permute-start | bytes 1572872 | tf_op jit(solution)/shard_map/ppermute | solution.py:452
  12.4 15.5 %collective-permute-start.3 = (f32[8,16,1024]{2,1,0:T(8,128)S(1)}, f32[8,16,1024]{2,1,0:T(8,128)S(1)}, u32[]{:S(2)}, u32[]{:S(2)}) collective-permute-start(f32[8,16,1024]{2,1,0:T(8,128)S(1)} %get-tuple-element.51), channel_id=1, source_target_pairs={{16,32},{17,33},{18,34},{19,35},{20,36},{21,37},{22,38},{23,39},{2... | collective-permute-start | bytes 1572872 | tf_op jit(solution)/shard_map/ppermute | solution.py:451
  29.2 6.1 %copy-start.1 = (s32[256,1]{0,1:T(1,128)S(1)}, s32[256,1]{0,1:T(1,128)}, u32[]{:S(2)}) copy-start(s32[256,1]{0,1:T(1,128)} %param.21) | copy-start | bytes 3076
  31.3 21.1 %collective-permute-start.6 = (f32[32,8,1024]{2,1,0:T(8,128)S(1)}, f32[32,8,1024]{2,1,0:T(8,128)S(1)}, u32[]{:S(2)}, u32[]{:S(2)}) collective-permute-start(f32[32,8,1024]{2,1,0:T(8,128)S(1)} %get-tuple-element.68), channel_id=1, source_target_pairs={{0,1},{1,0},{2,3},{3,2},{4,5},{5,4},{6,7},{7,6},{8,9},{9,8},{10,11... | collective-permute-start | bytes 3145736 | tf_op jit(solution)/shard_map/ppermute | solution.py:458
  31.8 20.5 %collective-permute-start.7 = (f32[32,8,1024]{2,1,0:T(8,128)S(1)}, f32[32,8,1024]{2,1,0:T(8,128)S(1)}, u32[]{:S(2)}, u32[]{:S(2)}) collective-permute-start(f32[32,8,1024]{2,1,0:T(8,128)S(1)} %get-tuple-element.69), channel_id=1, source_target_pairs={{1,2},{2,1},{3,4},{4,3},{5,6},{6,5},{7,8},{8,7},{9,10},{10,9},{11,... | collective-permute-start | bytes 3145736 | tf_op jit(solution)/shard_map/ppermute | solution.py:457
  35.5 16.9 %collective-permute-start.4 = (f32[8,16,1024]{2,1,0:T(8,128)S(1)}, f32[8,16,1024]{2,1,0:T(8,128)S(1)}, u32[]{:S(2)}, u32[]{:S(2)}) collective-permute-start(f32[8,16,1024]{2,1,0:T(8,128)S(1)} %get-tuple-element.66), channel_id=1, source_target_pairs={{0,16},{16,0},{32,48},{48,32},{64,80},{80,64},{96,112},{112,96},{1... | collective-permute-start | bytes 1572872 | tf_op jit(solution)/shard_map/ppermute | solution.py:452
  37.7 14.7 %collective-permute-start.5 = (f32[8,16,1024]{2,1,0:T(8,128)S(1)}, f32[8,16,1024]{2,1,0:T(8,128)S(1)}, u32[]{:S(2)}, u32[]{:S(2)}) collective-permute-start(f32[8,16,1024]{2,1,0:T(8,128)S(1)} %get-tuple-element.67), channel_id=1, source_target_pairs={{16,32},{17,33},{18,34},{19,35},{20,36},{21,37},{22,38},{23,39},{2... | collective-permute-start | bytes 1572872 | tf_op jit(solution)/shard_map/ppermute | solution.py:451

commit v5 on v4

--- a/solution.py
+++ b/solution.py
@@ -15,9 +15,9 @@
 BLOCK = (CX, CY, NZ)
 XFACE = (8, CY, NZ)
 YFACE = (CX, 8, NZ)
-STRIP = 24
+STRIP = CY
 LAYER = TZ * STRIP
-ROWS = (CX + 8) * LAYER + 8
+ROWS = CX * LAYER
 F32 = jnp.float32
 BF16 = jnp.bfloat16
 
@@ -36,31 +36,8 @@
     ref[x, t * 8 : t * 8 + 8, z * 128 : z * 128 + 128] = value
 
 
-def strip(x, t, z, shift=0):
-    return pl.ds(x * LAYER + (4 * LAYER + z * STRIP + 8 + t * 8 + shift), 8)
-
-
-def clear(*refs):
-    zero = jnp.zeros((8, 128), F32)
-
-    def gaps(x, carry):
-        for z in range(TZ):
-            for ref in refs:
-                ref[pl.ds(pl.multiple_of(x * LAYER + z * STRIP, 8), 8), :] = zero
-        return carry
-
-    def layer(i, carry):
-        x = jnp.where(i < 4, i, i + CX)
-        for z in range(TZ):
-            for t in range(2):
-                for ref in refs:
-                    ref[pl.ds(pl.multiple_of(x * LAYER + z * STRIP + 8 + t * 8, 8), 8), :] = zero
-        return carry
-
-    lax.fori_loop(0, CX + 8, gaps, 0)
-    lax.fori_loop(0, 8, layer, 0)
-    for ref in refs:
-        ref[pl.ds(ROWS - 8, 8), :] = zero
+def strip(x, t, z):
+    return pl.ds(pl.multiple_of(x * LAYER + (z * STRIP + t * 8), 8), 8)
 
 
 def pack_y(sub, even, ya, yb, x, z, w0, w1, b0, b1):
@@ -97,41 +74,24 @@
         copy.wait()
 
 
-def pack_kernel(place, wave_in, born_in, wave_rows, born_rows, ya, yb, wave, born, sems):
+def pack_kernel(place, wave, born, wave_rows, born_rows, ya, yb):
     sub, _ = iotas()
     even_y = place[1] == 0
-    parts = 4
-    each = CX // parts
-
-    def copies(c):
-        part = pl.ds(c * each, each)
-        return (
-            pltpu.make_async_copy(wave_in.at[part], wave.at[part], sems.at[0, c]),
-            pltpu.make_async_copy(born_in.at[part], born.at[part], sems.at[1, c]),
-        )
-
-    for c in range(parts):
-        for copy in copies(c):
-            copy.start()
-    clear(wave_rows, born_rows)
-    for c in range(parts):
-        for copy in copies(c):
-            copy.wait()
-
-        def step(x, carry):
-            for z in range(TZ):
-                w0, w1, b0, b1 = tile(wave, x, 0, z), tile(wave, x, 1, z), tile(born, x, 0, z), tile(born, x, 1, z)
-                pack_y(sub, even_y, ya, yb, x, z, w0, w1, b0, b1)
-                wave_rows[strip(x, 0, z), :] = w0
-                wave_rows[strip(x, 1, z), :] = w1
-                born_rows[strip(x, 0, z), :] = b0
-                born_rows[strip(x, 1, z), :] = b1
-            return carry
-
-        lax.fori_loop(c * each, (c + 1) * each, step, 0)
-
-
-def along_z(ref, high, low, table, out):
+
+    def step(x, carry):
+        for z in range(TZ):
+            w0, w1, b0, b1 = tile(wave, x, 0, z), tile(wave, x, 1, z), tile(born, x, 0, z), tile(born, x, 1, z)
+            pack_y(sub, even_y, ya, yb, x, z, w0, w1, b0, b1)
+            wave_rows[strip(x, 0, z), :] = w0
+            wave_rows[strip(x, 1, z), :] = w1
+            born_rows[strip(x, 0, z), :] = b0
+            born_rows[strip(x, 1, z), :] = b1
+        return carry
+
+    lax.fori_loop(0, CX, step, 0)
+
+
+def stencil(ref, high, low, z_weights, xy_weights, out):
     zero = jnp.zeros((CX * CY, 128), BF16)
     for half in (high, low):
         half[:, 0:128] = zero
@@ -140,7 +100,7 @@
     def split(x, carry):
         rows = pl.ds(pl.multiple_of(x * CY, CY), CY)
         for z in range(TZ):
-            value = ref[pl.ds(pl.multiple_of(x * LAYER + (4 * LAYER + z * STRIP + 8), 8), CY), :]
+            value = ref[pl.ds(pl.multiple_of(x * LAYER + z * STRIP, CY), CY), :]
             top = value.astype(BF16)
             high[rows, 128 + z * 128 : 256 + z * 128] = top
             low[rows, 128 + z * 128 : 256 + z * 128] = (value - top.astype(F32)).astype(BF16)
@@ -149,17 +109,18 @@
     lax.fori_loop(0, CX, split, 0, unroll=2)
     for c in range(NZ // 256):
         window = slice(c * 256, c * 256 + 512)
-        both = jnp.concatenate([high[:, window], low[:, window]], axis=1)
-        out[:, c * 256 : c * 256 + 256] = jnp.dot(both, table[...], preferred_element_type=F32)
-
-
-def spread(ref, z_sum, x, t, z):
+        inside = slice(c * 256 + 128, c * 256 + 384)
+        wide = jnp.concatenate([high[:, window], low[:, window]], axis=1)
+        tall = jnp.concatenate([high[:, inside], low[:, inside]], axis=0)
+        twice = jnp.concatenate([xy_weights[...], xy_weights[...]], axis=1)
+        out[:, c * 256 : c * 256 + 256] = jnp.dot(wide, z_weights[...], preferred_element_type=F32) + jnp.dot(
+            twice, tall, preferred_element_type=F32
+        )
+
+
+def spread(ref, around, x, t, z):
     here = ref[strip(x, t, z), :]
-    total = CENTER * here + z_sum[pl.ds(pl.multiple_of(x * CY + t * 8, 8), 8), z * 128 : z * 128 + 128]
-    for k in range(1, 5):
-        flat = ref[strip(x, t, z, k), :] + ref[strip(x, t, z, -k), :]
-        deep = ref[strip(x, t, z, k * LAYER), :] + ref[strip(x, t, z, -k * LAYER), :]
-        total = total + WEIGHTS[k - 1] * (flat + deep)
+    total = CENTER * here + around[pl.ds(pl.multiple_of(x * CY + t * 8, 8), 8), z * 128 : z * 128 + 128]
     return here, total
 
 
@@ -196,9 +157,8 @@
 
 
 def inner_first(
-    cells, amps, wave, born, table, taps, weights, wave_old_in, born_old_in, courant_in, contrast_in,
-    wave_part, born_part, courant, contrast, picks, wave_next, born_next,
-    wave_old, born_old, high, low, wave_z, born_z, sems,
+    cells, amps, wave, born, z_weights, xy_weights, taps, weights, wave_old_in, born_old_in, courant_in, contrast_in,
+    wave_part, born_part, courant, contrast, picks, wave_old, born_old, high, low, wave_sum_all, born_sum_all, sems,
 ):
     copies = [
         pltpu.make_async_copy(a, b, sems.at[i])
@@ -208,10 +168,9 @@
     ]
     for copy in copies:
         copy.start()
-    along_z(wave, high, low, table, wave_z)
-    along_z(born, high, low, table, born_z)
+    stencil(wave, high, low, z_weights, xy_weights, wave_sum_all)
+    stencil(born, high, low, z_weights, xy_weights, born_sum_all)
     make_picks(taps, weights, picks)
-    clear(wave_next, born_next)
     for copy in copies:
         copy.wait()
 
@@ -220,10 +179,10 @@
             for t in range(2):
                 speed = tile(courant, x, t, z) * (1.0 / SCALE)
                 put(courant, x, t, z, speed)
-                here, total = spread(wave, wave_z, x, t, z)
+                here, total = spread(wave, wave_sum_all, x, t, z)
                 moved = speed * total
                 put(wave_part, x, t, z, (2.0 * here - tile(wave_old, x, t, z)) + moved)
-                here, total = spread(born, born_z, x, t, z)
+                here, total = spread(born, born_sum_all, x, t, z)
                 moved = speed * total + tile(contrast, x, t, z) * moved
                 put(born_part, x, t, z, (2.0 * here - tile(born_old, x, t, z)) + moved)
         return carry
@@ -233,8 +192,8 @@
 
 
 def inner_second(
-    cells, amps, rows_at, wave, born, table, wave_old, born_old, courant, contrast, picks, wave_now, born_now,
-    wave_part, born_part, first, wave_out, born_out, high, low, wave_z, born_z, rows, sems,
+    cells, amps, rows_at, wave, born, z_weights, xy_weights, wave_old, born_old, courant, contrast, picks, wave_now, born_now,
+    wave_part, born_part, first, wave_out, born_out, high, low, wave_sum_all, born_sum_all, rows, sems,
 ):
     copies = [
         pltpu.make_async_copy(wave_now, wave_out, sems.at[0]),
@@ -242,17 +201,17 @@
     ]
     for copy in copies:
         copy.start()
-    along_z(wave, high, low, table, wave_z)
-    along_z(born, high, low, table, born_z)
+    stencil(wave, high, low, z_weights, xy_weights, wave_sum_all)
+    stencil(born, high, low, z_weights, xy_weights, born_sum_all)
 
     def step(x, carry):
         for z in range(TZ):
             for t in range(2):
                 speed = tile(courant, x, t, z)
-                here, total = spread(wave, wave_z, x, t, z)
+                here, total = spread(wave, wave_sum_all, x, t, z)
                 moved = speed * total
                 put(wave_part, x, t, z, (2.0 * here - wave_old[strip(x, t, z), :]) + moved)
-                here, total = spread(born, born_z, x, t, z)
+                here, total = spread(born, born_sum_all, x, t, z)
                 moved = speed * total + tile(contrast, x, t, z) * moved
                 put(born_part, x, t, z, (2.0 * here - born_old[strip(x, t, z), :]) + moved)
         return carry
@@ -327,36 +286,24 @@
 
 
 def fix_edges(
-    place, ends, wave_part, born_part, courant, contrast, rxa, rxb, rya, ryb, rows_a, rows_b,
-    wave, born, wave_rows, born_rows, xa, xb,
+    place, ends, wave_part, born_part, courant, contrast, rxa, rxb, rya, ryb,
+    wave, born, wave_rows, born_rows, ya, yb, xa, xb,
 ):
     fix(
         place, ends, wave_part, born_part, courant, contrast, rxa, rxb, rya, ryb,
-        wave, born, wave_rows, born_rows, None, True, False,
+        wave, born, wave_rows, born_rows, (ya, yb), True, False,
     )
     pack_x(place[0] == 0, xa, xb, wave, born)
 
 
 def fix_middle(
-    place, ends, wave_part, born_part, courant, contrast, rya, ryb, wave_in, born_in, rows_a, rows_b,
+    place, ends, wave_part, born_part, courant, contrast, rya, ryb, wave_in, born_in, rows_a, rows_b, ya_in, yb_in,
     wave, born, wave_rows, born_rows, ya, yb,
 ):
     fix(
         place, ends, wave_part, born_part, courant, contrast, None, None, rya, ryb,
         wave, born, wave_rows, born_rows, (ya, yb), False, True,
     )
-    sub, _ = iotas()
-    even_y = place[1] == 0
-
-    def step(i, carry):
-        x = jnp.where(i < 4, i, i + CX - 8)
-        for z in range(TZ):
-            pack_y(
-                sub, even_y, ya, yb, x, z, tile(wave, x, 0, z), tile(wave, x, 1, z), tile(born, x, 0, z), tile(born, x, 1, z)
-            )
-        return carry
-
-    lax.fori_loop(0, 8, step, 0)
 
 
 def take(rows_at, grid, picks, rows, out):
@@ -457,6 +404,20 @@
     ryb = lax.ppermute(yb, "gy", pairs(16, 1))
     rya = lax.ppermute(ya, "gy", pairs(16, 0))
     return rya, ryb
+
+
+def xy_table():
+    size = CX * CY
+    row = lax.broadcasted_iota(jnp.int32, (size, size), 0)
+    col = lax.broadcasted_iota(jnp.int32, (size, size), 1)
+    apart = jnp.abs(row - col)
+    along_y = jnp.where(row // CY == col // CY, apart, 0)
+    along_x = jnp.where(apart % CY == 0, apart // CY, 0)
+    gap = jnp.maximum(along_x, along_y)
+    table = jnp.zeros((size, size), F32)
+    for k in range(1, 5):
+        table = jnp.where(gap == k, WEIGHTS[k - 1], table)
+    return table.astype(BF16)
 
 
 def z_table():
@@ -497,23 +458,23 @@
     )
     halo_x = swap_x(xa, xb)
     wave_rows, born_rows, ya, yb = call(
-        pack_kernel, (place, still(wave_now), still(born_now)), [SM, HB, HB],
-        [kept((ROWS, 128))] * 2 + y_faces, [field, field, pltpu.SemaphoreType.DMA((2, 4))], 10, 2,
+        pack_kernel, (place, wave_now, born_now), [SM, VM, VM],
+        [kept((ROWS, 128))] * 2 + y_faces, [], 8, 2,
     )
     halo_y = swap_y(ya, yb)
-    table = z_table()
-    wave_part, born_part, speed, factor, picks, wave_mid_rows, born_mid_rows = call(
+    tables = (z_table(), xy_table())
+    wave_part, born_part, speed, factor, picks = call(
         inner_first,
         (
-            src_cell, src_amp[:, 0], wave_rows, born_rows, table, rcv_cell.T, rcv_weight.T,
+            src_cell, src_amp[:, 0], wave_rows, born_rows, *tables, rcv_cell.T, rcv_weight.T,
             still(wave_old), still(born_old), still(courant), still(contrast),
         ),
-        [SM, SM] + [VM] * 5 + [HB] * 4,
-        [kept(BLOCK)] * 4 + [kept((2048, 128))] + [kept((ROWS, 128))] * 2, [field, field, *halves, pltpu.SemaphoreType.DMA((4,))], 14, 8,
+        [SM, SM] + [VM] * 6 + [HB] * 4,
+        [kept(BLOCK)] * 4 + [kept((2048, 128))], [field, field, *halves, pltpu.SemaphoreType.DMA((4,))], 14, 8,
     )
 
     cell = rcv_cell.T
-    rows_at = ((cell >> 14) + 4) * LAYER + ((cell >> 7) & 7) * STRIP + 8 + ((cell >> 10) & 15)
+    rows_at = (cell >> 14) * LAYER + ((cell >> 7) & 7) * STRIP + ((cell >> 10) & 15)
     dest = rcv_dest[:, 0]
     order = jnp.arange(256, dtype=jnp.int32)
     earlier = (dest[:, None] == dest[None, :]) & (order[None, :] < order[:, None])
@@ -523,22 +484,22 @@
 
     shared = (wave_part, born_part, speed, factor)
     *mid, xa, xb = call(
-        fix_edges, (place, ends, *shared, *halo_x, *halo_y, wave_mid_rows, born_mid_rows),
-        [SM] * 2 + [VM] * 10, fixed + x_faces, [], 4, 2, {10: 2, 11: 3},
+        fix_edges, (place, ends, *shared, *halo_x, *halo_y),
+        [SM] * 2 + [VM] * 8, fixed + y_faces + x_faces, [], 4, 2,
     )
     next_x = swap_x(xa, xb)
     wave_mid, born_mid, wave_mid_rows, born_mid_rows, ya, yb = call(
         fix_middle, (place, ends, *shared, *halo_y, *mid),
-        [SM] * 2 + [VM] * 10, fixed + y_faces, [], 4, 2, {8: 0, 9: 1, 10: 2, 11: 3},
+        [SM] * 2 + [VM] * 12, fixed + y_faces, [], 4, 2, {i + 8: i for i in range(6)},
     )
     next_y = swap_y(ya, yb)
     wave_part, born_part, first, wave_next, born_next = call(
         inner_second,
         (
-            src_cell, src_amp[:, 1], rows_at, wave_mid_rows, born_mid_rows, table, wave_rows, born_rows,
+            src_cell, src_amp[:, 1], rows_at, wave_mid_rows, born_mid_rows, *tables, wave_rows, born_rows,
             speed, factor, picks, wave_mid, born_mid,
         ),
-        [SM] * 3 + [VM] * 10,
+        [SM] * 3 + [VM] * 11,
         [kept(BLOCK)] * 2 + [plain((256, 128)), away(BLOCK), away(BLOCK)],
         [*halves, pltpu.VMEM((2048, 128), F32), pltpu.SemaphoreType.DMA((2,))], 12, 10,
     )

time: 91.3 us -> 87.2 us (0.955)
  Pallas kernels: 43.4 us -> 32.6 us
  blocking collectives: 32.2 us -> 37 us
  other arithmetic: 1.4 us -> 3.25 us
    pallas_call x7, Pallas kernels: 43.4 us -> 32.6 us  [call(): pl.pallas_call(kernel, out_shape=tuple((o[1] for o in outs)), in_specs=sp...]
    all_to_all x1, blocking collectives: 32.2 us -> 37 us  [steps(): lax.all_to_all(packed.reshape(128, 1, 128), ('gx', 'gy'), split_axis=0, c...]
    convert_element_type x0 -> x1, other arithmetic: none -> 1.84 us  [xy_table(): return table.astype(BF16)]
  transfers between devices with their start and end apart: 8 -> 8, of which waited for: 0 -> 0; matrix products, arithmetic and copies ran while one was open for 1% -> 4% of each run, Pallas kernels for 32% -> 23%
where the time goes in v5:
time: 87.2 us; the launch traced here: 87 us
  blocking collectives  37 us (42%)
  Pallas kernels  32.6 us (37%)
  starting transfers between devices  12.5 us (14%)
  other arithmetic  3.25 us (4%)
  between operations  0.92 us (1%)
    all_to_all x1, blocking collectives, steps(): lax.all_to_all(packed.reshape(128, 1, 128), ('gx', 'gy'), split_axis=0, c...  37 us
    pallas_call x7, Pallas kernels, call(): pl.pallas_call(kernel, out_shape=tuple((o[1] for o in outs)), in_specs=sp...  32.6 us
    ppermute x2, starting transfers between devices, swap_y(): ryb = lax.ppermute(yb, 'gy', pairs(16, 1))  7 us
    ppermute x2, starting transfers between devices, swap_x(): rxa = lax.ppermute(xa, 'gx', pairs(8, 0))  3.47 us
    ppermute x2, starting transfers between devices, swap_y(): rya = lax.ppermute(ya, 'gy', pairs(16, 0))  2.04 us
    convert_element_type x1, other arithmetic, xy_table(): return table.astype(BF16)  1.84 us
  transfers between devices with their start and end apart: 8, of which 0 were waited for; matrix products, arithmetic and copies ran while one was open for 4% of the time, Pallas kernels for 23%

profile of v5, /device:TPU:1, one launch (start us, length us, event | category | flops | bytes accessed | tf_op | source)
XLA Modules:
  0.0 87.0 jit_solution(8469866824351043309)
XLA Ops:
  0.6 0.1 add_convert_fusion.ends
  0.7 0.1 pad_add_fusion.place
  0.8 0.0 copy-start
  0.8 0.0 copy-start.1
  0.8 2.6 %shard_map.146 = (f32[8,16,1024]{2,1,0:T(8,128)S(1)}, f32[8,16,1024]{2,1,0:T(8,128)S(1)}, s32[2]{0:T(128)S(1)}, f32[2]{0:T(128)S(1)}) custom-call(s32[2]{0:T(128)S(1)} %pad_add_fusion.place, f32[2]{0:T(128)S(1)} %add_convert_fusion.ends, f32[32,16,1024]{2,1,0:T(8,128)} %wave.3, f32[32,16,1024]{2,1,0:T(8,128)} %born.3), custom_call_target="tpu_custom_call" | custom-call | bytes 3000000 | tf_op jit(solution)/shard_map/pallas_call | solution.py:383
  3.4 0.0 copy-done
  3.5 0.0 copy-done.1
  3.5 0.0 copy-start.6
  3.5 0.0 copy-start.2
  3.5 0.0 copy-start.4
  3.5 0.0 copy-start.5
  3.5 1.0 %shard_map.147 = (f32[4096,128]{1,0:T(8,128)S(1)}, f32[4096,128]{1,0:T(8,128)S(1)}, f32[32,8,1024]{2,1,0:T(8,128)S(1)}, f32[32,8,1024]{2,1,0:T(8,128)S(1)}) custom-call(s32[2]{0:T(128)S(1)} %get-tuple-element.40.place, f32[32,16,1024]{2,1,0:T(8,128)S(1)} %copy-done, f32[32,16,1024]{2,1,0:T(8,128)S(1)} %copy-done.1), custom_call_target="tpu_custom_call" | custom-call | bytes 6000000 | tf_op jit(solution)/shard_map/pallas_call | solution.py:383
  4.5 1.5 %collective-permute-start = (f32[32,8,1024]{2,1,0:T(8,128)S(1)}, f32[32,8,1024]{2,1,0:T(8,128)S(1)}, u32[]{:S(2)}, u32[]{:S(2)}) collective-permute-start(f32[32,8,1024]{2,1,0:T(8,128)S(1)} %get-tuple-element.48), channel_id=1, source_target_pairs={{0,1},{1,0},{2,3},{3,2},{4,5},{5,4},{6,7},{7,6},{8,9},{9,8},{10,11... | collective-permute-start | bytes 3145736 | tf_op jit(solution)/shard_map/ppermute | solution.py:405
  6.0 3.6 %collective-permute-start.1 = (f32[32,8,1024]{2,1,0:T(8,128)S(1)}, f32[32,8,1024]{2,1,0:T(8,128)S(1)}, u32[]{:S(2)}, u32[]{:S(2)}) collective-permute-start(f32[32,8,1024]{2,1,0:T(8,128)S(1)} %get-tuple-element.49), channel_id=1, source_target_pairs={{1,2},{2,1},{3,4},{4,3},{5,6},{6,5},{7,8},{8,7},{9,10},{10,9},{11,... | collective-permute-start | bytes 3145736 | tf_op jit(solution)/shard_map/ppermute | solution.py:404
  9.6 1.3 %collective-permute-start.2 = (f32[8,16,1024]{2,1,0:T(8,128)S(1)}, f32[8,16,1024]{2,1,0:T(8,128)S(1)}, u32[]{:S(2)}, u32[]{:S(2)}) collective-permute-start(f32[8,16,1024]{2,1,0:T(8,128)S(1)} %get-tuple-element.50), channel_id=1, source_target_pairs={{0,16},{16,0},{32,48},{48,32},{64,80},{80,64},{96,112},{112,96},{1... | collective-permute-start | bytes 1572872 | tf_op jit(solution)/shard_map/ppermute | solution.py:399
  10.9 0.0 collective-permute-start.3
  10.9 0.0 copy-done.6
  10.9 0.9 %select_convert_fusion.1.z_weights = bf16[1024,256]{1,0:T(8,128)(2,1)S(1)} fusion(s32[1024]{0:T(1024)S(1)} %get-tuple-element.82, s32[1024]{0:T(1024)S(1)} %get-tuple-element.83, pred[1024]{0:T(1024)(128)(4,1)S(1)} %fusion.18), kind=kLoop, calls=%fused_computation.15 | loop fusion | flops 3407872 | bytes 533504 | tf_op jit(solution)/shard_map/convert_element_type | solution.py:430
  11.9 1.8 %select_convert_fusion.xy_weights = bf16[512,512]{1,0:T(8,128)(2,1)S(1)} fusion(s32[512]{0:T(512)S(1)} %get-tuple-element.84, s32[512]{0:T(512)S(1)} %get-tuple-element.85, pred[512]{0:T(512)(128)(4,1)S(1)} %fusion.21), kind=kLoop, calls=%fused_computation.8 | loop fusion | flops 9699328 | bytes 528896 | tf_op jit(solution)/shard_map/convert_element_type | solution.py:420
  13.7 0.0 copy-done.2
  13.7 0.0 copy-done.4
  13.7 0.0 copy-done.5
  13.7 9.3 %shard_map.148 = (f32[32,16,1024]{2,1,0:T(8,128)S(1)}, f32[32,16,1024]{2,1,0:T(8,128)S(1)}, f32[32,16,1024]{2,1,0:T(8,128)S(1)}, f32[32,16,1024]{2,1,0:T(8,128)S(1)}, f32[2048,128]{1,0:T(8,128)S(1)}) custom-call(s32[4]{0:T(128)S(1)} %copy-done.5, f32[4]{0:T(128)S(1)} %get-tuple-element.80.amps, f32[4096,128]{1,0:T(8,128)S(1)} %get-tuple-element.42.wave.wave_old, ...), custom_call_target="tpu_custom_call" | custom-call | bytes 24000000 | tf_op jit(solution)/shard_map/pallas_call | solution.py:383
  23.0 0.0 collective-permute-done.2.rxa
  23.0 0.0 collective-permute-done.3.rxb
  23.0 0.0 collective-permute-done.rya
  23.1 0.0 collective-permute-done.1.ryb
  23.1 1.4 %shard_map.149 = (f32[32,16,1024]{2,1,0:T(8,128)S(1)}, f32[32,16,1024]{2,1,0:T(8,128)S(1)}, f32[4096,128]{1,0:T(8,128)S(1)}, f32[4096,128]{1,0:T(8,128)S(1)}, f3...) custom-call(s32[2]{0:T(128)S(1)} %get-tuple-element.40.place, ...), custom_call_target="tpu_custom_call" | custom-call | bytes 6000000 | tf_op jit(solution)/shard_map/pallas_call | solution.py:383
  24.5 0.0 copy-start.3
  24.5 2.0 %shard_map.150 = (f32[32,16,1024]{2,1,0:T(8,128)S(1)}, f32[32,16,1024]{2,1,0:T(8,128)S(1)}, f32[4096,128]{1,0:T(8,128)S(1)}, f32[4096,128]{1,0:T(8,128)S(1)}, f3...) custom-call(s32[2]{0:T(128)S(1)} %get-tuple-element.40.place, ...), custom_call_target="tpu_custom_call", output_to_operand_aliasing={{0}: (8, {}), {1}: (9, {}), {2}: (10, {}), {3}: (11, {}), {... | custom-call | bytes 6000000 | tf_op jit(solution)/shard_map/pallas_call | solution.py:383
  26.5 0.6 collective-permute-start.6
  27.0 3.4 %collective-permute-start.7 = (f32[32,8,1024]{2,1,0:T(8,128)S(1)}, f32[32,8,1024]{2,1,0:T(8,128)S(1)}, u32[]{:S(2)}, u32[]{:S(2)}) collective-permute-start(f32[32,8,1024]{2,1,0:T(8,128)S(1)} %get-tuple-element.69), channel_id=1, source_target_pairs={{1,2},{2,1},{3,4},{4,3},{5,6},{6,5},{7,8},{8,7},{9,10},{10,9},{11,... | collective-permute-start | bytes 3145736 | tf_op jit(solution)/shard_map/ppermute | solution.py:404
  30.5 0.0 copy-done.3
  30.5 0.2 convert_reduce_fusion
  30.7 2.2 %collective-permute-start.4 = (f32[8,16,1024]{2,1,0:T(8,128)S(1)}, f32[8,16,1024]{2,1,0:T(8,128)S(1)}, u32[]{:S(2)}, u32[]{:S(2)}) collective-permute-start(f32[8,16,1024]{2,1,0:T(8,128)S(1)} %get-tuple-element.66), channel_id=1, source_target_pairs={{0,16},{16,0},{32,48},{48,32},{64,80},{80,64},{96,112},{112,96},{1... | collective-permute-start | bytes 1572872 | tf_op jit(solution)/shard_map/ppermute | solution.py:399
  32.9 0.0 collective-permute-start.5
  32.9 0.1 fusion.14.slots
  33.0 10.4 %shard_map.151 = (f32[32,16,1024]{2,1,0:T(8,128)S(1)}, f32[32,16,1024]{2,1,0:T(8,128)S(1)}, f32[256,128]{1,0:T(8,128)S(1)}, f32[32,16,1024]{2,1,0:T(8,128)}, f32[32,16,1024]{2,1,0:T(8,128)}) custom-call(s32[4]{0:T(128)S(1)} %copy-done.5, f32[4]{0:T(128)S(1)} %get-tuple-element.81.amps, s32[8,256]{1,0:T(8,128)S(1)} %and_add_fusion.rows_at, ...), custom_call_target="tpu_custom_call" | custom-call | bytes 30000000 | tf_op jit(solution)/shard_map/pallas_call | solution.py:383
  43.4 0.0 collective-permute-done.4.rxa
  43.5 0.0 collective-permute-done.5.rxb
  43.5 0.0 collective-permute-done.6.rya
  43.5 0.0 collective-permute-done.7.ryb
  43.5 5.8 %shard_map.152 = (f32[32,16,1024]{2,1,0:T(8,128)}, f32[32,16,1024]{2,1,0:T(8,128)}, f32[128,128]{1,0:T(8,128)S(1)}) custom-call(s32[2]{0:T(128)S(1)} %get-tuple-element.40.place, f32[2]{0:T(128)S(1)} %get-tuple-element.41.ends, s32[8,256]{1,0:T(8,128)S(1)} %and_add_fusion.rows_at, f32[32,16,1024]{2,1,0:T(8,128)S(1)} %get-tuple-element.64.wave_part, ...), custom_call_target="tpu_custom_call" | custom-call | bytes 15000000 | tf_op jit(solution)/shard_map/pallas_call | solution.py:383
  49.3 37.0 %all_to_all.5 = f32[128,1,128]{2,1,0:T(1,128)S(1)} all-to-all(f32[128,1,128]{2,1,0:T(1,128)S(1)} %bitcast.18), channel_id=1, replica_groups=mesh['gx'=8,'gy'=16] {'gx','gy'}, dimensions={0} | all-to-all | bytes 131072 | tf_op jit(solution)/shard_map/all_to_all | solution.py:516
  86.3 0.7 copy.28
  (8 shorter events, 0.0 us)
Async XLA Ops:
  0.8 2.7 %copy-start = (f32[32,16,1024]{2,1,0:T(8,128)S(1)}, f32[32,16,1024]{2,1,0:T(8,128)}, u32[]{:S(2)}) copy-start(f32[32,16,1024]{2,1,0:T(8,128)} %wave.3) | copy-start | bytes 6291460
  0.8 2.7 %copy-start.1 = (f32[32,16,1024]{2,1,0:T(8,128)S(1)}, f32[32,16,1024]{2,1,0:T(8,128)}, u32[]{:S(2)}) copy-start(f32[32,16,1024]{2,1,0:T(8,128)} %born.3) | copy-start | bytes 6291460
  3.5 7.4 %copy-start.6 = (f32[4,2]{0,1:T(2,128)S(1)}, f32[4,2]{0,1:T(2,128)}, u32[]{:S(2)}) copy-start(f32[4,2]{0,1:T(2,128)} %param.18) | copy-start | bytes 100
  3.5 10.2 %copy-start.2 = (s32[256,8]{0,1:T(8,128)S(1)}, s32[256,8]{0,1:T(8,128)}, u32[]{:S(2)}) copy-start(s32[256,8]{0,1:T(8,128)} %param.19) | copy-start | bytes 24580
  3.5 10.2 %copy-start.4 = (f32[256,8]{0,1:T(8,128)S(1)}, f32[256,8]{0,1:T(8,128)}, u32[]{:S(2)}) copy-start(f32[256,8]{0,1:T(8,128)} %param.20) | copy-start | bytes 24580
  3.5 10.2 %copy-start.5 = (s32[4]{0:T(128)S(1)}, s32[4]{0:T(128)}, u32[]{:S(2)}) copy-start(s32[4]{0:T(128)} %cells.3) | copy-start | bytes 52
  4.5 18.5 %collective-permute-start = (f32[32,8,1024]{2,1,0:T(8,128)S(1)}, f32[32,8,1024]{2,1,0:T(8,128)S(1)}, u32[]{:S(2)}, u32[]{:S(2)}) collective-permute-start(f32[32,8,1024]{2,1,0:T(8,128)S(1)} %get-tuple-element.48), channel_id=1, source_target_pairs={{0,1},{1,0},{2,3},{3,2},{4,5},{5,4},{6,7},{7,6},{8,9},{9,8},{10,11... | collective-permute-start | bytes 3145736 | tf_op jit(solution)/shard_map/ppermute | solution.py:405
  6.0 17.1 %collective-permute-start.1 = (f32[32,8,1024]{2,1,0:T(8,128)S(1)}, f32[32,8,1024]{2,1,0:T(8,128)S(1)}, u32[]{:S(2)}, u32[]{:S(2)}) collective-permute-start(f32[32,8,1024]{2,1,0:T(8,128)S(1)} %get-tuple-element.49), channel_id=1, source_target_pairs={{1,2},{2,1},{3,4},{4,3},{5,6},{6,5},{7,8},{8,7},{9,10},{10,9},{11,... | collective-permute-start | bytes 3145736 | tf_op jit(solution)/shard_map/ppermute | solution.py:404
  9.6 13.5 %collective-permute-start.2 = (f32[8,16,1024]{2,1,0:T(8,128)S(1)}, f32[8,16,1024]{2,1,0:T(8,128)S(1)}, u32[]{:S(2)}, u32[]{:S(2)}) collective-permute-start(f32[8,16,1024]{2,1,0:T(8,128)S(1)} %get-tuple-element.50), channel_id=1, source_target_pairs={{0,16},{16,0},{32,48},{48,32},{64,80},{80,64},{96,112},{112,96},{1... | collective-permute-start | bytes 1572872 | tf_op jit(solution)/shard_map/ppermute | solution.py:399
  10.9 12.2 %collective-permute-start.3 = (f32[8,16,1024]{2,1,0:T(8,128)S(1)}, f32[8,16,1024]{2,1,0:T(8,128)S(1)}, u32[]{:S(2)}, u32[]{:S(2)}) collective-permute-start(f32[8,16,1024]{2,1,0:T(8,128)S(1)} %get-tuple-element.51), channel_id=1, source_target_pairs={{16,32},{17,33},{18,34},{19,35},{20,36},{21,37},{22,38},{23,39},{2... | collective-permute-start | bytes 1572872 | tf_op jit(solution)/shard_map/ppermute | solution.py:398
  24.5 6.0 %copy-start.3 = (s32[256,1]{0,1:T(1,128)S(1)}, s32[256,1]{0,1:T(1,128)}, u32[]{:S(2)}) copy-start(s32[256,1]{0,1:T(1,128)} %param.21) | copy-start | bytes 3076
  26.5 17.0 %collective-permute-start.6 = (f32[32,8,1024]{2,1,0:T(8,128)S(1)}, f32[32,8,1024]{2,1,0:T(8,128)S(1)}, u32[]{:S(2)}, u32[]{:S(2)}) collective-permute-start(f32[32,8,1024]{2,1,0:T(8,128)S(1)} %get-tuple-element.68), channel_id=1, source_target_pairs={{0,1},{1,0},{2,3},{3,2},{4,5},{5,4},{6,7},{7,6},{8,9},{9,8},{10,11... | collective-permute-start | bytes 3145736 | tf_op jit(solution)/shard_map/ppermute | solution.py:405
  27.0 16.4 %collective-permute-start.7 = (f32[32,8,1024]{2,1,0:T(8,128)S(1)}, f32[32,8,1024]{2,1,0:T(8,128)S(1)}, u32[]{:S(2)}, u32[]{:S(2)}) collective-permute-start(f32[32,8,1024]{2,1,0:T(8,128)S(1)} %get-tuple-element.69), channel_id=1, source_target_pairs={{1,2},{2,1},{3,4},{4,3},{5,6},{6,5},{7,8},{8,7},{9,10},{10,9},{11,... | collective-permute-start | bytes 3145736 | tf_op jit(solution)/shard_map/ppermute | solution.py:404
  30.7 12.8 %collective-permute-start.4 = (f32[8,16,1024]{2,1,0:T(8,128)S(1)}, f32[8,16,1024]{2,1,0:T(8,128)S(1)}, u32[]{:S(2)}, u32[]{:S(2)}) collective-permute-start(f32[8,16,1024]{2,1,0:T(8,128)S(1)} %get-tuple-element.66), channel_id=1, source_target_pairs={{0,16},{16,0},{32,48},{48,32},{64,80},{80,64},{96,112},{112,96},{1... | collective-permute-start | bytes 1572872 | tf_op jit(solution)/shard_map/ppermute | solution.py:399
  32.9 10.6 %collective-permute-start.5 = (f32[8,16,1024]{2,1,0:T(8,128)S(1)}, f32[8,16,1024]{2,1,0:T(8,128)S(1)}, u32[]{:S(2)}, u32[]{:S(2)}) collective-permute-start(f32[8,16,1024]{2,1,0:T(8,128)S(1)} %get-tuple-element.67), channel_id=1, source_target_pairs={{16,32},{17,33},{18,34},{19,35},{20,36},{21,37},{22,38},{23,39},{2... | collective-permute-start | bytes 1572872 | tf_op jit(solution)/shard_map/ppermute | solution.py:398

commit v6 on v5

--- a/solution.py
+++ b/solution.py
@@ -192,8 +192,8 @@
 
 
 def inner_second(
-    cells, amps, rows_at, wave, born, z_weights, xy_weights, wave_old, born_old, courant, contrast, picks, wave_now, born_now,
-    wave_part, born_part, first, wave_out, born_out, high, low, wave_sum_all, born_sum_all, rows, sems,
+    cells, amps, rows_at, wave, born, z_weights, xy_weights, wave_old, born_old, courant, contrast, picks, slots, wave_now, born_now,
+    wave_part, born_part, first, wave_out, born_out, high, low, wave_sum_all, born_sum_all, rows, sums, sems,
 ):
     copies = [
         pltpu.make_async_copy(wave_now, wave_out, sems.at[0]),
@@ -218,54 +218,60 @@
 
     lax.fori_loop(0, CX, step, 0)
     add_sources(cells, amps, contrast, wave_part, born_part)
-    take(rows_at, born, picks, rows, first)
+    take(rows_at, born, picks, rows, sums)
+    lane = lax.broadcasted_iota(jnp.int32, (256, 128), 1)
+    first[...] = jnp.where(lane < 4, jnp.sum(sums[...], axis=1, keepdims=True), 0.0) * slots[...]
     for copy in copies:
         copy.wait()
 
 
-def fix(
-    place, ends, wave_part, born_part, courant, contrast, xa, xb, ya, yb, wave, born, wave_rows, born_rows, y_faces,
-    edges, middle,
-):
+def fix(place, ends, parts, scales, x_halo, y_halo, outs, y_faces, edges, middle, tiles=(0, 1)):
+    wave_part, born_part = parts
+    courant, contrast = scales
+    wave, born, wave_rows, born_rows = outs
     sub, _ = iotas()
     even_x = place[0] == 0
     even_y = place[1] == 0
     part = lax.bitwise_and(sub, 3)
+
     low_weights = [jnp.where(part < k, WEIGHTS[k - 1], 0.0) for k in range(1, 4)]
     high_weights = [jnp.where(part >= 4 - k, WEIGHTS[k - 1], 0.0) for k in range(1, 4)]
 
     def one(x, side, offset):
         for z in range(TZ):
-            from_a, from_b = tile(ya, x, 0, z), tile(yb, x, 0, z)
-            low = jnp.where(even_y, from_b, from_a)
-            high = jnp.where(even_y, from_a, from_b)
-            low_sum, high_sum = WEIGHTS[3] * low, WEIGHTS[3] * high
-            for k in range(1, 4):
-                low_sum = low_sum + low_weights[k - 1] * pltpu.roll(low, 4 + k, 0)
-                high_sum = high_sum + high_weights[k - 1] * pltpu.roll(high, 4 - k, 0)
-            wave_sums = [
-                jnp.where(sub < 4, low_sum, 0.0),
-                jnp.where(sub < 4, 0.0, pltpu.roll(high_sum, 4, 0)),
-            ]
-            born_sums = [
-                jnp.where(sub < 4, pltpu.roll(low_sum, 4, 0), 0.0),
-                jnp.where(sub < 4, 0.0, high_sum),
-            ]
+            low, high = y_halo(x, z)
+            wave_sums, born_sums = [None, None], [None, None]
+            if low is not None:
+                total = WEIGHTS[3] * low
+                for k in range(1, 4):
+                    total = total + low_weights[k - 1] * pltpu.roll(low, 4 + k, 0)
+                wave_sums[0] = jnp.where(sub < 4, total, 0.0)
+                born_sums[0] = jnp.where(sub < 4, pltpu.roll(total, 4, 0), 0.0)
+            if high is not None:
+                total = WEIGHTS[3] * high
+                for k in range(1, 4):
+                    total = total + high_weights[k - 1] * pltpu.roll(high, 4 - k, 0)
+                wave_sums[1] = jnp.where(sub < 4, 0.0, pltpu.roll(total, 4, 0))
+                born_sums[1] = jnp.where(sub < 4, 0.0, total)
             finals = []
-            for t in range(2):
+            for t in tiles:
                 wave_sum, born_sum = wave_sums[t], born_sums[t]
                 if side:
                     for m in range(4):
                         reach = offset + 4 - m if side < 0 else 4 - offset + m
                         if 1 <= reach <= 4:
-                            lone, other = (xb, xa) if side < 0 else (xa, xb)
+                            lone, other = (x_halo[1], x_halo[0]) if side < 0 else x_halo
                             w = WEIGHTS[reach - 1] * ends[0 if side < 0 else 1]
-                            wave_sum = wave_sum + w * jnp.where(even_x, tile(lone, m, t, z), tile(other, m, t, z))
-                            born_sum = born_sum + w * jnp.where(even_x, tile(lone, m + 4, t, z), tile(other, m + 4, t, z))
-                speed = tile(courant, x, t, z)
-                moved = speed * wave_sum
-                wave_value = tile(wave_part, x, t, z) + moved
-                born_value = tile(born_part, x, t, z) + (tile(contrast, x, t, z) * moved + speed * born_sum)
+                            wave_term = w * jnp.where(even_x, tile(lone, m, t, z), tile(other, m, t, z))
+                            born_term = w * jnp.where(even_x, tile(lone, m + 4, t, z), tile(other, m + 4, t, z))
+                            wave_sum = wave_term if wave_sum is None else wave_sum + wave_term
+                            born_sum = born_term if born_sum is None else born_sum + born_term
+                wave_value, born_value = tile(wave_part, x, t, z), tile(born_part, x, t, z)
+                if wave_sum is not None:
+                    speed = tile(courant, x, t, z)
+                    moved = speed * wave_sum
+                    wave_value = wave_value + moved
+                    born_value = born_value + (tile(contrast, x, t, z) * moved + speed * born_sum)
                 put(wave, x, t, z, wave_value)
                 put(born, x, t, z, born_value)
                 if wave_rows is not None:
@@ -282,7 +288,26 @@
         for x in range(CX - 4, CX):
             one(x, 1, x - (CX - 4))
     if middle:
-        lax.fori_loop(4, CX - 4, lambda x, carry: (one(x, 0, 0), carry)[1], 0)
+        first, end = middle
+        lax.fori_loop(first, end, lambda x, carry: (one(x, 0, 0), carry)[1], 0)
+
+
+def both_sides(place, ya, yb):
+    even_y = place[1] == 0
+
+    def pick(x, z):
+        from_a, from_b = tile(ya, x, 0, z), tile(yb, x, 0, z)
+        return jnp.where(even_y, from_b, from_a), jnp.where(even_y, from_a, from_b)
+
+    return pick
+
+
+def low_side(face):
+    return lambda x, z: (tile(face, x, 0, z), None)
+
+
+def high_side(face):
+    return lambda x, z: (None, tile(face, x, 0, z))
 
 
 def fix_edges(
@@ -290,8 +315,8 @@
     wave, born, wave_rows, born_rows, ya, yb, xa, xb,
 ):
     fix(
-        place, ends, wave_part, born_part, courant, contrast, rxa, rxb, rya, ryb,
-        wave, born, wave_rows, born_rows, (ya, yb), True, False,
+        place, ends, (wave_part, born_part), (courant, contrast), (rxa, rxb), both_sides(place, rya, ryb),
+        (wave, born, wave_rows, born_rows), (ya, yb), True, None,
     )
     pack_x(place[0] == 0, xa, xb, wave, born)
 
@@ -301,20 +326,35 @@
     wave, born, wave_rows, born_rows, ya, yb,
 ):
     fix(
-        place, ends, wave_part, born_part, courant, contrast, None, None, rya, ryb,
-        wave, born, wave_rows, born_rows, (ya, yb), False, True,
-    )
+        place, ends, (wave_part, born_part), (courant, contrast), None, both_sides(place, rya, ryb),
+        (wave, born, wave_rows, born_rows), (ya, yb), False, (4, CX - 4),
+    )
+
+
+def fix_early(
+    place, ends, wave_part, born_part, courant, contrast, rxa, rxb, rya, wave, born, born_rows,
+):
+    for even in (True, False):
+
+        @pl.when((place[1] == 0) == even)
+        def _():
+            fix(
+                place, ends, (wave_part, born_part), (courant, contrast), (rxa, rxb),
+                high_side(rya) if even else low_side(rya),
+                (wave, born, None, born_rows), None, True, (4, CX - 4),
+            )
 
 
 def take(rows_at, grid, picks, rows, out):
     def step(g, carry):
-        for j in range(8):
-            r = g * 8 + j
-            for t in range(8):
-                rows[pl.ds(r * 8 + t, 1), :] = grid[pl.ds(rows_at[t, r], 1), :]
+        for half in range(2):
+            for j in range(8):
+                for t in range(8):
+                    source = rows_at[g * 8 + (half * 1024 + t * 128 + j)]
+                    rows[pl.ds(g * 64 + (half * 1024 + j * 8 + t), 1), :] = grid[pl.ds(source, 1), :]
         return carry
 
-    lax.fori_loop(0, 32, step, 0)
+    lax.fori_loop(0, 16, step, 0)
 
     def total(g, carry):
         part = pl.ds(pl.multiple_of(g * 256, 256), 256)
@@ -326,13 +366,19 @@
 
 
 def last_kernel(
-    place, ends, rows_at, wave_part, born_part, courant, contrast, rxa, rxb, rya, ryb,
-    picks, first, slots, dest, wave_out, born_out, packed, wave, born, grid, rows, sums, sems,
-):
-    fix(
-        place, ends, wave_part, born_part, courant, contrast, rxa, rxb, rya, ryb,
-        wave, born, None, grid, None, True, True,
-    )
+    place, rows_at, wave_in, born_in, grid_in, courant, contrast, ryb, picks, first, slots, dest,
+    wave, born, grid, wave_out, born_out, packed, rows, sums, sems,
+):
+    for even in (True, False):
+
+        @pl.when((place[1] == 0) == even)
+        def _():
+            fix(
+                place, None, (wave_in, born_in), (courant, contrast), None,
+                low_side(ryb) if even else high_side(ryb),
+                (wave, born, None, grid), None, False, (0, CX), (0,) if even else (1,),
+            )
+
     copies = [
         pltpu.make_async_copy(wave, wave_out, sems.at[0]),
         pltpu.make_async_copy(born, born_out, sems.at[1]),
@@ -340,10 +386,9 @@
     for copy in copies:
         copy.start()
     take(rows_at, grid, picks, rows, sums)
-    one = jnp.sum(first[...], axis=1, keepdims=True)
     two = jnp.sum(sums[...], axis=1, keepdims=True)
     lane = lax.broadcasted_iota(jnp.int32, (256, 128), 1)
-    spread_out = jnp.where(lane < 4, one, two) * slots[...]
+    spread_out = first[...] + jnp.where(lane < 4, 0.0, two) * slots[...]
     owner = lax.broadcasted_iota(jnp.int32, (128, 256), 0)
     chosen = jnp.where(owner == dest[...], 1.0, 0.0).astype(F32)
     packed[...] = jnp.dot(chosen, spread_out, precision=lax.Precision.HIGHEST, preferred_element_type=F32)
@@ -475,6 +520,7 @@
 
     cell = rcv_cell.T
     rows_at = (cell >> 14) * LAYER + ((cell >> 7) & 7) * STRIP + ((cell >> 10) & 15)
+    rows_at = rows_at.reshape(8, 2, 128).transpose(1, 0, 2).reshape(2048)
     dest = rcv_dest[:, 0]
     order = jnp.arange(256, dtype=jnp.int32)
     earlier = (dest[:, None] == dest[None, :]) & (order[None, :] < order[:, None])
@@ -497,21 +543,23 @@
         inner_second,
         (
             src_cell, src_amp[:, 1], rows_at, wave_mid_rows, born_mid_rows, *tables, wave_rows, born_rows,
-            speed, factor, picks, wave_mid, born_mid,
+            speed, factor, picks, slots, wave_mid, born_mid,
         ),
-        [SM] * 3 + [VM] * 11,
+        [SM] * 3 + [VM] * 12,
         [kept(BLOCK)] * 2 + [plain((256, 128)), away(BLOCK), away(BLOCK)],
-        [*halves, pltpu.VMEM((2048, 128), F32), pltpu.SemaphoreType.DMA((2,))], 12, 10,
-    )
-    wave_last, born_last, packed = call(
+        [*halves, pltpu.VMEM((2048, 128), F32), pltpu.VMEM((256, 128), F32), pltpu.SemaphoreType.DMA((2,))], 12, 10,
+    )
+    near = call(
+        fix_early, (place, ends, wave_part, born_part, speed, factor, *next_x, next_y[0]),
+        [SM] * 2 + [VM] * 7, [kept(BLOCK)] * 2 + [kept((ROWS, 128))], [], 4, 3, {2: 0, 3: 1},
+    )
+    *_, wave_last, born_last, packed = call(
         last_kernel,
-        (place, ends, rows_at, wave_part, born_part, speed, factor, *next_x, *next_y, picks, first, slots, dest[None, :]),
-        [SM] * 3 + [VM] * 12,
-        [away(BLOCK), away(BLOCK), plain((128, 128))],
-        [
-            field, field, pltpu.VMEM((ROWS, 128), F32), pltpu.VMEM((2048, 128), F32),
-            pltpu.VMEM((256, 128), F32), pltpu.SemaphoreType.DMA((2,)),
-        ], 16, 5,
+        (place, rows_at, *near, speed, factor, next_y[1], picks, first, slots, dest[None, :]),
+        [SM] * 2 + [VM] * 10,
+        [kept(BLOCK)] * 2 + [kept((ROWS, 128)), away(BLOCK), away(BLOCK), plain((128, 128))],
+        [pltpu.VMEM((2048, 128), F32), pltpu.VMEM((256, 128), F32), pltpu.SemaphoreType.DMA((2,))],
+        8, 4, {2: 0, 3: 1, 4: 2},
     )
     arrived = lax.all_to_all(
         packed.reshape(128, 1, 128), ("gx", "gy"), split_axis=0, concat_axis=0, tiled=True

time: 87.2 us -> 85.7 us (0.983)
  blocking collectives: 37 us -> 34.8 us
    all_to_all x1, blocking collectives: 37 us -> 34.8 us  [steps(): lax.all_to_all(packed.reshape(128, 1, 128), ('gx', 'gy'), split_axis=0, c...]
    pallas_call x7 -> x8, Pallas kernels: 32.6 us -> 33.3 us  [call(): pl.pallas_call(kernel, out_shape=tuple((o[1] for o in outs)), in_specs=sp...]
  transfers between devices with their start and end apart: 8 -> 8, of which waited for: 0 -> 0; matrix products, arithmetic and copies ran while one was open for 4% -> 4% of each run, Pallas kernels for 23% -> 25%
where the time goes in v6:
time: 85.7 us; the launch traced here: 85.5 us
  blocking collectives  34.8 us (41%)
  Pallas kernels  33.3 us (39%)
  starting transfers between devices  12.5 us (15%)
  other arithmetic  3.25 us (4%)
  between operations  0.92 us (1%)
    all_to_all x1, blocking collectives, steps(): lax.all_to_all(packed.reshape(128, 1, 128), ('gx', 'gy'), split_axis=0, c...  34.8 us
    pallas_call x8, Pallas kernels, call(): pl.pallas_call(kernel, out_shape=tuple((o[1] for o in outs)), in_specs=sp...  33.3 us
    ppermute x2, starting transfers between devices, swap_y(): ryb = lax.ppermute(yb, 'gy', pairs(16, 1))  7 us
    ppermute x2, starting transfers between devices, swap_x(): rxa = lax.ppermute(xa, 'gx', pairs(8, 0))  3.47 us
    ppermute x2, starting transfers between devices, swap_y(): rya = lax.ppermute(ya, 'gy', pairs(16, 0))  2.04 us
    convert_element_type x1, other arithmetic, xy_table(): return table.astype(BF16)  1.84 us
  transfers between devices with their start and end apart: 8, of which 0 were waited for; matrix products, arithmetic and copies ran while one was open for 4% of the time, Pallas kernels for 25%

profile of v6, /device:TPU:1, one launch (start us, length us, event | category | flops | bytes accessed | tf_op | source)
XLA Modules:
  0.0 85.5 jit_solution(100601141195942987)
XLA Ops:
  0.6 0.1 add_convert_fusion.ends
  0.7 0.1 pad_add_fusion.place
  0.8 0.0 copy-start
  0.8 0.0 copy-start.1
  0.8 2.6 %shard_map.146 = (f32[8,16,1024]{2,1,0:T(8,128)S(1)}, f32[8,16,1024]{2,1,0:T(8,128)S(1)}, s32[2]{0:T(128)S(1)}, f32[2]{0:T(128)S(1)}) custom-call(s32[2]{0:T(128)S(1)} %pad_add_fusion.place, f32[2]{0:T(128)S(1)} %add_convert_fusion.ends, f32[32,16,1024]{2,1,0:T(8,128)} %wave.3, f32[32,16,1024]{2,1,0:T(8,128)} %born.3), custom_call_target="tpu_custom_call" | custom-call | bytes 3000000 | tf_op jit(solution)/shard_map/pallas_call | solution.py:428
  3.4 0.0 copy-done
  3.5 0.0 copy-done.1
  3.5 0.0 copy-start.6
  3.5 0.0 copy-start.2
  3.5 0.0 copy-start.4
  3.5 0.0 copy-start.5
  3.5 1.0 %shard_map.147 = (f32[4096,128]{1,0:T(8,128)S(1)}, f32[4096,128]{1,0:T(8,128)S(1)}, f32[32,8,1024]{2,1,0:T(8,128)S(1)}, f32[32,8,1024]{2,1,0:T(8,128)S(1)}) custom-call(s32[2]{0:T(128)S(1)} %get-tuple-element.43.place, f32[32,16,1024]{2,1,0:T(8,128)S(1)} %copy-done, f32[32,16,1024]{2,1,0:T(8,128)S(1)} %copy-done.1), custom_call_target="tpu_custom_call" | custom-call | bytes 6000000 | tf_op jit(solution)/shard_map/pallas_call | solution.py:428
  4.5 1.5 %collective-permute-start = (f32[32,8,1024]{2,1,0:T(8,128)S(1)}, f32[32,8,1024]{2,1,0:T(8,128)S(1)}, u32[]{:S(2)}, u32[]{:S(2)}) collective-permute-start(f32[32,8,1024]{2,1,0:T(8,128)S(1)} %get-tuple-element.51), channel_id=1, source_target_pairs={{0,1},{1,0},{2,3},{3,2},{4,5},{5,4},{6,7},{7,6},{8,9},{9,8},{10,11... | collective-permute-start | bytes 3145736 | tf_op jit(solution)/shard_map/ppermute | solution.py:450
  6.0 3.6 %collective-permute-start.1 = (f32[32,8,1024]{2,1,0:T(8,128)S(1)}, f32[32,8,1024]{2,1,0:T(8,128)S(1)}, u32[]{:S(2)}, u32[]{:S(2)}) collective-permute-start(f32[32,8,1024]{2,1,0:T(8,128)S(1)} %get-tuple-element.52), channel_id=1, source_target_pairs={{1,2},{2,1},{3,4},{4,3},{5,6},{6,5},{7,8},{8,7},{9,10},{10,9},{11,... | collective-permute-start | bytes 3145736 | tf_op jit(solution)/shard_map/ppermute | solution.py:449
  9.6 1.3 %collective-permute-start.2 = (f32[8,16,1024]{2,1,0:T(8,128)S(1)}, f32[8,16,1024]{2,1,0:T(8,128)S(1)}, u32[]{:S(2)}, u32[]{:S(2)}) collective-permute-start(f32[8,16,1024]{2,1,0:T(8,128)S(1)} %get-tuple-element.53), channel_id=1, source_target_pairs={{0,16},{16,0},{32,48},{48,32},{64,80},{80,64},{96,112},{112,96},{1... | collective-permute-start | bytes 1572872 | tf_op jit(solution)/shard_map/ppermute | solution.py:444
  10.9 0.0 collective-permute-start.3
  10.9 0.0 copy-done.6
  10.9 0.9 %select_convert_fusion.1.z_weights = bf16[1024,256]{1,0:T(8,128)(2,1)S(1)} fusion(s32[1024]{0:T(1024)S(1)} %get-tuple-element.88, s32[1024]{0:T(1024)S(1)} %get-tuple-element.89, pred[1024]{0:T(1024)(128)(4,1)S(1)} %fusion.18), kind=kLoop, calls=%fused_computation.15 | loop fusion | flops 3407872 | bytes 533504 | tf_op jit(solution)/shard_map/convert_element_type | solution.py:475
  11.9 1.8 %select_convert_fusion.xy_weights = bf16[512,512]{1,0:T(8,128)(2,1)S(1)} fusion(s32[512]{0:T(512)S(1)} %get-tuple-element.90, s32[512]{0:T(512)S(1)} %get-tuple-element.91, pred[512]{0:T(512)(128)(4,1)S(1)} %fusion.21), kind=kLoop, calls=%fused_computation.8 | loop fusion | flops 9699328 | bytes 528896 | tf_op jit(solution)/shard_map/convert_element_type | solution.py:465
  13.7 0.0 copy-done.2
  13.7 0.0 copy-done.4
  13.7 0.0 copy-done.5
  13.7 9.3 %shard_map.148 = (f32[32,16,1024]{2,1,0:T(8,128)S(1)}, f32[32,16,1024]{2,1,0:T(8,128)S(1)}, f32[32,16,1024]{2,1,0:T(8,128)S(1)}, f32[32,16,1024]{2,1,0:T(8,128)S(1)}, f32[2048,128]{1,0:T(8,128)S(1)}) custom-call(s32[4]{0:T(128)S(1)} %copy-done.5, f32[4]{0:T(128)S(1)} %get-tuple-element.86.amps, f32[4096,128]{1,0:T(8,128)S(1)} %get-tuple-element.45.wave.wave_old, ...), custom_call_target="tpu_custom_call" | custom-call | bytes 24000000 | tf_op jit(solution)/shard_map/pallas_call | solution.py:428
  23.0 0.0 collective-permute-done.2.rxa
  23.0 0.0 collective-permute-done.3.rxb
  23.0 0.0 collective-permute-done.rya
  23.1 0.0 collective-permute-done.1.ryb
  23.1 1.4 %shard_map.149 = (f32[32,16,1024]{2,1,0:T(8,128)S(1)}, f32[32,16,1024]{2,1,0:T(8,128)S(1)}, f32[4096,128]{1,0:T(8,128)S(1)}, f32[4096,128]{1,0:T(8,128)S(1)}, f3...) custom-call(s32[2]{0:T(128)S(1)} %get-tuple-element.43.place, ...), custom_call_target="tpu_custom_call" | custom-call | bytes 6000000 | tf_op jit(solution)/shard_map/pallas_call | solution.py:428
  24.4 0.0 copy-start.3
  24.5 2.0 %shard_map.150 = (f32[32,16,1024]{2,1,0:T(8,128)S(1)}, f32[32,16,1024]{2,1,0:T(8,128)S(1)}, f32[4096,128]{1,0:T(8,128)S(1)}, f32[4096,128]{1,0:T(8,128)S(1)}, f3...) custom-call(s32[2]{0:T(128)S(1)} %get-tuple-element.43.place, ...), custom_call_target="tpu_custom_call", output_to_operand_aliasing={{0}: (8, {}), {1}: (9, {}), {2}: (10, {}), {3}: (11, {}), {... | custom-call | bytes 6000000 | tf_op jit(solution)/shard_map/pallas_call | solution.py:428
  26.4 0.6 collective-permute-start.6
  27.0 3.4 %collective-permute-start.7 = (f32[32,8,1024]{2,1,0:T(8,128)S(1)}, f32[32,8,1024]{2,1,0:T(8,128)S(1)}, u32[]{:S(2)}, u32[]{:S(2)}) collective-permute-start(f32[32,8,1024]{2,1,0:T(8,128)S(1)} %get-tuple-element.75), channel_id=1, source_target_pairs={{1,2},{2,1},{3,4},{4,3},{5,6},{6,5},{7,8},{8,7},{9,10},{10,9},{11,... | collective-permute-start | bytes 3145736 | tf_op jit(solution)/shard_map/ppermute | solution.py:449
  30.5 0.0 copy-done.3
  30.5 0.2 convert_reduce_fusion
  30.7 2.2 %collective-permute-start.4 = (f32[8,16,1024]{2,1,0:T(8,128)S(1)}, f32[8,16,1024]{2,1,0:T(8,128)S(1)}, u32[]{:S(2)}, u32[]{:S(2)}) collective-permute-start(f32[8,16,1024]{2,1,0:T(8,128)S(1)} %get-tuple-element.69), channel_id=1, source_target_pairs={{0,16},{16,0},{32,48},{48,32},{64,80},{80,64},{96,112},{112,96},{1... | collective-permute-start | bytes 1572872 | tf_op jit(solution)/shard_map/ppermute | solution.py:444
  32.8 0.0 collective-permute-start.5
  32.9 0.1 fusion.14.slots
  33.0 9.9 %shard_map.151 = (f32[32,16,1024]{2,1,0:T(8,128)S(1)}, f32[32,16,1024]{2,1,0:T(8,128)S(1)}, f32[256,128]{1,0:T(8,128)S(1)}, f32[32,16,1024]{2,1,0:T(8,128)}, f32[32,16,1024]{2,1,0:T(8,128)}) custom-call(s32[4]{0:T(128)S(1)} %copy-done.5, f32[4]{0:T(128)S(1)} %get-tuple-element.87.amps, s32[2048]{0:T(1024)S(1)} %add_bitcast_fusion.rows_at, ...), custom_call_target="tpu_custom_call" | custom-call | bytes 30000000 | tf_op jit(solution)/shard_map/pallas_call | solution.py:428
  42.8 0.0 collective-permute-done.4.rxa
  42.9 0.0 collective-permute-done.5.rxb
  42.9 0.0 collective-permute-done.6.rya
  42.9 2.6 %shard_map.152 = (f32[32,16,1024]{2,1,0:T(8,128)S(1)}, f32[32,16,1024]{2,1,0:T(8,128)S(1)}, f32[4096,128]{1,0:T(8,128)S(1)}) custom-call(s32[2]{0:T(128)S(1)} %get-tuple-element.43.place, f32[2]{0:T(128)S(1)} %get-tuple-element.44.ends, f32[32,16,1024]{2,1,0:T(8,128)S(1)} %get-tuple-element.67.wave_part, ...), custom_call_target="tpu_custom_call", output_to_operand_aliasing={{0}: (2, {}), {1}: (3, {})} | custom-call | bytes 9000000 | tf_op jit(solution)/shard_map/pallas_call | solution.py:428
  45.5 0.0 collective-permute-done.7.ryb
  45.5 4.6 %shard_map.153 = (f32[32,16,1024]{2,1,0:T(8,128)S(1)}, f32[32,16,1024]{2,1,0:T(8,128)S(1)}, f32[4096,128]{1,0:T(8,128)S(1)}, f32[32,16,1024]{2,1,0:T(8,128)}, f3...) custom-call(s32[2]{0:T(128)S(1)} %get-tuple-element.43.place, ...), custom_call_target="tpu_custom_call", output_to_operand_aliasing={{0}: (2, {}), {1}: (3, {}), {2}: (4, {})} | custom-call | bytes 12000000 | tf_op jit(solution)/shard_map/pallas_call | solution.py:428
  50.0 34.8 %all_to_all.5 = f32[128,1,128]{2,1,0:T(1,128)S(1)} all-to-all(f32[128,1,128]{2,1,0:T(1,128)S(1)} %bitcast.24), channel_id=1, replica_groups=mesh['gx'=8,'gy'=16] {'gx','gy'}, dimensions={0} | all-to-all | bytes 131072 | tf_op jit(solution)/shard_map/all_to_all | solution.py:564
  84.9 0.7 copy.33
  (8 shorter events, 0.0 us)
Async XLA Ops:
  0.8 2.7 %copy-start = (f32[32,16,1024]{2,1,0:T(8,128)S(1)}, f32[32,16,1024]{2,1,0:T(8,128)}, u32[]{:S(2)}) copy-start(f32[32,16,1024]{2,1,0:T(8,128)} %wave.3) | copy-start | bytes 6291460
  0.8 2.7 %copy-start.1 = (f32[32,16,1024]{2,1,0:T(8,128)S(1)}, f32[32,16,1024]{2,1,0:T(8,128)}, u32[]{:S(2)}) copy-start(f32[32,16,1024]{2,1,0:T(8,128)} %born.3) | copy-start | bytes 6291460
  3.5 7.4 %copy-start.6 = (f32[4,2]{0,1:T(2,128)S(1)}, f32[4,2]{0,1:T(2,128)}, u32[]{:S(2)}) copy-start(f32[4,2]{0,1:T(2,128)} %param.18) | copy-start | bytes 100
  3.5 10.2 %copy-start.2 = (s32[256,8]{0,1:T(8,128)S(1)}, s32[256,8]{0,1:T(8,128)}, u32[]{:S(2)}) copy-start(s32[256,8]{0,1:T(8,128)} %param.19) | copy-start | bytes 24580
  3.5 10.2 %copy-start.4 = (f32[256,8]{0,1:T(8,128)S(1)}, f32[256,8]{0,1:T(8,128)}, u32[]{:S(2)}) copy-start(f32[256,8]{0,1:T(8,128)} %param.20) | copy-start | bytes 24580
  3.5 10.2 %copy-start.5 = (s32[4]{0:T(128)S(1)}, s32[4]{0:T(128)}, u32[]{:S(2)}) copy-start(s32[4]{0:T(128)} %cells.3) | copy-start | bytes 52
  4.5 18.5 %collective-permute-start = (f32[32,8,1024]{2,1,0:T(8,128)S(1)}, f32[32,8,1024]{2,1,0:T(8,128)S(1)}, u32[]{:S(2)}, u32[]{:S(2)}) collective-permute-start(f32[32,8,1024]{2,1,0:T(8,128)S(1)} %get-tuple-element.51), channel_id=1, source_target_pairs={{0,1},{1,0},{2,3},{3,2},{4,5},{5,4},{6,7},{7,6},{8,9},{9,8},{10,11... | collective-permute-start | bytes 3145736 | tf_op jit(solution)/shard_map/ppermute | solution.py:450
  6.0 17.1 %collective-permute-start.1 = (f32[32,8,1024]{2,1,0:T(8,128)S(1)}, f32[32,8,1024]{2,1,0:T(8,128)S(1)}, u32[]{:S(2)}, u32[]{:S(2)}) collective-permute-start(f32[32,8,1024]{2,1,0:T(8,128)S(1)} %get-tuple-element.52), channel_id=1, source_target_pairs={{1,2},{2,1},{3,4},{4,3},{5,6},{6,5},{7,8},{8,7},{9,10},{10,9},{11,... | collective-permute-start | bytes 3145736 | tf_op jit(solution)/shard_map/ppermute | solution.py:449
  9.6 13.5 %collective-permute-start.2 = (f32[8,16,1024]{2,1,0:T(8,128)S(1)}, f32[8,16,1024]{2,1,0:T(8,128)S(1)}, u32[]{:S(2)}, u32[]{:S(2)}) collective-permute-start(f32[8,16,1024]{2,1,0:T(8,128)S(1)} %get-tuple-element.53), channel_id=1, source_target_pairs={{0,16},{16,0},{32,48},{48,32},{64,80},{80,64},{96,112},{112,96},{1... | collective-permute-start | bytes 1572872 | tf_op jit(solution)/shard_map/ppermute | solution.py:444
  10.9 12.2 %collective-permute-start.3 = (f32[8,16,1024]{2,1,0:T(8,128)S(1)}, f32[8,16,1024]{2,1,0:T(8,128)S(1)}, u32[]{:S(2)}, u32[]{:S(2)}) collective-permute-start(f32[8,16,1024]{2,1,0:T(8,128)S(1)} %get-tuple-element.54), channel_id=1, source_target_pairs={{16,32},{17,33},{18,34},{19,35},{20,36},{21,37},{22,38},{23,39},{2... | collective-permute-start | bytes 1572872 | tf_op jit(solution)/shard_map/ppermute | solution.py:443
  24.4 6.0 %copy-start.3 = (s32[256,1]{0,1:T(1,128)S(1)}, s32[256,1]{0,1:T(1,128)}, u32[]{:S(2)}) copy-start(s32[256,1]{0,1:T(1,128)} %param.21) | copy-start | bytes 3076
  26.4 16.4 %collective-permute-start.6 = (f32[32,8,1024]{2,1,0:T(8,128)S(1)}, f32[32,8,1024]{2,1,0:T(8,128)S(1)}, u32[]{:S(2)}, u32[]{:S(2)}) collective-permute-start(f32[32,8,1024]{2,1,0:T(8,128)S(1)} %get-tuple-element.71), channel_id=1, source_target_pairs={{0,1},{1,0},{2,3},{3,2},{4,5},{5,4},{6,7},{7,6},{8,9},{9,8},{10,11... | collective-permute-start | bytes 3145736 | tf_op jit(solution)/shard_map/ppermute | solution.py:450
  27.0 18.5 %collective-permute-start.7 = (f32[32,8,1024]{2,1,0:T(8,128)S(1)}, f32[32,8,1024]{2,1,0:T(8,128)S(1)}, u32[]{:S(2)}, u32[]{:S(2)}) collective-permute-start(f32[32,8,1024]{2,1,0:T(8,128)S(1)} %get-tuple-element.75), channel_id=1, source_target_pairs={{1,2},{2,1},{3,4},{4,3},{5,6},{6,5},{7,8},{8,7},{9,10},{10,9},{11,... | collective-permute-start | bytes 3145736 | tf_op jit(solution)/shard_map/ppermute | solution.py:449
  30.7 12.2 %collective-permute-start.4 = (f32[8,16,1024]{2,1,0:T(8,128)S(1)}, f32[8,16,1024]{2,1,0:T(8,128)S(1)}, u32[]{:S(2)}, u32[]{:S(2)}) collective-permute-start(f32[8,16,1024]{2,1,0:T(8,128)S(1)} %get-tuple-element.69), channel_id=1, source_target_pairs={{0,16},{16,0},{32,48},{48,32},{64,80},{80,64},{96,112},{112,96},{1... | collective-permute-start | bytes 1572872 | tf_op jit(solution)/shard_map/ppermute | solution.py:444
  32.8 10.0 %collective-permute-start.5 = (f32[8,16,1024]{2,1,0:T(8,128)S(1)}, f32[8,16,1024]{2,1,0:T(8,128)S(1)}, u32[]{:S(2)}, u32[]{:S(2)}) collective-permute-start(f32[8,16,1024]{2,1,0:T(8,128)S(1)} %get-tuple-element.70), channel_id=1, source_target_pairs={{16,32},{17,33},{18,34},{19,35},{20,36},{21,37},{22,38},{23,39},{2... | collective-permute-start | bytes 1572872 | tf_op jit(solution)/shard_map/ppermute | solution.py:443

commit v7 on v6

--- a/solution.py
+++ b/solution.py
@@ -225,13 +225,12 @@
         copy.wait()
 
 
-def fix(place, ends, parts, scales, x_halo, y_halo, outs, y_faces, edges, middle, tiles=(0, 1)):
+def fix(place, ends, parts, scales, x_halo, y_halo, outs, face, edges, middle, tiles=(0, 1)):
     wave_part, born_part = parts
     courant, contrast = scales
     wave, born, wave_rows, born_rows = outs
     sub, _ = iotas()
     even_x = place[0] == 0
-    even_y = place[1] == 0
     part = lax.bitwise_and(sub, 3)
 
     low_weights = [jnp.where(part < k, WEIGHTS[k - 1], 0.0) for k in range(1, 4)]
@@ -253,7 +252,7 @@
                     total = total + high_weights[k - 1] * pltpu.roll(high, 4 - k, 0)
                 wave_sums[1] = jnp.where(sub < 4, 0.0, pltpu.roll(total, 4, 0))
                 born_sums[1] = jnp.where(sub < 4, 0.0, total)
-            finals = []
+            finals = {}
             for t in tiles:
                 wave_sum, born_sum = wave_sums[t], born_sums[t]
                 if side:
@@ -277,10 +276,15 @@
                 if wave_rows is not None:
                     wave_rows[strip(x, t, z), :] = wave_value
                 born_rows[strip(x, t, z), :] = born_value
-                finals.append((wave_value, born_value))
-            if y_faces is not None:
-                (w0, b0), (w1, b1) = finals
-                pack_y(sub, even_y, *y_faces, x, z, w0, w1, b0, b1)
+                finals[t] = (wave_value, born_value)
+            if face is not None:
+                ref, t = face
+                wave_value, born_value = finals[t]
+                if t == 0:
+                    packed = jnp.where(sub < 4, wave_value, pltpu.roll(born_value, 4, 0))
+                else:
+                    packed = jnp.where(sub < 4, pltpu.roll(wave_value, 4, 0), born_value)
+                put(ref, x, 0, z, packed)
 
     if edges:
         for x in range(4):
@@ -292,16 +296,6 @@
         lax.fori_loop(first, end, lambda x, carry: (one(x, 0, 0), carry)[1], 0)
 
 
-def both_sides(place, ya, yb):
-    even_y = place[1] == 0
-
-    def pick(x, z):
-        from_a, from_b = tile(ya, x, 0, z), tile(yb, x, 0, z)
-        return jnp.where(even_y, from_b, from_a), jnp.where(even_y, from_a, from_b)
-
-    return pick
-
-
 def low_side(face):
     return lambda x, z: (tile(face, x, 0, z), None)
 
@@ -310,39 +304,50 @@
     return lambda x, z: (None, tile(face, x, 0, z))
 
 
-def fix_edges(
-    place, ends, wave_part, born_part, courant, contrast, rxa, rxb, rya, ryb,
-    wave, born, wave_rows, born_rows, ya, yb, xa, xb,
-):
-    fix(
-        place, ends, (wave_part, born_part), (courant, contrast), (rxa, rxb), both_sides(place, rya, ryb),
-        (wave, born, wave_rows, born_rows), (ya, yb), True, None,
-    )
-    pack_x(place[0] == 0, xa, xb, wave, born)
-
-
-def fix_middle(
-    place, ends, wave_part, born_part, courant, contrast, rya, ryb, wave_in, born_in, rows_a, rows_b, ya_in, yb_in,
-    wave, born, wave_rows, born_rows, ya, yb,
-):
-    fix(
-        place, ends, (wave_part, born_part), (courant, contrast), None, both_sides(place, rya, ryb),
-        (wave, born, wave_rows, born_rows), (ya, yb), False, (4, CX - 4),
-    )
-
-
-def fix_early(
-    place, ends, wave_part, born_part, courant, contrast, rxa, rxb, rya, wave, born, born_rows,
-):
+def fix_early(place, ends, parts, scales, rxa, rxb, rya, outs, ya):
     for even in (True, False):
 
         @pl.when((place[1] == 0) == even)
         def _():
             fix(
-                place, ends, (wave_part, born_part), (courant, contrast), (rxa, rxb),
-                high_side(rya) if even else low_side(rya),
-                (wave, born, None, born_rows), None, True, (4, CX - 4),
+                place, ends, parts, scales, (rxa, rxb), high_side(rya) if even else low_side(rya), outs,
+                None if ya is None else (ya, 1 if even else 0), True, (4, CX - 4),
             )
+
+
+def fix_late(place, parts, scales, ryb, outs, yb):
+    for even in (True, False):
+
+        @pl.when((place[1] == 0) == even)
+        def _():
+            side = 0 if even else 1
+            fix(
+                place, None, parts, scales, None, low_side(ryb) if even else high_side(ryb), outs,
+                None if yb is None else (yb, side), False, (0, CX), (side,),
+            )
+
+
+def early_first(
+    place, ends, wave_part, born_part, courant, contrast, rxa, rxb, rya, wave, born, wave_rows, born_rows, ya,
+):
+    outs = (wave, born, wave_rows, born_rows)
+    fix_early(place, ends, (wave_part, born_part), (courant, contrast), rxa, rxb, rya, outs, ya)
+
+
+def late_first(
+    place, wave_in, born_in, wave_rows_in, born_rows_in, courant, contrast, ryb,
+    wave, born, wave_rows, born_rows, yb, xa, xb,
+):
+    outs = (wave, born, wave_rows, born_rows)
+    fix_late(place, (wave_in, born_in), (courant, contrast), ryb, outs, yb)
+    pack_x(place[0] == 0, xa, xb, wave, born)
+
+
+def early_second(
+    place, ends, wave_part, born_part, courant, contrast, rxa, rxb, rya, wave, born, born_rows,
+):
+    outs = (wave, born, None, born_rows)
+    fix_early(place, ends, (wave_part, born_part), (courant, contrast), rxa, rxb, rya, outs, None)
 
 
 def take(rows_at, grid, picks, rows, out):
@@ -369,16 +374,7 @@
     place, rows_at, wave_in, born_in, grid_in, courant, contrast, ryb, picks, first, slots, dest,
     wave, born, grid, wave_out, born_out, packed, rows, sums, sems,
 ):
-    for even in (True, False):
-
-        @pl.when((place[1] == 0) == even)
-        def _():
-            fix(
-                place, None, (wave_in, born_in), (courant, contrast), None,
-                low_side(ryb) if even else high_side(ryb),
-                (wave, born, None, grid), None, False, (0, CX), (0,) if even else (1,),
-            )
-
+    fix_late(place, (wave_in, born_in), (courant, contrast), ryb, (wave, born, None, grid), None)
     copies = [
         pltpu.make_async_copy(wave, wave_out, sems.at[0]),
         pltpu.make_async_copy(born, born_out, sems.at[1]),
@@ -528,16 +524,15 @@
     lane = lax.broadcasted_iota(jnp.int32, (256, 128), 1)
     slots = jnp.where((lane < 8) & (lane % 4 == slot[:, None]), 1.0, 0.0).astype(F32)
 
-    shared = (wave_part, born_part, speed, factor)
-    *mid, xa, xb = call(
-        fix_edges, (place, ends, *shared, *halo_x, *halo_y),
-        [SM] * 2 + [VM] * 8, fixed + y_faces + x_faces, [], 4, 2,
+    *mid, ya = call(
+        early_first, (place, ends, wave_part, born_part, speed, factor, *halo_x, halo_y[0]),
+        [SM] * 2 + [VM] * 7, fixed + y_faces[:1], [], 4, 3, {2: 0, 3: 1},
+    )
+    wave_mid, born_mid, wave_mid_rows, born_mid_rows, yb, xa, xb = call(
+        late_first, (place, *mid, speed, factor, halo_y[1]),
+        [SM] + [VM] * 7, fixed + y_faces[:1] + x_faces, [], 4, 2, {i + 1: i for i in range(4)},
     )
     next_x = swap_x(xa, xb)
-    wave_mid, born_mid, wave_mid_rows, born_mid_rows, ya, yb = call(
-        fix_middle, (place, ends, *shared, *halo_y, *mid),
-        [SM] * 2 + [VM] * 12, fixed + y_faces, [], 4, 2, {i + 8: i for i in range(6)},
-    )
     next_y = swap_y(ya, yb)
     wave_part, born_part, first, wave_next, born_next = call(
         inner_second,
@@ -550,7 +545,7 @@
         [*halves, pltpu.VMEM((2048, 128), F32), pltpu.VMEM((256, 128), F32), pltpu.SemaphoreType.DMA((2,))], 12, 10,
     )
     near = call(
-        fix_early, (place, ends, wave_part, born_part, speed, factor, *next_x, next_y[0]),
+        early_second, (place, ends, wave_part, born_part, speed, factor, *next_x, next_y[0]),
         [SM] * 2 + [VM] * 7, [kept(BLOCK)] * 2 + [kept((ROWS, 128))], [], 4, 3, {2: 0, 3: 1},
     )
     *_, wave_last, born_last, packed = call(

time: 85.7 us -> 86.8 us (1.013)
  Pallas kernels: 33.3 us -> 35.3 us
  blocking collectives: 34.8 us -> 33.3 us
    pallas_call x8, Pallas kernels: 33.3 us -> 35.3 us  [call(): pl.pallas_call(kernel, out_shape=tuple((o[1] for o in outs)), in_specs=sp...]
    all_to_all x1, blocking collectives: 34.8 us -> 33.3 us  [steps(): lax.all_to_all(packed.reshape(128, 1, 128), ('gx', 'gy'), split_axis=0, c...]
  transfers between devices with their start and end apart: 8 -> 8, of which waited for: 0 -> 0; matrix products, arithmetic and copies ran while one was open for 4% -> 4% of each run, Pallas kernels for 25% -> 31%
where the time goes in v7:
time: 86.8 us; the launch traced here: 86.6 us
  Pallas kernels  35.3 us (41%)
  blocking collectives  33.3 us (38%)
  starting transfers between devices  13.1 us (15%)
  other arithmetic  3.25 us (4%)
  between operations  0.95 us (1%)
    pallas_call x8, Pallas kernels, call(): pl.pallas_call(kernel, out_shape=tuple((o[1] for o in outs)), in_specs=sp...  35.3 us
    all_to_all x1, blocking collectives, steps(): lax.all_to_all(packed.reshape(128, 1, 128), ('gx', 'gy'), split_axis=0, c...  33.3 us
    ppermute x2, starting transfers between devices, swap_y(): ryb = lax.ppermute(yb, 'gy', pairs(16, 1))  7.53 us
    ppermute x2, starting transfers between devices, swap_x(): rxa = lax.ppermute(xa, 'gx', pairs(8, 0))  3.67 us
    convert_element_type x1, other arithmetic, xy_table(): return table.astype(BF16)  1.84 us
  transfers between devices with their start and end apart: 8, of which 0 were waited for; matrix products, arithmetic and copies ran while one was open for 4% of the time, Pallas kernels for 31%

profile of v7, /device:TPU:1, one launch (start us, length us, event | category | flops | bytes accessed | tf_op | source)
XLA Modules:
  0.0 86.6 jit_solution(6634332484482384554)
XLA Ops:
  0.6 0.1 add_convert_fusion.ends
  0.7 0.1 pad_add_fusion.place
  0.8 0.0 copy-start
  0.8 0.0 copy-start.1
  0.8 2.6 %shard_map.146 = (f32[8,16,1024]{2,1,0:T(8,128)S(1)}, f32[8,16,1024]{2,1,0:T(8,128)S(1)}, s32[2]{0:T(128)S(1)}, f32[2]{0:T(128)S(1)}) custom-call(s32[2]{0:T(128)S(1)} %pad_add_fusion.place, f32[2]{0:T(128)S(1)} %add_convert_fusion.ends, f32[32,16,1024]{2,1,0:T(8,128)} %wave.3, f32[32,16,1024]{2,1,0:T(8,128)} %born.3), custom_call_target="tpu_custom_call" | custom-call | bytes 3000000 | tf_op jit(solution)/shard_map/pallas_call | solution.py:424
  3.4 0.0 copy-done
  3.5 0.0 copy-done.1
  3.5 0.0 copy-start.6
  3.5 0.0 copy-start.2
  3.5 0.0 copy-start.4
  3.5 0.0 copy-start.5
  3.5 1.0 %shard_map.147 = (f32[4096,128]{1,0:T(8,128)S(1)}, f32[4096,128]{1,0:T(8,128)S(1)}, f32[32,8,1024]{2,1,0:T(8,128)S(1)}, f32[32,8,1024]{2,1,0:T(8,128)S(1)}) custom-call(s32[2]{0:T(128)S(1)} %get-tuple-element.41.place, f32[32,16,1024]{2,1,0:T(8,128)S(1)} %copy-done, f32[32,16,1024]{2,1,0:T(8,128)S(1)} %copy-done.1), custom_call_target="tpu_custom_call" | custom-call | bytes 6000000 | tf_op jit(solution)/shard_map/pallas_call | solution.py:424
  4.5 1.5 %collective-permute-start.2 = (f32[32,8,1024]{2,1,0:T(8,128)S(1)}, f32[32,8,1024]{2,1,0:T(8,128)S(1)}, u32[]{:S(2)}, u32[]{:S(2)}) collective-permute-start(f32[32,8,1024]{2,1,0:T(8,128)S(1)} %get-tuple-element.51), channel_id=1, source_target_pairs={{0,1},{1,0},{2,3},{3,2},{4,5},{5,4},{6,7},{7,6},{8,9},{9,8},{10,11... | collective-permute-start | bytes 3145736 | tf_op jit(solution)/shard_map/ppermute | solution.py:446
  6.0 1.3 %collective-permute-start = (f32[8,16,1024]{2,1,0:T(8,128)S(1)}, f32[8,16,1024]{2,1,0:T(8,128)S(1)}, u32[]{:S(2)}, u32[]{:S(2)}) collective-permute-start(f32[8,16,1024]{2,1,0:T(8,128)S(1)} %get-tuple-element.49), channel_id=1, source_target_pairs={{0,16},{16,0},{32,48},{48,32},{64,80},{80,64},{96,112},{112,96},{1... | collective-permute-start | bytes 1572872 | tf_op jit(solution)/shard_map/ppermute | solution.py:440
  7.3 0.4 collective-permute-start.1
  7.7 3.6 %collective-permute-start.3 = (f32[32,8,1024]{2,1,0:T(8,128)S(1)}, f32[32,8,1024]{2,1,0:T(8,128)S(1)}, u32[]{:S(2)}, u32[]{:S(2)}) collective-permute-start(f32[32,8,1024]{2,1,0:T(8,128)S(1)} %get-tuple-element.56), channel_id=1, source_target_pairs={{1,2},{2,1},{3,4},{4,3},{5,6},{6,5},{7,8},{8,7},{9,10},{10,9},{11,... | collective-permute-start | bytes 3145736 | tf_op jit(solution)/shard_map/ppermute | solution.py:445
  11.3 0.0 copy-done.6
  11.3 0.9 %select_convert_fusion.1.z_weights = bf16[1024,256]{1,0:T(8,128)(2,1)S(1)} fusion(s32[1024]{0:T(1024)S(1)} %get-tuple-element.84, s32[1024]{0:T(1024)S(1)} %get-tuple-element.85, pred[1024]{0:T(1024)(128)(4,1)S(1)} %fusion.18), kind=kLoop, calls=%fused_computation.15 | loop fusion | flops 3407872 | bytes 533504 | tf_op jit(solution)/shard_map/convert_element_type | solution.py:471
  12.3 1.8 %select_convert_fusion.xy_weights = bf16[512,512]{1,0:T(8,128)(2,1)S(1)} fusion(s32[512]{0:T(512)S(1)} %get-tuple-element.86, s32[512]{0:T(512)S(1)} %get-tuple-element.87, pred[512]{0:T(512)(128)(4,1)S(1)} %fusion.21), kind=kLoop, calls=%fused_computation.8 | loop fusion | flops 9699328 | bytes 528896 | tf_op jit(solution)/shard_map/convert_element_type | solution.py:461
  14.1 0.0 copy-done.2
  14.1 0.0 copy-done.4
  14.1 0.0 copy-done.5
  14.2 9.4 %shard_map.148 = (f32[32,16,1024]{2,1,0:T(8,128)S(1)}, f32[32,16,1024]{2,1,0:T(8,128)S(1)}, f32[32,16,1024]{2,1,0:T(8,128)S(1)}, f32[32,16,1024]{2,1,0:T(8,128)S(1)}, f32[2048,128]{1,0:T(8,128)S(1)}) custom-call(s32[4]{0:T(128)S(1)} %copy-done.5, f32[4]{0:T(128)S(1)} %get-tuple-element.82.amps, f32[4096,128]{1,0:T(8,128)S(1)} %get-tuple-element.43.wave.wave_old, ...), custom_call_target="tpu_custom_call" | custom-call | bytes 24000000 | tf_op jit(solution)/shard_map/pallas_call | solution.py:424
  23.5 0.0 collective-permute-done.rxa
  23.6 0.0 collective-permute-done.1.rxb
  23.6 0.0 collective-permute-done.2.rya
  23.6 2.8 %shard_map.149 = (f32[32,16,1024]{2,1,0:T(8,128)S(1)}, f32[32,16,1024]{2,1,0:T(8,128)S(1)}, f32[4096,128]{1,0:T(8,128)S(1)}, f32[4096,128]{1,0:T(8,128)S(1)}, f32[32,8,1024]{2,1,0:T(8,128)S(1)}) custom-call(s32[2]{0:T(128)S(1)} %get-tuple-element.41.place, f32[2]{0:T(128)S(1)} %get-tuple-element.42.ends, ...), custom_call_target="tpu_custom_call", output_to_operand_aliasing={{0}: (2, {}), {1}: (3, {})} | custom-call | bytes 9000000 | tf_op jit(solution)/shard_map/pallas_call | solution.py:424
  26.4 0.1 collective-permute-start.6
  26.5 0.0 collective-permute-done.3.ryb
  26.5 0.0 copy-start.3
  26.5 2.2 %shard_map.150 = (f32[32,16,1024]{2,1,0:T(8,128)S(1)}, f32[32,16,1024]{2,1,0:T(8,128)S(1)}, f32[4096,128]{1,0:T(8,128)S(1)}, f32[4096,128]{1,0:T(8,128)S(1)}, f3...) custom-call(s32[2]{0:T(128)S(1)} %get-tuple-element.41.place, ...), custom_call_target="tpu_custom_call", output_to_operand_aliasing={{0}: (1, {}), {1}: (2, {}), {2}: (3, {}), {3}: (4, {})} | custom-call | bytes 6000000 | tf_op jit(solution)/shard_map/pallas_call | solution.py:424
  28.7 4.0 %collective-permute-start.7 = (f32[32,8,1024]{2,1,0:T(8,128)S(1)}, f32[32,8,1024]{2,1,0:T(8,128)S(1)}, u32[]{:S(2)}, u32[]{:S(2)}) collective-permute-start(f32[32,8,1024]{2,1,0:T(8,128)S(1)} %get-tuple-element.71), channel_id=1, source_target_pairs={{1,2},{2,1},{3,4},{4,3},{5,6},{6,5},{7,8},{8,7},{9,10},{10,9},{11,... | collective-permute-start | bytes 3145736 | tf_op jit(solution)/shard_map/ppermute | solution.py:445
  32.7 0.0 copy-done.3
  32.7 0.2 convert_reduce_fusion
  32.8 2.3 %collective-permute-start.4 = (f32[8,16,1024]{2,1,0:T(8,128)S(1)}, f32[8,16,1024]{2,1,0:T(8,128)S(1)}, u32[]{:S(2)}, u32[]{:S(2)}) collective-permute-start(f32[8,16,1024]{2,1,0:T(8,128)S(1)} %get-tuple-element.65), channel_id=1, source_target_pairs={{0,16},{16,0},{32,48},{48,32},{64,80},{80,64},{96,112},{112,96},{1... | collective-permute-start | bytes 1572872 | tf_op jit(solution)/shard_map/ppermute | solution.py:440
  35.2 0.0 collective-permute-start.5
  35.2 0.1 fusion.14.slots
  35.3 9.9 %shard_map.151 = (f32[32,16,1024]{2,1,0:T(8,128)S(1)}, f32[32,16,1024]{2,1,0:T(8,128)S(1)}, f32[256,128]{1,0:T(8,128)S(1)}, f32[32,16,1024]{2,1,0:T(8,128)}, f32[32,16,1024]{2,1,0:T(8,128)}) custom-call(s32[4]{0:T(128)S(1)} %copy-done.5, f32[4]{0:T(128)S(1)} %get-tuple-element.83.amps, s32[2048]{0:T(1024)S(1)} %add_bitcast_fusion.rows_at, ...), custom_call_target="tpu_custom_call" | custom-call | bytes 30000000 | tf_op jit(solution)/shard_map/pallas_call | solution.py:424
  45.2 0.0 collective-permute-done.4.rxa
  45.2 0.0 collective-permute-done.5.rxb
  45.2 0.0 collective-permute-done.6.rya
  45.2 2.8 %shard_map.152 = (f32[32,16,1024]{2,1,0:T(8,128)S(1)}, f32[32,16,1024]{2,1,0:T(8,128)S(1)}, f32[4096,128]{1,0:T(8,128)S(1)}) custom-call(s32[2]{0:T(128)S(1)} %get-tuple-element.41.place, f32[2]{0:T(128)S(1)} %get-tuple-element.42.ends, f32[32,16,1024]{2,1,0:T(8,128)S(1)} %get-tuple-element.63.wave_part, ...), custom_call_target="tpu_custom_call", output_to_operand_aliasing={{0}: (2, {}), {1}: (3, {})} | custom-call | bytes 9000000 | tf_op jit(solution)/shard_map/pallas_call | solution.py:424
  48.0 0.0 collective-permute-done.7.ryb
  48.0 4.6 %shard_map.153 = (f32[32,16,1024]{2,1,0:T(8,128)S(1)}, f32[32,16,1024]{2,1,0:T(8,128)S(1)}, f32[4096,128]{1,0:T(8,128)S(1)}, f32[32,16,1024]{2,1,0:T(8,128)}, f3...) custom-call(s32[2]{0:T(128)S(1)} %get-tuple-element.41.place, ...), custom_call_target="tpu_custom_call", output_to_operand_aliasing={{0}: (2, {}), {1}: (3, {}), {2}: (4, {})} | custom-call | bytes 12000000 | tf_op jit(solution)/shard_map/pallas_call | solution.py:424
  52.6 33.3 %all_to_all.5 = f32[128,1,128]{2,1,0:T(1,128)S(1)} all-to-all(f32[128,1,128]{2,1,0:T(1,128)S(1)} %bitcast.24), channel_id=1, replica_groups=mesh['gx'=8,'gy'=16] {'gx','gy'}, dimensions={0} | all-to-all | bytes 131072 | tf_op jit(solution)/shard_map/all_to_all | solution.py:559
  86.0 0.7 copy.33
  (8 shorter events, 0.0 us)
Async XLA Ops:
  0.8 2.7 %copy-start = (f32[32,16,1024]{2,1,0:T(8,128)S(1)}, f32[32,16,1024]{2,1,0:T(8,128)}, u32[]{:S(2)}) copy-start(f32[32,16,1024]{2,1,0:T(8,128)} %wave.3) | copy-start | bytes 6291460
  0.8 2.7 %copy-start.1 = (f32[32,16,1024]{2,1,0:T(8,128)S(1)}, f32[32,16,1024]{2,1,0:T(8,128)}, u32[]{:S(2)}) copy-start(f32[32,16,1024]{2,1,0:T(8,128)} %born.3) | copy-start | bytes 6291460
  3.5 7.8 %copy-start.6 = (f32[4,2]{0,1:T(2,128)S(1)}, f32[4,2]{0,1:T(2,128)}, u32[]{:S(2)}) copy-start(f32[4,2]{0,1:T(2,128)} %param.18) | copy-start | bytes 100
  3.5 10.7 %copy-start.2 = (s32[256,8]{0,1:T(8,128)S(1)}, s32[256,8]{0,1:T(8,128)}, u32[]{:S(2)}) copy-start(s32[256,8]{0,1:T(8,128)} %param.19) | copy-start | bytes 24580
  3.5 10.6 %copy-start.4 = (f32[256,8]{0,1:T(8,128)S(1)}, f32[256,8]{0,1:T(8,128)}, u32[]{:S(2)}) copy-start(f32[256,8]{0,1:T(8,128)} %param.20) | copy-start | bytes 24580
  3.5 10.6 %copy-start.5 = (s32[4]{0:T(128)S(1)}, s32[4]{0:T(128)}, u32[]{:S(2)}) copy-start(s32[4]{0:T(128)} %cells.3) | copy-start | bytes 52
  4.5 19.0 %collective-permute-start.2 = (f32[32,8,1024]{2,1,0:T(8,128)S(1)}, f32[32,8,1024]{2,1,0:T(8,128)S(1)}, u32[]{:S(2)}, u32[]{:S(2)}) collective-permute-start(f32[32,8,1024]{2,1,0:T(8,128)S(1)} %get-tuple-element.51), channel_id=1, source_target_pairs={{0,1},{1,0},{2,3},{3,2},{4,5},{5,4},{6,7},{7,6},{8,9},{9,8},{10,11... | collective-permute-start | bytes 3145736 | tf_op jit(solution)/shard_map/ppermute | solution.py:446
  6.0 17.5 %collective-permute-start = (f32[8,16,1024]{2,1,0:T(8,128)S(1)}, f32[8,16,1024]{2,1,0:T(8,128)S(1)}, u32[]{:S(2)}, u32[]{:S(2)}) collective-permute-start(f32[8,16,1024]{2,1,0:T(8,128)S(1)} %get-tuple-element.49), channel_id=1, source_target_pairs={{0,16},{16,0},{32,48},{48,32},{64,80},{80,64},{96,112},{112,96},{1... | collective-permute-start | bytes 1572872 | tf_op jit(solution)/shard_map/ppermute | solution.py:440
  7.3 16.2 %collective-permute-start.1 = (f32[8,16,1024]{2,1,0:T(8,128)S(1)}, f32[8,16,1024]{2,1,0:T(8,128)S(1)}, u32[]{:S(2)}, u32[]{:S(2)}) collective-permute-start(f32[8,16,1024]{2,1,0:T(8,128)S(1)} %get-tuple-element.50), channel_id=1, source_target_pairs={{16,32},{17,33},{18,34},{19,35},{20,36},{21,37},{22,38},{23,39},{2... | collective-permute-start | bytes 1572872 | tf_op jit(solution)/shard_map/ppermute | solution.py:439
  7.7 18.8 %collective-permute-start.3 = (f32[32,8,1024]{2,1,0:T(8,128)S(1)}, f32[32,8,1024]{2,1,0:T(8,128)S(1)}, u32[]{:S(2)}, u32[]{:S(2)}) collective-permute-start(f32[32,8,1024]{2,1,0:T(8,128)S(1)} %get-tuple-element.56), channel_id=1, source_target_pairs={{1,2},{2,1},{3,4},{4,3},{5,6},{6,5},{7,8},{8,7},{9,10},{10,9},{11,... | collective-permute-start | bytes 3145736 | tf_op jit(solution)/shard_map/ppermute | solution.py:445
  26.4 18.9 %collective-permute-start.6 = (f32[32,8,1024]{2,1,0:T(8,128)S(1)}, f32[32,8,1024]{2,1,0:T(8,128)S(1)}, u32[]{:S(2)}, u32[]{:S(2)}) collective-permute-start(f32[32,8,1024]{2,1,0:T(8,128)S(1)} %get-tuple-element.67), channel_id=1, source_target_pairs={{0,1},{1,0},{2,3},{3,2},{4,5},{5,4},{6,7},{7,6},{8,9},{9,8},{10,11... | collective-permute-start | bytes 3145736 | tf_op jit(solution)/shard_map/ppermute | solution.py:446
  26.5 6.2 %copy-start.3 = (s32[256,1]{0,1:T(1,128)S(1)}, s32[256,1]{0,1:T(1,128)}, u32[]{:S(2)}) copy-start(s32[256,1]{0,1:T(1,128)} %param.21) | copy-start | bytes 3076
  28.7 19.4 %collective-permute-start.7 = (f32[32,8,1024]{2,1,0:T(8,128)S(1)}, f32[32,8,1024]{2,1,0:T(8,128)S(1)}, u32[]{:S(2)}, u32[]{:S(2)}) collective-permute-start(f32[32,8,1024]{2,1,0:T(8,128)S(1)} %get-tuple-element.71), channel_id=1, source_target_pairs={{1,2},{2,1},{3,4},{4,3},{5,6},{6,5},{7,8},{8,7},{9,10},{10,9},{11,... | collective-permute-start | bytes 3145736 | tf_op jit(solution)/shard_map/ppermute | solution.py:445
  32.8 12.4 %collective-permute-start.4 = (f32[8,16,1024]{2,1,0:T(8,128)S(1)}, f32[8,16,1024]{2,1,0:T(8,128)S(1)}, u32[]{:S(2)}, u32[]{:S(2)}) collective-permute-start(f32[8,16,1024]{2,1,0:T(8,128)S(1)} %get-tuple-element.65), channel_id=1, source_target_pairs={{0,16},{16,0},{32,48},{48,32},{64,80},{80,64},{96,112},{112,96},{1... | collective-permute-start | bytes 1572872 | tf_op jit(solution)/shard_map/ppermute | solution.py:440
  35.2 10.0 %collective-permute-start.5 = (f32[8,16,1024]{2,1,0:T(8,128)S(1)}, f32[8,16,1024]{2,1,0:T(8,128)S(1)}, u32[]{:S(2)}, u32[]{:S(2)}) collective-permute-start(f32[8,16,1024]{2,1,0:T(8,128)S(1)} %get-tuple-element.66), channel_id=1, source_target_pairs={{16,32},{17,33},{18,34},{19,35},{20,36},{21,37},{22,38},{23,39},{2... | collective-permute-start | bytes 1572872 | tf_op jit(solution)/shard_map/ppermute | solution.py:439

commit v8 on v6

--- a/solution.py
+++ b/solution.py
@@ -289,7 +289,8 @@
             one(x, 1, x - (CX - 4))
     if middle:
         first, end = middle
-        lax.fori_loop(first, end, lambda x, carry: (one(x, 0, 0), carry)[1], 0)
+        unroll = 2 if len(tiles) == 1 else 1
+        lax.fori_loop(first, end, lambda x, carry: (one(x, 0, 0), carry)[1], 0, unroll=unroll)
 
 
 def both_sides(place, ya, yb):
@@ -346,15 +347,10 @@
 
 
 def take(rows_at, grid, picks, rows, out):
-    def step(g, carry):
-        for half in range(2):
-            for j in range(8):
-                for t in range(8):
-                    source = rows_at[g * 8 + (half * 1024 + t * 128 + j)]
-                    rows[pl.ds(g * 64 + (half * 1024 + j * 8 + t), 1), :] = grid[pl.ds(source, 1), :]
-        return carry
-
-    lax.fori_loop(0, 16, step, 0)
+    for r in range(256):
+        for t in range(8):
+            source = rows_at[r // 128 * 1024 + t * 128 + r % 128]
+            rows[r * 8 + t : r * 8 + t + 1, :] = grid[pl.ds(source, 1), :]
 
     def total(g, carry):
         part = pl.ds(pl.multiple_of(g * 256, 256), 256)
@@ -390,8 +386,14 @@
     lane = lax.broadcasted_iota(jnp.int32, (256, 128), 1)
     spread_out = first[...] + jnp.where(lane < 4, 0.0, two) * slots[...]
     owner = lax.broadcasted_iota(jnp.int32, (128, 256), 0)
-    chosen = jnp.where(owner == dest[...], 1.0, 0.0).astype(F32)
-    packed[...] = jnp.dot(chosen, spread_out, precision=lax.Precision.HIGHEST, preferred_element_type=F32)
+    chosen = jnp.where(owner == dest[...], 1.0, 0.0).astype(BF16)
+    pieces = []
+    for _ in range(3):
+        pieces.append(spread_out.astype(BF16))
+        spread_out = spread_out - pieces[-1].astype(F32)
+    packed[...] = jnp.dot(
+        jnp.concatenate([chosen] * 3, axis=1), jnp.concatenate(pieces, axis=0), preferred_element_type=F32
+    )
     for copy in copies:
         copy.wait()
 

time: 85.7 us -> 85.3 us (level)
  Pallas kernels: 33.3 us -> 32.1 us
    pallas_call x8, Pallas kernels: 33.3 us -> 32.1 us  [call(): pl.pallas_call(kernel, out_shape=tuple((o[1] for o in outs)), in_specs=sp...]
  transfers between devices with their start and end apart: 8 -> 8, of which waited for: 0 -> 1; matrix products, arithmetic and copies ran while one was open for 4% -> 4% of each run, Pallas kernels for 25% -> 25%
where the time goes in v8:
time: 85.3 us; the launch traced here: 85.2 us
  blocking collectives  35.4 us (42%)
  Pallas kernels  32.1 us (38%)
  starting transfers between devices  12.5 us (15%)
  other arithmetic  3.25 us (4%)
  between operations  0.9 us (1%)
    all_to_all x1, blocking collectives, steps(): lax.all_to_all(packed.reshape(128, 1, 128), ('gx', 'gy'), split_axis=0, c...  35.4 us
    pallas_call x8, Pallas kernels, call(): pl.pallas_call(kernel, out_shape=tuple((o[1] for o in outs)), in_specs=sp...  32.1 us
    ppermute x2, starting transfers between devices, swap_y(): ryb = lax.ppermute(yb, 'gy', pairs(16, 1))  7 us
    ppermute x2, starting transfers between devices, swap_x(): rxa = lax.ppermute(xa, 'gx', pairs(8, 0))  3.47 us
    ppermute x2, starting transfers between devices, swap_y(): rya = lax.ppermute(ya, 'gy', pairs(16, 0))  2.04 us
    convert_element_type x1, other arithmetic, xy_table(): return table.astype(BF16)  1.84 us
  transfers between devices with their start and end apart: 8, of which 1 were waited for; matrix products, arithmetic and copies ran while one was open for 4% of the time, Pallas kernels for 25%

profile of v8, /device:TPU:1, one launch (start us, length us, event | category | flops | bytes accessed | tf_op | source)
XLA Modules:
  0.0 85.2 jit_solution(7415225112836091184)
XLA Ops:
  0.6 0.1 add_convert_fusion.ends
  0.7 0.1 pad_add_fusion.place
  0.8 0.0 copy-start
  0.8 0.0 copy-start.1
  0.8 2.6 %shard_map.146 = (f32[8,16,1024]{2,1,0:T(8,128)S(1)}, f32[8,16,1024]{2,1,0:T(8,128)S(1)}, s32[2]{0:T(128)S(1)}, f32[2]{0:T(128)S(1)}) custom-call(s32[2]{0:T(128)S(1)} %pad_add_fusion.place, f32[2]{0:T(128)S(1)} %add_convert_fusion.ends, f32[32,16,1024]{2,1,0:T(8,128)} %wave.3, f32[32,16,1024]{2,1,0:T(8,128)} %born.3), custom_call_target="tpu_custom_call" | custom-call | bytes 3000000 | tf_op jit(solution)/shard_map/pallas_call | solution.py:430
  3.4 0.0 copy-done
  3.5 0.0 copy-done.1
  3.5 0.0 copy-start.6
  3.5 0.0 copy-start.2
  3.5 0.0 copy-start.4
  3.5 0.0 copy-start.5
  3.5 1.0 %shard_map.147 = (f32[4096,128]{1,0:T(8,128)S(1)}, f32[4096,128]{1,0:T(8,128)S(1)}, f32[32,8,1024]{2,1,0:T(8,128)S(1)}, f32[32,8,1024]{2,1,0:T(8,128)S(1)}) custom-call(s32[2]{0:T(128)S(1)} %get-tuple-element.43.place, f32[32,16,1024]{2,1,0:T(8,128)S(1)} %copy-done, f32[32,16,1024]{2,1,0:T(8,128)S(1)} %copy-done.1), custom_call_target="tpu_custom_call" | custom-call | bytes 6000000 | tf_op jit(solution)/shard_map/pallas_call | solution.py:430
  4.5 1.5 %collective-permute-start = (f32[32,8,1024]{2,1,0:T(8,128)S(1)}, f32[32,8,1024]{2,1,0:T(8,128)S(1)}, u32[]{:S(2)}, u32[]{:S(2)}) collective-permute-start(f32[32,8,1024]{2,1,0:T(8,128)S(1)} %get-tuple-element.51), channel_id=1, source_target_pairs={{0,1},{1,0},{2,3},{3,2},{4,5},{5,4},{6,7},{7,6},{8,9},{9,8},{10,11... | collective-permute-start | bytes 3145736 | tf_op jit(solution)/shard_map/ppermute | solution.py:452
  6.0 3.6 %collective-permute-start.1 = (f32[32,8,1024]{2,1,0:T(8,128)S(1)}, f32[32,8,1024]{2,1,0:T(8,128)S(1)}, u32[]{:S(2)}, u32[]{:S(2)}) collective-permute-start(f32[32,8,1024]{2,1,0:T(8,128)S(1)} %get-tuple-element.52), channel_id=1, source_target_pairs={{1,2},{2,1},{3,4},{4,3},{5,6},{6,5},{7,8},{8,7},{9,10},{10,9},{11,... | collective-permute-start | bytes 3145736 | tf_op jit(solution)/shard_map/ppermute | solution.py:451
  9.6 1.3 %collective-permute-start.2 = (f32[8,16,1024]{2,1,0:T(8,128)S(1)}, f32[8,16,1024]{2,1,0:T(8,128)S(1)}, u32[]{:S(2)}, u32[]{:S(2)}) collective-permute-start(f32[8,16,1024]{2,1,0:T(8,128)S(1)} %get-tuple-element.53), channel_id=1, source_target_pairs={{0,16},{16,0},{32,48},{48,32},{64,80},{80,64},{96,112},{112,96},{1... | collective-permute-start | bytes 1572872 | tf_op jit(solution)/shard_map/ppermute | solution.py:446
  10.9 0.0 collective-permute-start.3
  10.9 0.0 copy-done.6
  10.9 0.9 %select_convert_fusion.1.z_weights = bf16[1024,256]{1,0:T(8,128)(2,1)S(1)} fusion(s32[1024]{0:T(1024)S(1)} %get-tuple-element.88, s32[1024]{0:T(1024)S(1)} %get-tuple-element.89, pred[1024]{0:T(1024)(128)(4,1)S(1)} %fusion.18), kind=kLoop, calls=%fused_computation.15 | loop fusion | flops 3407872 | bytes 533504 | tf_op jit(solution)/shard_map/convert_element_type | solution.py:477
  11.9 1.8 %select_convert_fusion.xy_weights = bf16[512,512]{1,0:T(8,128)(2,1)S(1)} fusion(s32[512]{0:T(512)S(1)} %get-tuple-element.90, s32[512]{0:T(512)S(1)} %get-tuple-element.91, pred[512]{0:T(512)(128)(4,1)S(1)} %fusion.21), kind=kLoop, calls=%fused_computation.8 | loop fusion | flops 9699328 | bytes 528896 | tf_op jit(solution)/shard_map/convert_element_type | solution.py:467
  13.7 0.0 copy-done.2
  13.7 0.0 copy-done.4
  13.7 0.0 copy-done.5
  13.7 9.3 %shard_map.148 = (f32[32,16,1024]{2,1,0:T(8,128)S(1)}, f32[32,16,1024]{2,1,0:T(8,128)S(1)}, f32[32,16,1024]{2,1,0:T(8,128)S(1)}, f32[32,16,1024]{2,1,0:T(8,128)S(1)}, f32[2048,128]{1,0:T(8,128)S(1)}) custom-call(s32[4]{0:T(128)S(1)} %copy-done.5, f32[4]{0:T(128)S(1)} %get-tuple-element.86.amps, f32[4096,128]{1,0:T(8,128)S(1)} %get-tuple-element.45.wave.wave_old, ...), custom_call_target="tpu_custom_call" | custom-call | bytes 24000000 | tf_op jit(solution)/shard_map/pallas_call | solution.py:430
  23.0 0.0 collective-permute-done.2.rxa
  23.0 0.0 collective-permute-done.3.rxb
  23.0 0.0 collective-permute-done.rya
  23.1 0.0 collective-permute-done.1.ryb
  23.1 1.4 %shard_map.149 = (f32[32,16,1024]{2,1,0:T(8,128)S(1)}, f32[32,16,1024]{2,1,0:T(8,128)S(1)}, f32[4096,128]{1,0:T(8,128)S(1)}, f32[4096,128]{1,0:T(8,128)S(1)}, f3...) custom-call(s32[2]{0:T(128)S(1)} %get-tuple-element.43.place, ...), custom_call_target="tpu_custom_call" | custom-call | bytes 6000000 | tf_op jit(solution)/shard_map/pallas_call | solution.py:430
  24.4 0.0 copy-start.3
  24.5 2.0 %shard_map.150 = (f32[32,16,1024]{2,1,0:T(8,128)S(1)}, f32[32,16,1024]{2,1,0:T(8,128)S(1)}, f32[4096,128]{1,0:T(8,128)S(1)}, f32[4096,128]{1,0:T(8,128)S(1)}, f3...) custom-call(s32[2]{0:T(128)S(1)} %get-tuple-element.43.place, ...), custom_call_target="tpu_custom_call", output_to_operand_aliasing={{0}: (8, {}), {1}: (9, {}), {2}: (10, {}), {3}: (11, {}), {... | custom-call | bytes 6000000 | tf_op jit(solution)/shard_map/pallas_call | solution.py:430
  26.4 0.6 collective-permute-start.6
  27.0 3.4 %collective-permute-start.7 = (f32[32,8,1024]{2,1,0:T(8,128)S(1)}, f32[32,8,1024]{2,1,0:T(8,128)S(1)}, u32[]{:S(2)}, u32[]{:S(2)}) collective-permute-start(f32[32,8,1024]{2,1,0:T(8,128)S(1)} %get-tuple-element.75), channel_id=1, source_target_pairs={{1,2},{2,1},{3,4},{4,3},{5,6},{6,5},{7,8},{8,7},{9,10},{10,9},{11,... | collective-permute-start | bytes 3145736 | tf_op jit(solution)/shard_map/ppermute | solution.py:451
  30.5 0.0 copy-done.3
  30.5 0.2 convert_reduce_fusion
  30.7 2.2 %collective-permute-start.4 = (f32[8,16,1024]{2,1,0:T(8,128)S(1)}, f32[8,16,1024]{2,1,0:T(8,128)S(1)}, u32[]{:S(2)}, u32[]{:S(2)}) collective-permute-start(f32[8,16,1024]{2,1,0:T(8,128)S(1)} %get-tuple-element.69), channel_id=1, source_target_pairs={{0,16},{16,0},{32,48},{48,32},{64,80},{80,64},{96,112},{112,96},{1... | collective-permute-start | bytes 1572872 | tf_op jit(solution)/shard_map/ppermute | solution.py:446
  32.8 0.0 collective-permute-start.5
  32.9 0.1 fusion.14.slots
  33.0 9.2 %shard_map.151 = (f32[32,16,1024]{2,1,0:T(8,128)S(1)}, f32[32,16,1024]{2,1,0:T(8,128)S(1)}, f32[256,128]{1,0:T(8,128)S(1)}, f32[32,16,1024]{2,1,0:T(8,128)}, f32[32,16,1024]{2,1,0:T(8,128)}) custom-call(s32[4]{0:T(128)S(1)} %copy-done.5, f32[4]{0:T(128)S(1)} %get-tuple-element.87.amps, s32[2048]{0:T(1024)S(1)} %add_bitcast_fusion.rows_at, ...), custom_call_target="tpu_custom_call" | custom-call | bytes 30000000 | tf_op jit(solution)/shard_map/pallas_call | solution.py:430
  42.2 0.3 collective-permute-done.4.rxa
  42.5 0.0 collective-permute-done.5.rxb
  42.5 0.0 collective-permute-done.6.rya
  42.5 2.6 %shard_map.152 = (f32[32,16,1024]{2,1,0:T(8,128)S(1)}, f32[32,16,1024]{2,1,0:T(8,128)S(1)}, f32[4096,128]{1,0:T(8,128)S(1)}) custom-call(s32[2]{0:T(128)S(1)} %get-tuple-element.43.place, f32[2]{0:T(128)S(1)} %get-tuple-element.44.ends, f32[32,16,1024]{2,1,0:T(8,128)S(1)} %get-tuple-element.67.wave_part, ...), custom_call_target="tpu_custom_call", output_to_operand_aliasing={{0}: (2, {}), {1}: (3, {})} | custom-call | bytes 9000000 | tf_op jit(solution)/shard_map/pallas_call | solution.py:430
  45.1 0.0 collective-permute-done.7.ryb
  45.1 4.0 %shard_map.153 = (f32[32,16,1024]{2,1,0:T(8,128)S(1)}, f32[32,16,1024]{2,1,0:T(8,128)S(1)}, f32[4096,128]{1,0:T(8,128)S(1)}, f32[32,16,1024]{2,1,0:T(8,128)}, f3...) custom-call(s32[2]{0:T(128)S(1)} %get-tuple-element.43.place, ...), custom_call_target="tpu_custom_call", output_to_operand_aliasing={{0}: (2, {}), {1}: (3, {}), {2}: (4, {})} | custom-call | bytes 12000000 | tf_op jit(solution)/shard_map/pallas_call | solution.py:430
  49.2 35.4 %all_to_all.5 = f32[128,1,128]{2,1,0:T(1,128)S(1)} all-to-all(f32[128,1,128]{2,1,0:T(1,128)S(1)} %bitcast.24), channel_id=1, replica_groups=mesh['gx'=8,'gy'=16] {'gx','gy'}, dimensions={0} | all-to-all | bytes 131072 | tf_op jit(solution)/shard_map/all_to_all | solution.py:566
  84.5 0.7 copy.33
  (8 shorter events, 0.0 us)
Async XLA Ops:
  0.8 2.7 %copy-start = (f32[32,16,1024]{2,1,0:T(8,128)S(1)}, f32[32,16,1024]{2,1,0:T(8,128)}, u32[]{:S(2)}) copy-start(f32[32,16,1024]{2,1,0:T(8,128)} %wave.3) | copy-start | bytes 6291460
  0.8 2.7 %copy-start.1 = (f32[32,16,1024]{2,1,0:T(8,128)S(1)}, f32[32,16,1024]{2,1,0:T(8,128)}, u32[]{:S(2)}) copy-start(f32[32,16,1024]{2,1,0:T(8,128)} %born.3) | copy-start | bytes 6291460
  3.5 7.4 %copy-start.6 = (f32[4,2]{0,1:T(2,128)S(1)}, f32[4,2]{0,1:T(2,128)}, u32[]{:S(2)}) copy-start(f32[4,2]{0,1:T(2,128)} %param.18) | copy-start | bytes 100
  3.5 10.2 %copy-start.2 = (s32[256,8]{0,1:T(8,128)S(1)}, s32[256,8]{0,1:T(8,128)}, u32[]{:S(2)}) copy-start(s32[256,8]{0,1:T(8,128)} %param.19) | copy-start | bytes 24580
  3.5 10.2 %copy-start.4 = (f32[256,8]{0,1:T(8,128)S(1)}, f32[256,8]{0,1:T(8,128)}, u32[]{:S(2)}) copy-start(f32[256,8]{0,1:T(8,128)} %param.20) | copy-start | bytes 24580
  3.5 10.2 %copy-start.5 = (s32[4]{0:T(128)S(1)}, s32[4]{0:T(128)}, u32[]{:S(2)}) copy-start(s32[4]{0:T(128)} %cells.3) | copy-start | bytes 52
  4.5 18.5 %collective-permute-start = (f32[32,8,1024]{2,1,0:T(8,128)S(1)}, f32[32,8,1024]{2,1,0:T(8,128)S(1)}, u32[]{:S(2)}, u32[]{:S(2)}) collective-permute-start(f32[32,8,1024]{2,1,0:T(8,128)S(1)} %get-tuple-element.51), channel_id=1, source_target_pairs={{0,1},{1,0},{2,3},{3,2},{4,5},{5,4},{6,7},{7,6},{8,9},{9,8},{10,11... | collective-permute-start | bytes 3145736 | tf_op jit(solution)/shard_map/ppermute | solution.py:452
  6.0 17.1 %collective-permute-start.1 = (f32[32,8,1024]{2,1,0:T(8,128)S(1)}, f32[32,8,1024]{2,1,0:T(8,128)S(1)}, u32[]{:S(2)}, u32[]{:S(2)}) collective-permute-start(f32[32,8,1024]{2,1,0:T(8,128)S(1)} %get-tuple-element.52), channel_id=1, source_target_pairs={{1,2},{2,1},{3,4},{4,3},{5,6},{6,5},{7,8},{8,7},{9,10},{10,9},{11,... | collective-permute-start | bytes 3145736 | tf_op jit(solution)/shard_map/ppermute | solution.py:451
  9.6 13.5 %collective-permute-start.2 = (f32[8,16,1024]{2,1,0:T(8,128)S(1)}, f32[8,16,1024]{2,1,0:T(8,128)S(1)}, u32[]{:S(2)}, u32[]{:S(2)}) collective-permute-start(f32[8,16,1024]{2,1,0:T(8,128)S(1)} %get-tuple-element.53), channel_id=1, source_target_pairs={{0,16},{16,0},{32,48},{48,32},{64,80},{80,64},{96,112},{112,96},{1... | collective-permute-start | bytes 1572872 | tf_op jit(solution)/shard_map/ppermute | solution.py:446
  10.9 12.2 %collective-permute-start.3 = (f32[8,16,1024]{2,1,0:T(8,128)S(1)}, f32[8,16,1024]{2,1,0:T(8,128)S(1)}, u32[]{:S(2)}, u32[]{:S(2)}) collective-permute-start(f32[8,16,1024]{2,1,0:T(8,128)S(1)} %get-tuple-element.54), channel_id=1, source_target_pairs={{16,32},{17,33},{18,34},{19,35},{20,36},{21,37},{22,38},{23,39},{2... | collective-permute-start | bytes 1572872 | tf_op jit(solution)/shard_map/ppermute | solution.py:445
  24.4 6.0 %copy-start.3 = (s32[256,1]{0,1:T(1,128)S(1)}, s32[256,1]{0,1:T(1,128)}, u32[]{:S(2)}) copy-start(s32[256,1]{0,1:T(1,128)} %param.21) | copy-start | bytes 3076
  26.4 16.1 %collective-permute-start.6 = (f32[32,8,1024]{2,1,0:T(8,128)S(1)}, f32[32,8,1024]{2,1,0:T(8,128)S(1)}, u32[]{:S(2)}, u32[]{:S(2)}) collective-permute-start(f32[32,8,1024]{2,1,0:T(8,128)S(1)} %get-tuple-element.71), channel_id=1, source_target_pairs={{0,1},{1,0},{2,3},{3,2},{4,5},{5,4},{6,7},{7,6},{8,9},{9,8},{10,11... | collective-permute-start | bytes 3145736 | tf_op jit(solution)/shard_map/ppermute | solution.py:452
  27.0 18.1 %collective-permute-start.7 = (f32[32,8,1024]{2,1,0:T(8,128)S(1)}, f32[32,8,1024]{2,1,0:T(8,128)S(1)}, u32[]{:S(2)}, u32[]{:S(2)}) collective-permute-start(f32[32,8,1024]{2,1,0:T(8,128)S(1)} %get-tuple-element.75), channel_id=1, source_target_pairs={{1,2},{2,1},{3,4},{4,3},{5,6},{6,5},{7,8},{8,7},{9,10},{10,9},{11,... | collective-permute-start | bytes 3145736 | tf_op jit(solution)/shard_map/ppermute | solution.py:451
  30.7 11.8 %collective-permute-start.4 = (f32[8,16,1024]{2,1,0:T(8,128)S(1)}, f32[8,16,1024]{2,1,0:T(8,128)S(1)}, u32[]{:S(2)}, u32[]{:S(2)}) collective-permute-start(f32[8,16,1024]{2,1,0:T(8,128)S(1)} %get-tuple-element.69), channel_id=1, source_target_pairs={{0,16},{16,0},{32,48},{48,32},{64,80},{80,64},{96,112},{112,96},{1... | collective-permute-start | bytes 1572872 | tf_op jit(solution)/shard_map/ppermute | solution.py:446
  32.8 9.7 %collective-permute-start.5 = (f32[8,16,1024]{2,1,0:T(8,128)S(1)}, f32[8,16,1024]{2,1,0:T(8,128)S(1)}, u32[]{:S(2)}, u32[]{:S(2)}) collective-permute-start(f32[8,16,1024]{2,1,0:T(8,128)S(1)} %get-tuple-element.70), channel_id=1, source_target_pairs={{16,32},{17,33},{18,34},{19,35},{20,36},{21,37},{22,38},{23,39},{2... | collective-permute-start | bytes 1572872 | tf_op jit(solution)/shard_map/ppermute | solution.py:445
